TPU v7x, 512 devices: a whole 4x8x8 slice. The times are simulated.
512 devices in a mesh: patch: 64 (over z, x, core), lev: 8 (over y).
Axes of the slice: x: 4, y: 8, z: 8, core: 2. Of those that a mesh axis runs over, the one named last changes fastest.
Arguments:
- fields: bfloat16 [8, 128, 131072], P(None, 'lev', 'patch'), may hold values from -6 to 6
- interp: bfloat16 [512, 128, 256], P('patch'), may hold values from -0.375 to 0.375
- conv_weight: bfloat16 [512, 8, 128, 128], P('patch'), may hold values from -0.1875 to 0.1875
- vert_weight: float32 [128, 5], replicated, may hold values from 0.1 to 0.5
- send_tiles: int32 [64, 4, 2], P('patch'), may hold values from 0 to 8, as said below
- tile_pattern: int32 [512, 8], P('patch'), may hold values from 0 to 15, as said below
Outputs:
- localized: float32 [8, 128, 131072], P(None, 'lev', 'patch')
Inputs may be any that keep to these rules, and one draw needn't show every extreme that they name: `send_tiles`: in every draw some link carries 2 tiles; every link carries at least one tile; the tiles of one link are distinct. `tile_pattern`: each row names distinct entries, each an own tile or a filled received slot.
All inputs are finite; a program needn't handle non-finite values.
Results may differ from a plain program's by a relative error of at most 0.0048.
Values may be sent and summed in bfloat16 or wider, within the bound.
No kernel may reach another device: no remote copies, remote signals or barrier semaphores. Data moves between devices by JAX's collectives and lax.ppermute only.
A program may use at most 64 MiB of HBM per device.

v0:
```python
import jax
import jax.numpy as jnp
from jax import lax
from jax.sharding import PartitionSpec as P

HIGHEST = lax.Precision.HIGHEST


def passed_along(block, axis, distance):
    devices = range(lax.axis_size(axis))
    route = [((i - distance) % len(devices), i) for i in devices]
    return lax.ppermute(block, axis, route)


def padded(block, sides, width):
    for axis, dim in sides:
        count = lax.axis_size(axis)
        forward = [(i, i + 1) for i in range(count - 1)]
        backward = [(target, source) for source, target in forward]
        low = lax.ppermute(
            lax.slice_in_dim(block, block.shape[dim] - width, None, axis=dim), axis, forward
        )
        high = lax.ppermute(lax.slice_in_dim(block, 0, width, axis=dim), axis, backward)
        block = jnp.concatenate([low, block, high], axis=dim)
    return block


def link_offsets(reach_len):
    return [
        position - reach_len if position < reach_len else position - reach_len + 1
        for position in range(2 * reach_len)
    ]


def vertical_adjoint(values, weights, length, half_width):
    summed = jnp.zeros(values.shape[:-2] + (length, values.shape[-1]), jnp.float32)
    for offset in range(-half_width, half_width + 1):
        factor = weights[half_width + offset : half_width + offset + length, half_width - offset]
        summed = summed + factor[:, None] * values[
            ..., half_width + offset : half_width + offset + length, :
        ].astype(jnp.float32)
    return summed


def vertical_forward(values, weights, length, half_width):
    summed = jnp.zeros(values.shape[:-2] + (length, values.shape[-1]), jnp.float32)
    for offset in range(2 * half_width + 1):
        factor = weights[half_width : half_width + length, offset]
        summed = summed + factor[:, None] * values[..., offset : offset + length, :].astype(
            jnp.float32
        )
    return summed


def move_links(pieces, reach_len, offsets, backward):
    if backward:
        return jnp.stack(
            [
                passed_along(pieces[position], "patch", -offsets[position])
                for position in range(2 * reach_len)
            ]
        )
    return jnp.stack(
        [
            passed_along(pieces[position], "patch", offsets[position])
            for position in range(2 * reach_len)
        ]
    )


def shards(fields, interp, conv_weight, vert_weight, send_tiles, tile_pattern):
    members, level_len, column_len = fields.shape
    tile_count, tile_len, fine_len = interp.shape
    reach_len = send_tiles.shape[1] // 2
    slot_most = send_tiles.shape[2]
    half_width = (vert_weight.shape[1] - 1) // 2
    row_count = members * level_len
    extended_len = tile_count + 2 * reach_len * slot_most
    offsets = link_offsets(reach_len)
    coarse = jnp.einsum(
        "rtf,tcf->trc",
        fields.reshape(row_count, tile_count, fine_len),
        interp,
        preferred_element_type=jnp.float32,
    ).astype(jnp.bfloat16)
    chosen = tile_pattern[:, :, None] == jnp.arange(extended_len, dtype=jnp.int32)[None, None, :]
    sending = (
        send_tiles[0][:, :, None] == jnp.arange(tile_count, dtype=jnp.int32)[None, None, :]
    ).astype(jnp.bfloat16)
    products = jnp.einsum("tro,tkio->tkri", coarse, conv_weight, preferred_element_type=jnp.float32)
    summed = jnp.einsum("tke,tkri->eri", chosen.astype(jnp.float32), products, precision=HIGHEST)
    own_part = summed[:tile_count]
    returning = (
        summed[tile_count:]
        .reshape(2 * reach_len, slot_most, row_count, tile_len)
        .astype(jnp.bfloat16)
    )
    arrived_back = move_links(returning, reach_len, offsets, True)
    added = jnp.einsum("ost,osri->tri", sending, arrived_back, preferred_element_type=jnp.float32)
    adjoint = (
        (own_part + added).astype(jnp.bfloat16).reshape(tile_count, members, level_len, tile_len)
    )
    start = lax.axis_index("lev") * level_len
    padded_weights = jnp.pad(vert_weight, ((2 * half_width, 2 * half_width), (0, 0)))
    window = lax.dynamic_slice_in_dim(padded_weights, start, level_len + 4 * half_width, 0)
    inner = window[half_width : half_width + level_len + 2 * half_width]
    widened = padded(adjoint, (("lev", 2),), 2 * half_width)
    middle = vertical_adjoint(widened, window, level_len + 2 * half_width, half_width)
    level_ids = start - half_width + jnp.arange(level_len + 2 * half_width, dtype=jnp.int32)
    inside = (level_ids >= 0) & (level_ids < vert_weight.shape[0])
    middle = jnp.where(inside[:, None], middle, 0.0).astype(jnp.bfloat16)
    smoothed = vertical_forward(middle, inner, level_len, half_width)
    smooth = smoothed.astype(jnp.bfloat16).reshape(tile_count, row_count, tile_len)
    slots = jnp.einsum("ost,tri->osri", sending, smooth, preferred_element_type=jnp.float32).astype(
        jnp.bfloat16
    )
    arrived = move_links(slots, reach_len, offsets, False)
    extended = jnp.concatenate([smooth, arrived.reshape(-1, row_count, tile_len)], axis=0)
    picked = jnp.einsum(
        "tke,eri->tkri", chosen.astype(jnp.bfloat16), extended, preferred_element_type=jnp.float32
    ).astype(jnp.bfloat16)
    mixed = jnp.einsum(
        "tkri,tkio->tro", picked, conv_weight, preferred_element_type=jnp.float32
    ).astype(jnp.bfloat16)
    result = jnp.einsum("tro,tof->rtf", mixed, interp, preferred_element_type=jnp.float32)
    return result.reshape(members, level_len, column_len)


def solution(mesh):
    in_specs = (
        P(None, "lev", "patch"),
        P("patch", None, None),
        P("patch", None, None, None),
        P(),
        P("patch", None, None),
        P("patch", None),
    )
    out_specs = P(None, "lev", "patch")
    return jax.shard_map(shards, mesh=mesh, in_specs=in_specs, out_specs=out_specs, check_vma=False)
```

profile of v0, /device:TPU:24, one launch (start us, length us, event | category | flops | bytes accessed | tf_op | source)
XLA Modules:
  0.0 81.2 jit_solution(365150887682621270)
XLA Ops:
  0.0 0.0 copy-start
  0.0 0.9 %copy.34 = s32[8,8]{0,1:T(8,128)S(1)} copy(s32[8,8]{1,0:T(8,128)} %param.11) | data formatting | bytes 512 | tf_op args[5]
  0.9 1.1 %copy.51 = bf16[16,8,8,256]{3,2,1,0:T(8,128)(2,1)S(1)} copy(bf16[16,8,8,256]{3,1,2,0:T(8,128)(2,1)} %bitcast.107) | data formatting | bytes 1048576
  2.1 0.0 copy-done
  2.1 3.9 %convolution_bitcast_fusion = f32[8,8,128,128]{3,2,1,0:T(8,128)} fusion(bf16[8,8,128,128]{3,2,1,0:T(8,128)(2,1)S(1)} %copy-done, bf16[8,128,256]{2,1,0:T(8,128)(2,1)} %param.7, bf16[128,8,256]{2,1,0:T(8,128)(2,1)S(1)} %bitcast.105), kind=kOutput, calls=%fused_computation.2 | convolution fusion | flops 335675392 | bytes 7340032 | tf_op jit(solution)/shard_map/tro,tkio->tkri/dot_general | solution.py:90
  5.9 5.9 %fusion.39 = (bf16[16,128,128]{2,0,1:T(8,128)(2,1)S(1)}, f32[16,128,128]{2,0,1:T(8,128)S(1)}) fusion(f32[8,8,128,128]{3,2,1,0:T(8,128)} %convolution_bitcast_fusion, s32[8,8]{0,1:T(8,128)S(1)} %copy.34), kind=kOutput, calls=%fused_computation.56 | convolution fusion | flops 201589760 | bytes 5767424 | tf_op jit(solution)/shard_map/tke,tkri->eri/dot_general | solution.py:91
  11.8 0.8 %fusion.36 = (bf16[2,128,128]{2,0,1:T(2,128)(2,1)}, bf16[2,128,128]{2,0,1:T(2,128)(2,1)S(1)}, bf16[2,128,128]{2,0,1:T(2,128)(2,1)S(1)}, bf16[2,128,128]{2,0,1:T(2,128)(2,1)S(1)}) fusion(bf16[16,128,128]{2,0,1:T(8,128)(2,1)S(1)} %get-tuple-element.25), kind=kLoop, calls=%fused_computation.53 | loop fusion | bytes 524288 | tf_op jit(solution)/shard_map/slice | solution.py:59
  12.6 3.4 %collective-permute-start = (bf16[2,128,128]{2,0,1:T(2,128)(2,1)}, bf16[2,128,128]{2,0,1:T(2,128)(2,1)S(1)}, u32[]{:S(2)}, u32[]{:S(2)}) collective-permute-start(bf16[2,128,128]{2,0,1:T(2,128)(2,1)} %get-tuple-element.5), channel_id=1, source_target_pairs={{496,0},{504,8},{0,16},{8,24},{16,32},{24,40},{32,48},{40,56},{48,... | collective-permute-start | bytes 196616 | tf_op jit(solution)/shard_map/ppermute | solution.py:12
  16.0 1.9 %collective-permute-start.1 = (bf16[2,128,128]{2,0,1:T(2,128)(2,1)S(1)}, bf16[2,128,128]{2,0,1:T(2,128)(2,1)S(1)}, u32[]{:S(2)}, u32[]{:S(2)}) collective-permute-start(bf16[2,128,128]{2,0,1:T(2,128)(2,1)S(1)} %get-tuple-element.8), channel_id=1, source_target_pairs={{504,0},{0,8},{8,16},{16,24},{24,32},{32,40},{40,48},{48,56},{56,6... | collective-permute-start | bytes 196616 | tf_op jit(solution)/shard_map/ppermute | solution.py:12
  17.9 11.1 %collective-permute-start.2 = (bf16[2,128,128]{2,0,1:T(2,128)(2,1)S(1)}, bf16[2,128,128]{2,0,1:T(2,128)(2,1)S(1)}, u32[]{:S(2)}, u32[]{:S(2)}) collective-permute-start(bf16[2,128,128]{2,0,1:T(2,128)(2,1)S(1)} %get-tuple-element.7), channel_id=1, source_target_pairs={{8,0},{16,8},{24,16},{32,24},{40,32},{48,40},{56,48},{64,56},{72,6... | collective-permute-start | bytes 196616 | tf_op jit(solution)/shard_map/ppermute | solution.py:12
  29.1 4.2 %collective-permute-start.3 = (bf16[2,128,128]{2,0,1:T(2,128)(2,1)S(1)}, bf16[2,128,128]{2,0,1:T(2,128)(2,1)}, u32[]{:S(2)}, u32[]{:S(2)}) collective-permute-start(bf16[2,128,128]{2,0,1:T(2,128)(2,1)S(1)} %get-tuple-element.6), channel_id=1, source_target_pairs={{16,0},{24,8},{32,16},{40,24},{48,32},{56,40},{64,48},{72,56},{80,... | collective-permute-start | bytes 196616 | tf_op jit(solution)/shard_map/ppermute | solution.py:12
  33.3 0.0 copy-done.3
  33.3 0.1 pad_dynamic-slice_fusion
  33.4 0.7 slice_bitcast_fusion.8
  34.0 0.7 slice_bitcast_fusion.9
  34.7 0.0 copy-start.11
  34.7 0.0 collective-permute-done
  34.7 0.0 collective-permute-done.1
  34.7 0.0 collective-permute-done.2
  34.7 0.6 collective-permute-done.3
  35.3 1.3 %pad_maximum_fusion.1 = bf16[4,2,128,128]{3,1,2,0:T(2,128)(2,1)S(1)} fusion(bf16[1,2,128,128]{3,1,2,0:T(2,128)(2,1)} %bitcast.14, bf16[1,2,128,128]{3,1,2,0:T(2,128)(2,1)S(1)} %bitcast.114, bf16[1,2,128,128]{3,1,2,0:T(2,128)(2,1)S(1)} %bitcast.113, bf16[1,2,128,128]{3,1,2,0:T(2,128)(2,1)S(1)} %bitcast.112), kind=kLoop, calls=%fused_computation.23 | loop fusion | flops 393216 | bytes 524288 | tf_op jit(solution)/shard_map/stack | solution.py:57
  36.6 0.0 copy-done.2
  36.7 0.5 fusion.11
  37.2 4.7 %collective-permute-start.4 = (bf16[8,8,4,128]{3,0,2,1:T(8,128)(2,1)S(1)}, bf16[8,8,4,128]{3,0,2,1:T(8,128)(2,1)S(1)}, u32[]{:S(2)}, u32[]{:S(2)}) collective-permute-start(bf16[8,8,4,128]{3,0,2,1:T(8,128)(2,1)S(1)} %get-tuple-element.13), channel_id=1, source_target_pairs={{0,1},{1,2},{2,3},{3,4},{4,5},{5,6},{6,7},{8,9},{9,10},{10,11},{11... | collective-permute-start | bytes 196616 | tf_op jit(solution)/shard_map/ppermute | solution.py:20
  41.9 1.9 %collective-permute-start.5 = (bf16[8,8,4,128]{3,0,2,1:T(8,128)(2,1)S(1)}, bf16[8,8,4,128]{3,0,2,1:T(8,128)(2,1)S(1)}, u32[]{:S(2)}, u32[]{:S(2)}) collective-permute-start(bf16[8,8,4,128]{3,0,2,1:T(8,128)(2,1)S(1)} %get-tuple-element.14), channel_id=1, source_target_pairs={{1,0},{2,1},{3,2},{4,3},{5,4},{6,5},{7,6},{9,8},{10,9},{11,10},{12... | collective-permute-start | bytes 196616 | tf_op jit(solution)/shard_map/ppermute | solution.py:23
  43.8 0.0 collective-permute-done.4
  43.8 5.4 %collective-permute-done.5 = bf16[8,8,4,128]{3,0,2,1:T(8,128)(2,1)S(1)} collective-permute-done((bf16[8,8,4,128]{3,0,2,1:T(8,128)(2,1)S(1)}, bf16[8,8,4,128]{3,0,2,1:T(8,128)(2,1)S(1)}, u32[]{:S(2)}, u32[]{:S(2)}) %collective-permute-start.5) | collective-permute-done | bytes 65568 | tf_op jit(solution)/shard_map/ppermute | solution.py:23
  49.3 0.4 select_convert_fusion
  49.8 0.0 copy-done.4
  49.8 0.0 copy-done.5
  49.8 0.0 copy-done.6
  49.8 0.3 add_convert_fusion
  50.2 0.3 convolution_convert_fusion.1
  50.4 0.4 fusion.37
  50.9 7.5 %collective-permute-start.6 = (bf16[2,128,128]{2,1,0:T(8,128)(2,1)S(1)}, bf16[2,128,128]{2,1,0:T(8,128)(2,1)S(1)}, u32[]{:S(2)}, u32[]{:S(2)}) collective-permute-start(bf16[2,128,128]{2,1,0:T(8,128)(2,1)S(1)} %bitcast.108), channel_id=1, source_target_pairs={{16,0},{24,8},{32,16},{40,24},{48,32},{56,40},{64,48},{72,56},{80,... | collective-permute-start | bytes 196616 | tf_op jit(solution)/shard_map/ppermute | solution.py:12
  58.4 0.0 copy-start.1
  58.4 2.1 %collective-permute-start.7 = (bf16[2,128,128]{2,1,0:T(8,128)(2,1)S(1)}, bf16[2,128,128]{2,1,0:T(8,128)(2,1)S(1)}, u32[]{:S(2)}, u32[]{:S(2)}) collective-permute-start(bf16[2,128,128]{2,1,0:T(8,128)(2,1)S(1)} %bitcast.109), channel_id=1, source_target_pairs={{8,0},{16,8},{24,16},{32,24},{40,32},{48,40},{56,48},{64,56},{72,6... | collective-permute-start | bytes 196616 | tf_op jit(solution)/shard_map/ppermute | solution.py:12
  60.5 2.4 %collective-permute-start.8 = (bf16[2,128,128]{2,1,0:T(8,128)(2,1)S(1)}, bf16[2,128,128]{2,1,0:T(8,128)(2,1)S(1)}, u32[]{:S(2)}, u32[]{:S(2)}) collective-permute-start(bf16[2,128,128]{2,1,0:T(8,128)(2,1)S(1)} %bitcast.110), channel_id=1, source_target_pairs={{504,0},{0,8},{8,16},{16,24},{24,32},{32,40},{40,48},{48,56},{56,6... | collective-permute-start | bytes 196616 | tf_op jit(solution)/shard_map/ppermute | solution.py:12
  62.9 1.9 %collective-permute-start.9 = (bf16[2,128,128]{2,1,0:T(8,128)(2,1)S(1)}, bf16[2,128,128]{2,1,0:T(8,128)(2,1)S(1)}, u32[]{:S(2)}, u32[]{:S(2)}) collective-permute-start(bf16[2,128,128]{2,1,0:T(8,128)(2,1)S(1)} %bitcast.111), channel_id=1, source_target_pairs={{496,0},{504,8},{0,16},{8,24},{16,32},{24,40},{32,48},{40,56},{48,... | collective-permute-start | bytes 196616 | tf_op jit(solution)/shard_map/ppermute | solution.py:12
  64.9 0.0 collective-permute-done.6
  64.9 0.0 collective-permute-done.7
  64.9 4.5 %collective-permute-done.8 = bf16[2,128,128]{2,1,0:T(8,128)(2,1)S(1)} collective-permute-done((bf16[2,128,128]{2,1,0:T(8,128)(2,1)S(1)}, bf16[2,128,128]{2,1,0:T(8,128)(2,1)S(1)}, u32[]{:S(2)}, u32[]{:S(2)}) %collective-permute-start.8) | collective-permute-done | bytes 65568 | tf_op jit(solution)/shard_map/ppermute | solution.py:12
  69.4 3.0 %collective-permute-done.9 = bf16[2,128,128]{2,1,0:T(8,128)(2,1)S(1)} collective-permute-done((bf16[2,128,128]{2,1,0:T(8,128)(2,1)S(1)}, bf16[2,128,128]{2,1,0:T(8,128)(2,1)S(1)}, u32[]{:S(2)}, u32[]{:S(2)}) %collective-permute-start.9) | collective-permute-done | bytes 65568 | tf_op jit(solution)/shard_map/ppermute | solution.py:12
  72.5 0.3 copy.38
  72.7 2.1 %convolution_convert_fusion = bf16[8,8,128,128]{3,0,2,1:T(8,128)(2,1)} fusion(bf16[8,128,128]{2,0,1:T(8,128)(2,1)S(1)} %bitcast.106, bf16[8,128,128]{2,0,1:T(8,128)(2,1)S(1)} %bitcast.104, s32[8,8]{0,1:T(8,128)S(1)} %copy.34), kind=kOutput, calls=%fused_computation.5 | convolution fusion | flops 35652608 | bytes 2621696 | tf_op jit(solution)/shard_map/tke,eri->tkri/dot_general | solution.py:119
  74.8 3.5 %convolution_bitcast_fusion.1 = f32[128,8,256]{2,0,1:T(8,128)} fusion(bf16[8,128,256]{2,1,0:T(8,128)(2,1)S(1)} %copy-done.1, bf16[8,8,128,128]{3,2,1,0:T(8,128)(2,1)S(1)} %copy-done, bf16[8,8,128,128]{3,0,2,1:T(8,128)(2,1)} %convolution_convert_fusion), kind=kOutput, calls=%fused_computation.7 | convolution fusion | flops 335675392 | bytes 5767168 | tf_op jit(solution)/shard_map/tro,tof->rtf/dot_general | solution.py:125
  78.3 1.8 %copy.40 = f32[128,8,256]{2,1,0:T(8,128)S(1)} copy(f32[128,8,256]{2,0,1:T(8,128)} %convolution_bitcast_fusion.1) | data formatting | bytes 2097152 | tf_op jit(solution)/shard_map/tro,tof->rtf/transpose | solution.py:125
  80.1 1.1 %reshape.41 = f32[8,16,2048]{2,1,0:T(8,128)} reshape(f32[128,8,256]{2,1,0:T(8,128)S(1)} %copy.40) | data formatting | bytes 2097152 | tf_op jit(solution)/shard_map/reshape | solution.py:126
  (23 shorter events, 0.2 us)
Async XLA Ops:
  0.0 2.1 %copy-start = (bf16[8,8,128,128]{3,2,1,0:T(8,128)(2,1)S(1)}, bf16[8,8,128,128]{3,2,1,0:T(8,128)(2,1)}, u32[]{:S(2)}) copy-start(bf16[8,8,128,128]{3,2,1,0:T(8,128)(2,1)} %param.8) | copy-start | bytes 6291460
  5.9 27.3 %copy-start.3 = (f32[128,5]{0,1:T(8,128)S(1)}, f32[128,5]{0,1:T(8,128)}, u32[]{:S(2)}) copy-start(f32[128,5]{0,1:T(8,128)} %param.9) | copy-start | bytes 7684
  5.9 30.7 %copy-start.2 = (s32[1,4,2]{1,2,0:T(2,128)S(1)}, s32[1,4,2]{1,2,0:T(2,128)}, u32[]{:S(2)}) copy-start(s32[1,4,2]{1,2,0:T(2,128)} %param.10) | copy-start | bytes 100
  12.6 22.1 %collective-permute-start = (bf16[2,128,128]{2,0,1:T(2,128)(2,1)}, bf16[2,128,128]{2,0,1:T(2,128)(2,1)S(1)}, u32[]{:S(2)}, u32[]{:S(2)}) collective-permute-start(bf16[2,128,128]{2,0,1:T(2,128)(2,1)} %get-tuple-element.5), channel_id=1, source_target_pairs={{496,0},{504,8},{0,16},{8,24},{16,32},{24,40},{32,48},{40,56},{48,... | collective-permute-start | bytes 196616 | tf_op jit(solution)/shard_map/ppermute | solution.py:12
  16.0 18.7 %collective-permute-start.1 = (bf16[2,128,128]{2,0,1:T(2,128)(2,1)S(1)}, bf16[2,128,128]{2,0,1:T(2,128)(2,1)S(1)}, u32[]{:S(2)}, u32[]{:S(2)}) collective-permute-start(bf16[2,128,128]{2,0,1:T(2,128)(2,1)S(1)} %get-tuple-element.8), channel_id=1, source_target_pairs={{504,0},{0,8},{8,16},{16,24},{24,32},{32,40},{40,48},{48,56},{56,6... | collective-permute-start | bytes 196616 | tf_op jit(solution)/shard_map/ppermute | solution.py:12
  17.9 16.8 %collective-permute-start.2 = (bf16[2,128,128]{2,0,1:T(2,128)(2,1)S(1)}, bf16[2,128,128]{2,0,1:T(2,128)(2,1)S(1)}, u32[]{:S(2)}, u32[]{:S(2)}) collective-permute-start(bf16[2,128,128]{2,0,1:T(2,128)(2,1)S(1)} %get-tuple-element.7), channel_id=1, source_target_pairs={{8,0},{16,8},{24,16},{32,24},{40,32},{48,40},{56,48},{64,56},{72,6... | collective-permute-start | bytes 196616 | tf_op jit(solution)/shard_map/ppermute | solution.py:12
  29.1 6.3 %collective-permute-start.3 = (bf16[2,128,128]{2,0,1:T(2,128)(2,1)S(1)}, bf16[2,128,128]{2,0,1:T(2,128)(2,1)}, u32[]{:S(2)}, u32[]{:S(2)}) collective-permute-start(bf16[2,128,128]{2,0,1:T(2,128)(2,1)S(1)} %get-tuple-element.6), channel_id=1, source_target_pairs={{16,0},{24,8},{32,16},{40,24},{48,32},{56,40},{64,48},{72,56},{80,... | collective-permute-start | bytes 196616 | tf_op jit(solution)/shard_map/ppermute | solution.py:12
  34.7 14.6 %copy-start.7 = (f32[20]{0:T(128)S(1)}, f32[20]{0:T(128)}, u32[]{:S(2)}) copy-start(f32[20]{0:T(128)} %get-tuple-element.20) | copy-start | bytes 244
  34.7 14.6 %copy-start.8 = (f32[20]{0:T(128)S(1)}, f32[20]{0:T(128)}, u32[]{:S(2)}) copy-start(f32[20]{0:T(128)} %get-tuple-element.21) | copy-start | bytes 244
  34.7 14.6 %copy-start.9 = (f32[20]{0:T(128)S(1)}, f32[20]{0:T(128)}, u32[]{:S(2)}) copy-start(f32[20]{0:T(128)} %get-tuple-element.22) | copy-start | bytes 244
  34.7 14.6 %copy-start.10 = (f32[20]{0:T(128)S(1)}, f32[20]{0:T(128)}, u32[]{:S(2)}) copy-start(f32[20]{0:T(128)} %get-tuple-element.23) | copy-start | bytes 244
  34.7 14.7 %copy-start.11 = (f32[20]{0:T(128)S(1)}, f32[20]{0:T(128)}, u32[]{:S(2)}) copy-start(f32[20]{0:T(128)} %get-tuple-element.24) | copy-start | bytes 244
  35.3 14.5 %copy-start.4 = (f32[16]{0:T(128)S(1)}, f32[16]{0:T(128)}, u32[]{:S(2)}) copy-start(f32[16]{0:T(128)} %get-tuple-element.17) | copy-start | bytes 196
  35.3 14.5 %copy-start.5 = (f32[16]{0:T(128)S(1)}, f32[16]{0:T(128)}, u32[]{:S(2)}) copy-start(f32[16]{0:T(128)} %get-tuple-element.18) | copy-start | bytes 196
  35.3 14.5 %copy-start.6 = (f32[16]{0:T(128)S(1)}, f32[16]{0:T(128)}, u32[]{:S(2)}) copy-start(f32[16]{0:T(128)} %get-tuple-element.19) | copy-start | bytes 196
  37.2 6.6 %collective-permute-start.4 = (bf16[8,8,4,128]{3,0,2,1:T(8,128)(2,1)S(1)}, bf16[8,8,4,128]{3,0,2,1:T(8,128)(2,1)S(1)}, u32[]{:S(2)}, u32[]{:S(2)}) collective-permute-start(bf16[8,8,4,128]{3,0,2,1:T(8,128)(2,1)S(1)} %get-tuple-element.13), channel_id=1, source_target_pairs={{0,1},{1,2},{2,3},{3,4},{4,5},{5,6},{6,7},{8,9},{9,10},{10,11},{11... | collective-permute-start | bytes 196616 | tf_op jit(solution)/shard_map/ppermute | solution.py:20
  41.9 7.4 %collective-permute-start.5 = (bf16[8,8,4,128]{3,0,2,1:T(8,128)(2,1)S(1)}, bf16[8,8,4,128]{3,0,2,1:T(8,128)(2,1)S(1)}, u32[]{:S(2)}, u32[]{:S(2)}) collective-permute-start(bf16[8,8,4,128]{3,0,2,1:T(8,128)(2,1)S(1)} %get-tuple-element.14), channel_id=1, source_target_pairs={{1,0},{2,1},{3,2},{4,3},{5,4},{6,5},{7,6},{9,8},{10,9},{11,10},{12... | collective-permute-start | bytes 196616 | tf_op jit(solution)/shard_map/ppermute | solution.py:23
  50.9 14.0 %collective-permute-start.6 = (bf16[2,128,128]{2,1,0:T(8,128)(2,1)S(1)}, bf16[2,128,128]{2,1,0:T(8,128)(2,1)S(1)}, u32[]{:S(2)}, u32[]{:S(2)}) collective-permute-start(bf16[2,128,128]{2,1,0:T(8,128)(2,1)S(1)} %bitcast.108), channel_id=1, source_target_pairs={{16,0},{24,8},{32,16},{40,24},{48,32},{56,40},{64,48},{72,56},{80,... | collective-permute-start | bytes 196616 | tf_op jit(solution)/shard_map/ppermute | solution.py:12
  58.4 16.4 %copy-start.1 = (bf16[8,128,256]{2,1,0:T(8,128)(2,1)S(1)}, bf16[8,128,256]{2,1,0:T(8,128)(2,1)}, u32[]{:S(2)}) copy-start(bf16[8,128,256]{2,1,0:T(8,128)(2,1)} %param.7) | copy-start | bytes 1572868
  58.4 6.5 %collective-permute-start.7 = (bf16[2,128,128]{2,1,0:T(8,128)(2,1)S(1)}, bf16[2,128,128]{2,1,0:T(8,128)(2,1)S(1)}, u32[]{:S(2)}, u32[]{:S(2)}) collective-permute-start(bf16[2,128,128]{2,1,0:T(8,128)(2,1)S(1)} %bitcast.109), channel_id=1, source_target_pairs={{8,0},{16,8},{24,16},{32,24},{40,32},{48,40},{56,48},{64,56},{72,6... | collective-permute-start | bytes 196616 | tf_op jit(solution)/shard_map/ppermute | solution.py:12
  60.5 8.9 %collective-permute-start.8 = (bf16[2,128,128]{2,1,0:T(8,128)(2,1)S(1)}, bf16[2,128,128]{2,1,0:T(8,128)(2,1)S(1)}, u32[]{:S(2)}, u32[]{:S(2)}) collective-permute-start(bf16[2,128,128]{2,1,0:T(8,128)(2,1)S(1)} %bitcast.110), channel_id=1, source_target_pairs={{504,0},{0,8},{8,16},{16,24},{24,32},{32,40},{40,48},{48,56},{56,6... | collective-permute-start | bytes 196616 | tf_op jit(solution)/shard_map/ppermute | solution.py:12
  62.9 9.5 %collective-permute-start.9 = (bf16[2,128,128]{2,1,0:T(8,128)(2,1)S(1)}, bf16[2,128,128]{2,1,0:T(8,128)(2,1)S(1)}, u32[]{:S(2)}, u32[]{:S(2)}) collective-permute-start(bf16[2,128,128]{2,1,0:T(8,128)(2,1)S(1)} %bitcast.111), channel_id=1, source_target_pairs={{496,0},{504,8},{0,16},{8,24},{16,32},{24,40},{32,48},{40,56},{48,... | collective-permute-start | bytes 196616 | tf_op jit(solution)/shard_map/ppermute | solution.py:12
where the time goes:
time: 81.8 us; the launch traced here: 81.2 us
  starting transfers between devices  41.1 us (50%)
  matrix products  16 us (20%)
  waiting for transfers between devices  13.6 us (17%)
  local copies, waits for them, and re-layouts  8 us (10%)
  other arithmetic  2.16 us (3%)
    ppermute x8, starting transfers between devices, passed_along(): return lax.ppermute(block, axis, route)  34.5 us
    ppermute x8, waiting for transfers between devices, passed_along(): return lax.ppermute(block, axis, route)  8.13 us
    dot_general x1, matrix products, shards(): jnp.einsum('tke,tkri->eri', chosen.astype(jnp.float32), products, precisi...  5.86 us
    ppermute x1, waiting for transfers between devices, padded(): lax.ppermute(lax.slice_in_dim(block, 0, width, axis=dim), axis, backward)  5.42 us
    ppermute x1, starting transfers between devices, padded(): lax.ppermute(lax.slice_in_dim(block, block.shape[dim] - width, None, axis...  4.69 us
    dot_general x1, matrix products, shards(): jnp.einsum('tro,tkio->tkri', coarse, conv_weight, preferred_element_type=...  3.86 us
    dot_general x1, matrix products, shards(): jnp.einsum('tro,tof->rtf', mixed, interp, preferred_element_type=jnp.floa...  3.46 us
    unnamed x30, local copies, waits for them, and re-layouts  2.15 us
  transfers between devices with their start and end apart: 10, of which 4 were waited for; matrix products, arithmetic and copies ran while one was open for 2% of the time, Pallas kernels for 0%

commit v1 on v0

v1 whole, which is shorter than its diff:
```python
import jax
import jax.numpy as jnp
from jax import lax
from jax.experimental import pallas as pl
from jax.experimental.pallas import tpu as pltpu
from jax.sharding import PartitionSpec as P

BF16 = jnp.bfloat16
F32 = jnp.float32
HIGHEST = lax.Precision.HIGHEST


def nn(a, b):
    return lax.dot_general(a, b, (((1,), (0,)), ((), ())), preferred_element_type=F32)


def nt(a, b):
    return lax.dot_general(a, b, (((1,), (1,)), ((), ())), preferred_element_type=F32)


def iota(shape, dim):
    return lax.broadcasted_iota(jnp.int32, shape, dim)


def split(a):
    high = a.astype(BF16)
    return high, (a - high.astype(F32)).astype(BF16)


def restrict_kernel(members, level_len, halo, fields, interp, weights, partial, halo_matrix):
    tiles, tile_len, fine = interp.shape
    rows = members * level_len
    halo_rows = members * halo
    levels, taps = weights.shape
    half = taps // 2
    start = lax.axis_index("lev") * level_len
    distance = iota((levels, levels), 1) - iota((levels, levels), 0)
    table = weights[...]
    band = jnp.zeros((levels, levels), F32)
    for j in range(taps):
        band = band + jnp.where(distance == j - half, table[:, j : j + 1], 0.0)
    both = lax.dot_general(
        band, band, (((1,), (1,)), ((), ())), precision=HIGHEST, preferred_element_type=F32
    )
    pick = (
        iota((rows, levels), 1) == start + iota((rows, levels), 0) % level_len
    ).astype(BF16)
    place = iota((2 * halo_rows, levels), 0)
    level = jnp.where(
        place < halo_rows, start - halo + place % halo, start + level_len + place % halo
    )
    pick_halo = (iota((2 * halo_rows, levels), 1) == level).astype(BF16)
    same = iota((rows, rows), 0) // level_len == iota((rows, rows), 1) // level_len
    column = iota((rows, 2 * halo_rows), 1) % halo_rows
    same_halo = iota((rows, 2 * halo_rows), 0) // level_len == column // halo
    own_parts = []
    for i, part in enumerate(split(both)):
        chosen = nn(pick, part).astype(BF16)
        own_parts.append(jnp.where(same, nt(chosen, pick), 0.0).astype(BF16))
        halo_matrix[:, i * 2 * halo_rows : (i + 1) * 2 * halo_rows] = jnp.where(
            same_halo, nt(chosen, pick_halo), 0.0
        ).astype(BF16)
    own_matrix = jnp.concatenate(own_parts, axis=1)
    for t in range(tiles):
        block = fields[:, :, t * fine : (t + 1) * fine].reshape(rows, fine)
        coarse = nt(block, interp[t]).astype(BF16)
        partial[t] = nn(own_matrix, jnp.concatenate([coarse, coarse], axis=0))


def adjoint_kernel(
    pattern, partial, halo_matrix, low, high, interp, conv, own, up, down, entries
):
    tiles, tile_len, fine = interp.shape
    count = conv.shape[1]
    entries[...] = jnp.zeros_like(entries)
    matrix = halo_matrix[...]
    for t in range(tiles):
        span = slice(t * fine, (t + 1) * fine)
        block = jnp.concatenate([low[:, span], high[:, span]], axis=0)
        edge = nt(block, interp[t]).astype(BF16)
        smooth = partial[t] + nn(matrix, jnp.concatenate([edge, edge], axis=0))
        products = nt(
            smooth.astype(BF16), conv[t].reshape(count * tile_len, tile_len)
        )
        for k in range(count):
            entry = pattern[t, k]
            entries[entry] += products[:, k * tile_len : (k + 1) * tile_len]
    own[...] = entries[:tiles]
    up[...] = entries[tiles : tiles + 4].astype(BF16)
    down[0:2] = entries[tiles + 6 : tiles + 8].astype(BF16)
    down[2:4] = entries[tiles + 4 : tiles + 6].astype(BF16)


def add_to(total, tile, piece):
    @pl.when(tile < total.shape[0])
    def _():
        total[tile] += piece.astype(F32)


def partner_kernel(send, own, up, down, from_low, from_high, total, payload):
    tiles = own.shape[0]
    core = lax.axis_index("patch") % 2
    total[...] = own[...]
    for s in range(2):
        add_to(total, send[0, 0, s], from_low[s])
        add_to(total, send[0, 3, s], from_high[s])

    @pl.when(core == 0)
    def _():
        payload[0:2] = up[2:4]
        payload[2:4] = from_high[2:4]

    @pl.when(core == 1)
    def _():
        payload[0:2] = from_low[2:4]
        payload[2:4] = down[2:4]

    for o in range(2):
        for s in range(2):
            tile = send[0, 1 + o, s]
            payload[4 + 2 * o + s] = total[jnp.minimum(tile, tiles - 1)].astype(BF16)
            payload[8, 16 * (2 * o + s) : 16 * (2 * o + s) + 16, :] = jnp.full(
                (16, payload.shape[2]), tile.astype(F32)
            ).astype(BF16)


def complete_kernel(send, partial, payload, arrived, smooth, up, down, total):
    tiles = partial.shape[0]
    total[...] = partial[...]
    for o in range(2):
        for s in range(2):
            add_to(total, send[0, 1 + o, s], arrived[2 * o + s])
    smooth[...] = total[...].astype(BF16)
    for s in range(2):
        down[s] = smooth[jnp.minimum(send[0, 0, s], tiles - 1)]
        up[s] = smooth[jnp.minimum(send[0, 3, s], tiles - 1)]
    marks = [arrived[8, 16 * i : 16 * i + 1, :].astype(F32) for i in range(4)]
    for o in range(2):
        out = (down, up)[o]
        for s in range(2):
            mine = 2 * o + s
            tile = arrived[4 + mine].astype(F32) + payload[mine].astype(F32)
            for other in range(2):
                theirs = 2 * (1 - o) + other
                tile = tile + jnp.where(
                    marks[mine] == marks[theirs], payload[theirs].astype(F32), 0.0
                )
            out[2 + s] = tile.astype(BF16)


def forward_kernel(
    pattern, smooth, up, down, from_low, from_high, interp, conv, out, entries
):
    tiles, tile_len, fine = interp.shape
    count = conv.shape[1]
    members, level_len, _ = out.shape
    core = lax.axis_index("patch") % 2
    entries[0:tiles] = smooth[...]
    entries[tiles : tiles + 2] = from_high[0:2]
    entries[tiles + 6 : tiles + 8] = from_low[0:2]

    @pl.when(core == 0)
    def _():
        entries[tiles + 2 : tiles + 4] = down[2:4]
        entries[tiles + 4 : tiles + 6] = from_low[2:4]

    @pl.when(core == 1)
    def _():
        entries[tiles + 2 : tiles + 4] = from_high[2:4]
        entries[tiles + 4 : tiles + 6] = up[2:4]

    for t in range(tiles):
        picked = jnp.concatenate([entries[pattern[t, k]] for k in range(count)], axis=1)
        mixed = nn(picked, conv[t].reshape(count * tile_len, tile_len)).astype(BF16)
        out[:, :, t * fine : (t + 1) * fine] = nn(mixed, interp[t]).reshape(
            members, level_len, fine
        )


def call(kernel, outs, ins, smem, scratch=(), flops=1 << 24):
    def spec(i):
        return pl.BlockSpec(memory_space=pltpu.SMEM if i < smem else pltpu.VMEM)

    return pl.pallas_call(
        kernel,
        out_shape=outs,
        in_specs=[spec(i) for i in range(len(ins))],
        out_specs=jax.tree.map(lambda _: pl.BlockSpec(memory_space=pltpu.VMEM), outs),
        scratch_shapes=list(scratch),
        compiler_params=pltpu.CompilerParams(vmem_limit_bytes=32 << 20),
        cost_estimate=pl.CostEstimate(flops=flops, bytes_accessed=1 << 20, transcendentals=0),
    )(*ins)


def shape(dims, dtype):
    return jax.ShapeDtypeStruct(dims, dtype)


def shards(fields, interp, conv_weight, vert_weight, send_tiles, tile_pattern):
    members, level_len, columns = fields.shape
    tiles, tile_len, fine = interp.shape
    halo = vert_weight.shape[1] - 1
    rows = members * level_len
    patches = lax.axis_size("patch")
    levs = lax.axis_size("lev")

    def shift(block, distance):
        return lax.ppermute(
            block, "patch", [(i, (i + distance) % patches) for i in range(patches)]
        )

    upward = [(i, i + 1) for i in range(levs - 1)]
    downward = [(i + 1, i) for i in range(levs - 1)]
    low = lax.ppermute(
        fields[:, level_len - halo :, :].reshape(members * halo, columns), "lev", upward
    )
    high = lax.ppermute(fields[:, :halo, :].reshape(members * halo, columns), "lev", downward)

    def restrict_body(*refs):
        restrict_kernel(members, level_len, halo, *refs)

    tile_shape = (rows, tile_len)
    partial, halo_matrix = call(
        restrict_body,
        (
            shape((tiles,) + tile_shape, F32),
            shape((rows, 4 * members * halo), BF16),
        ),
        (fields, interp, vert_weight),
        0,
    )
    four = shape((4,) + tile_shape, BF16)
    own, up, down = call(
        adjoint_kernel,
        (shape((tiles,) + tile_shape, F32), four, four),
        (tile_pattern, partial, halo_matrix, low, high, interp, conv_weight),
        1,
        [pltpu.VMEM((tiles + 8,) + tile_shape, F32)],
    )
    from_low = shift(up, 2)
    from_high = shift(down, -2)

    total, payload = call(
        partner_kernel,
        (shape((tiles,) + tile_shape, F32), shape((9,) + tile_shape, BF16)),
        (send_tiles, own, up, down, from_low, from_high),
        1,
    )
    arrived = lax.ppermute(payload, "patch", [(i, i ^ 1) for i in range(patches)])
    smooth, up, down = call(
        complete_kernel,
        (shape((tiles,) + tile_shape, BF16), four, four),
        (send_tiles, total, payload, arrived),
        1,
        [pltpu.VMEM((tiles,) + tile_shape, F32)],
    )
    from_low = shift(up, 2)
    from_high = shift(down, -2)
    return call(
        forward_kernel,
        shape(fields.shape, F32),
        (tile_pattern, smooth, up, down, from_low, from_high, interp, conv_weight),
        1,
        [pltpu.VMEM((tiles + 8,) + tile_shape, BF16)],
    )


def solution(mesh):
    in_specs = (
        P(None, "lev", "patch"),
        P("patch", None, None),
        P("patch", None, None, None),
        P(),
        P("patch", None, None),
        P("patch", None),
    )
    out_specs = P(None, "lev", "patch")
    return jax.shard_map(shards, mesh=mesh, in_specs=in_specs, out_specs=out_specs, check_vma=False)
```

time: 81.8 us -> 60.4 us (0.74)
  matrix products: 16 us -> 0 us
  Pallas kernels: 0 us -> 9.99 us
  starting transfers between devices: 41.1 us -> 33.3 us
  waiting for transfers between devices: 13.6 us -> 8.86 us
  other arithmetic: 2.16 us -> 0 us
    dot_general x6 -> x0, matrix products: 16 us -> none  [the longest x1 5.86 us: shards(): jnp.einsum('tke,tkri->eri', chosen.astype(jnp.float32), products, precisi...]
    pallas_call x0 -> x5, Pallas kernels: none -> 9.99 us  [call(): pl.pallas_call(kernel, out_shape=outs, in_specs=[spec(i) for i in range(l...]
    ppermute x10 -> x7, starting transfers between devices: 41.1 us -> 33.3 us  [the longest x4 24.8 us: shift(): lax.ppermute(block, 'patch', [(i, (i + distance) % patches) for i in rang...]
    ppermute x10 -> x7, waiting for transfers between devices: 13.6 us -> 8.86 us  [the longest x4 5.43 us: shift(): lax.ppermute(block, 'patch', [(i, (i + distance) % patches) for i in rang...]
    unnamed x30 -> x22, local copies, waits for them, and re-layouts: 2.15 us -> 6.27 us
    transpose x1 -> x0, local copies, waits for them, and re-layouts: 1.84 us -> none  [shards(): jnp.einsum('tro,tof->rtf', mixed, interp, preferred_element_type=jnp.floa...]
    another operation x2 -> x0, other arithmetic: 1.35 us -> none  [the longest x1 1.32 us: move_links(): jnp.stack([passed_along(pieces[position], 'patch', -offsets[position]) fo...]
    mul x2 -> x0, local copies, waits for them, and re-layouts: 1.31 us -> none  [the longest x1 0.66 us: vertical_adjoint(): factor[:, None]]
  transfers between devices with their start and end apart: 10 -> 7, of which waited for: 4 -> 6; matrix products, arithmetic and copies ran while one was open for 2% -> 2% of each run, Pallas kernels for 0% -> 2%
where the time goes in v1:
time: 60.4 us; the launch traced here: 59.9 us
  starting transfers between devices  33.3 us (55%)
  Pallas kernels  9.99 us (17%)
  waiting for transfers between devices  8.86 us (15%)
  local copies, waits for them, and re-layouts  7.64 us (13%)
    ppermute x4, starting transfers between devices, shift(): lax.ppermute(block, 'patch', [(i, (i + distance) % patches) for i in rang...  24.8 us
    pallas_call x5, Pallas kernels, call(): pl.pallas_call(kernel, out_shape=outs, in_specs=[spec(i) for i in range(l...  9.99 us
    unnamed x22, local copies, waits for them, and re-layouts  6.27 us
    ppermute x4, waiting for transfers between devices, shift(): lax.ppermute(block, 'patch', [(i, (i + distance) % patches) for i in rang...  5.43 us
    ppermute x1, starting transfers between devices, shards(): lax.ppermute(fields[:, level_len - halo:, :].reshape(members * halo, colu...  4.7 us
    ppermute x1, starting transfers between devices, shards(): lax.ppermute(fields[:, :halo, :].reshape(members * halo, columns), 'lev',...  1.92 us
    ppermute x1, starting transfers between devices, shards(): lax.ppermute(payload, 'patch', [(i, i ^ 1) for i in range(patches)])  1.92 us
    ppermute x1, waiting for transfers between devices, shards(): lax.ppermute(fields[:, :halo, :].reshape(members * halo, columns), 'lev',...  1.87 us
  transfers between devices with their start and end apart: 7, of which 6 were waited for; matrix products, arithmetic and copies ran while one was open for 2% of the time, Pallas kernels for 2%

profile of v1, /device:TPU:24, one launch (start us, length us, event | category | flops | bytes accessed | tf_op | source)
XLA Modules:
  0.0 59.9 jit_solution(8820506937498188346)
XLA Ops:
  0.0 0.0 copy-start
  0.0 1.3 %fusion = (bf16[8,4,2048]{2,1,0:T(4,128)(2,1)S(1)}, bf16[8,4,2048]{2,1,0:T(4,128)(2,1)S(1)}) fusion(bf16[8,16,2048]{2,1,0:T(8,128)(2,1)} %refs_0_.1), kind=kLoop, calls=%fused_computation | loop fusion | bytes 524288 | tf_op jit(solution)/shard_map/slice | solution.py:217
  1.3 4.7 %collective-permute-start = (bf16[32,2048]{1,0:T(8,128)(2,1)S(1)}, bf16[32,2048]{1,0:T(8,128)(2,1)S(1)}, u32[]{:S(2)}, u32[]{:S(2)}) collective-permute-start(bf16[32,2048]{1,0:T(8,128)(2,1)S(1)} %reshape.6), channel_id=1, source_target_pairs={{0,1},{1,2},{2,3},{3,4},{4,5},{5,6},{6,7},{8,9},{9,10},{10,11},{11... | collective-permute-start | bytes 393224 | tf_op jit(solution)/shard_map/ppermute | solution.py:214
  6.1 1.9 %collective-permute-start.1 = (bf16[32,2048]{1,0:T(8,128)(2,1)S(1)}, bf16[32,2048]{1,0:T(8,128)(2,1)S(1)}, u32[]{:S(2)}, u32[]{:S(2)}) collective-permute-start(bf16[32,2048]{1,0:T(8,128)(2,1)S(1)} %reshape.7), channel_id=1, source_target_pairs={{1,0},{2,1},{3,2},{4,3},{5,4},{6,5},{7,6},{9,8},{10,9},{11,10},{12... | collective-permute-start | bytes 393224 | tf_op jit(solution)/shard_map/ppermute | solution.py:217
  8.0 0.8 %copy.10.refs_2_ = f32[128,5]{1,0:T(8,128)S(1)} copy(f32[128,5]{0,1:T(8,128)} %param.9) | data formatting | bytes 5120 | tf_op args[3]
  8.8 0.0 copy-start.1
  8.8 1.0 %copy-done.1 = bf16[8,128,256]{2,1,0:T(8,128)(2,1)S(1)} copy-done((bf16[8,128,256]{2,1,0:T(8,128)(2,1)S(1)}, bf16[8,128,256]{2,1,0:T(8,128)(2,1)}, u32[]{:S(2)}) %copy-start.1) | copy-done | bytes 524312
  9.9 0.0 copy-start.4
  9.9 1.0 %copy-done.4 = bf16[8,16,2048]{2,1,0:T(8,128)(2,1)S(1)} copy-done((bf16[8,16,2048]{2,1,0:T(8,128)(2,1)S(1)}, bf16[8,16,2048]{2,1,0:T(8,128)(2,1)}, u32[]{:S(2)}) %copy-start.4) | copy-done | bytes 524312
  10.9 0.0 copy-start.9
  10.9 1.4 %shard_map.64 = (f32[8,128,128]{2,1,0:T(8,128)S(1)}, bf16[128,128]{1,0:T(8,128)(2,1)S(1)}) custom-call(bf16[8,16,2048]{2,1,0:T(8,128)(2,1)S(1)} %copy-done.4, bf16[8,128,256]{2,1,0:T(8,128)(2,1)S(1)} %copy-done.1, f32[128,5]{1,0:T(8,128)S(1)} %copy.10.refs_2_), custom_call_target="tpu_custom_call" | custom-call | flops 16777216 | bytes 1048576 | tf_op jit(solution)/shard_map/pallas_call | solution.py:184
  12.3 0.0 collective-permute-done.low
  12.3 1.9 %collective-permute-done.1.high = bf16[32,2048]{1,0:T(8,128)(2,1)S(1)} collective-permute-done((bf16[32,2048]{1,0:T(8,128)(2,1)S(1)}, bf16[32,2048]{1,0:T(8,128)(2,1)S(1)}, u32[]{:S(2)}, u32[]{:S(2)}) %collective-permute-start.1) | collective-permute-done | bytes 131104 | tf_op jit(solution)/shard_map/ppermute | solution.py:217
  14.2 0.0 copy-start.5
  14.2 0.7 %copy-done.5 = bf16[32,2048]{1,0:T(8,128)(2,1)} copy-done((bf16[32,2048]{1,0:T(8,128)(2,1)}, bf16[32,2048]{1,0:T(8,128)(2,1)S(1)}, u32[]{:S(2)}) %copy-start.5) | copy-done | bytes 131096
  14.8 0.0 copy-done
  14.8 0.0 copy-start.2
  14.8 1.0 %copy-done.2 = bf16[8,128,256]{2,1,0:T(8,128)(2,1)S(1)} copy-done((bf16[8,128,256]{2,1,0:T(8,128)(2,1)S(1)}, bf16[8,128,256]{2,1,0:T(8,128)(2,1)}, u32[]{:S(2)}) %copy-start.2) | copy-done | bytes 524312
  15.9 0.0 copy-start.6
  15.9 0.9 %copy-done.6 = bf16[32,2048]{1,0:T(8,128)(2,1)S(1)} copy-done((bf16[32,2048]{1,0:T(8,128)(2,1)S(1)}, bf16[32,2048]{1,0:T(8,128)(2,1)}, u32[]{:S(2)}) %copy-start.6) | copy-done | bytes 131096
  16.8 0.0 copy-start.7
  16.8 0.7 %copy-done.7 = s32[8,8]{1,0:T(8,128)S(1)} copy-done((s32[8,8]{1,0:T(8,128)S(1)}, s32[8,8]{1,0:T(8,128)}, u32[]{:S(2)}) %copy-start.7) | copy-done | bytes 280
  17.5 0.0 copy-start.3
  17.5 0.0 copy-start.8
  17.5 3.6 %shard_map.65 = (f32[8,128,128]{2,1,0:T(8,128)S(1)}, bf16[4,128,128]{2,1,0:T(8,128)(2,1)S(1)}, bf16[4,128,128]{2,1,0:T(8,128)(2,1)S(1)}) custom-call(s32[8,8]{1,0:T(8,128)S(1)} %copy-done.7, f32[8,128,128]{2,1,0:T(8,128)S(1)} %get-tuple-element.15.partial, bf16[128,128]{1,0:T(8,128)(2,1)S(1)} %get-tuple-element.16.halo_matrix, ...), custom_call_target="tpu_custom_call" | custom-call | flops 16777216 | bytes 1048576 | tf_op jit(solution)/shard_map/pallas_call | solution.py:184
  21.1 3.4 %collective-permute-start.2 = (bf16[4,128,128]{2,1,0:T(8,128)(2,1)S(1)}, bf16[4,128,128]{2,1,0:T(8,128)(2,1)S(1)}, u32[]{:S(2)}, u32[]{:S(2)}) collective-permute-start(bf16[4,128,128]{2,1,0:T(8,128)(2,1)S(1)} %get-tuple-element.18.up), channel_id=1, source_target_pairs={{0,16},{8,24},{16,32},{24,40},{32,48},{40,56},{48,64},{56,72},{64,... | collective-permute-start | bytes 393224 | tf_op jit(solution)/shard_map/ppermute | solution.py:208
  24.5 11.7 %collective-permute-start.3 = (bf16[4,128,128]{2,1,0:T(8,128)(2,1)S(1)}, bf16[4,128,128]{2,1,0:T(8,128)(2,1)}, u32[]{:S(2)}, u32[]{:S(2)}) collective-permute-start(bf16[4,128,128]{2,1,0:T(8,128)(2,1)S(1)} %get-tuple-element.19.down), channel_id=1, source_target_pairs={{0,496},{8,504},{16,0},{24,8},{32,16},{40,24},{48,32},{56,40},{64,... | collective-permute-start | bytes 393224 | tf_op jit(solution)/shard_map/ppermute | solution.py:208
  36.1 0.0 copy-done.9
  36.2 0.1 copy.12.send
  36.2 0.9 %collective-permute-done.2.from_low = bf16[4,128,128]{2,1,0:T(8,128)(2,1)S(1)} collective-permute-done((bf16[4,128,128]{2,1,0:T(8,128)(2,1)S(1)}, bf16[4,128,128]{2,1,0:T(8,128)(2,1)S(1)}, u32[]{:S(2)}, u32[]{:S(2)}) %collective-permute-start.2) | collective-permute-done | bytes 131104 | tf_op jit(solution)/shard_map/ppermute | solution.py:208
  37.1 1.5 %collective-permute-done.3.from_high = bf16[4,128,128]{2,1,0:T(8,128)(2,1)} collective-permute-done((bf16[4,128,128]{2,1,0:T(8,128)(2,1)S(1)}, bf16[4,128,128]{2,1,0:T(8,128)(2,1)}, u32[]{:S(2)}, u32[]{:S(2)}) %collective-permute-start.3) | collective-permute-done | bytes 131104 | tf_op jit(solution)/shard_map/ppermute | solution.py:208
  38.6 1.0 %shard_map.66 = (f32[8,128,128]{2,1,0:T(8,128)S(1)}, bf16[9,128,128]{2,1,0:T(8,128)(2,1)S(1)}) custom-call(s32[1,4,2]{2,1,0:T(4,128)S(1)} %copy.12.send, f32[8,128,128]{2,1,0:T(8,128)S(1)} %get-tuple-element.17.own, bf16[4,128,128]{2,1,0:T(8,128)(2,1)S(1)} %get-tuple-element.18.up, bf16[4,128,128]{2,1,0:T(8,128)(2,1)S(1)} %get-tuple-element.19.down, ...), custom_call_target="tpu_custom_call" | custom-call | flops 16777216 | bytes 1048576 | tf_op jit(solution)/shard_map/pallas_call | solution.py:184
  39.7 1.9 %collective-permute-start.4 = (bf16[9,128,128]{2,1,0:T(8,128)(2,1)S(1)}, bf16[9,128,128]{2,1,0:T(8,128)(2,1)S(1)}, u32[]{:S(2)}, u32[]{:S(2)}) collective-permute-start(bf16[9,128,128]{2,1,0:T(8,128)(2,1)S(1)} %get-tuple-element.21.payload), channel_id=1, source_target_pairs={{0,8},{8,0},{16,24},{24,16},{32,40},{40,32},{48,56},{56,48},{64,72... | collective-permute-start | bytes 884744 | tf_op jit(solution)/shard_map/ppermute | solution.py:249
  41.6 1.5 %collective-permute-done.4.arrived = bf16[9,128,128]{2,1,0:T(8,128)(2,1)S(1)} collective-permute-done((bf16[9,128,128]{2,1,0:T(8,128)(2,1)S(1)}, bf16[9,128,128]{2,1,0:T(8,128)(2,1)S(1)}, u32[]{:S(2)}, u32[]{:S(2)}) %collective-permute-start.4) | collective-permute-done | bytes 294944 | tf_op jit(solution)/shard_map/ppermute | solution.py:249
  43.1 0.8 %shard_map.67 = (bf16[8,128,128]{2,1,0:T(8,128)(2,1)S(1)}, bf16[4,128,128]{2,1,0:T(8,128)(2,1)S(1)}, bf16[4,128,128]{2,1,0:T(8,128)(2,1)S(1)}) custom-call(s32[1,4,2]{2,1,0:T(4,128)S(1)} %copy.12.send, f32[8,128,128]{2,1,0:T(8,128)S(1)} %get-tuple-element.20.partial, bf16[9,128,128]{2,1,0:T(8,128)(2,1)S(1)} %get-tuple-element.21.payload, ...), custom_call_target="tpu_custom_call" | custom-call | flops 16777216 | bytes 1048576 | tf_op jit(solution)/shard_map/pallas_call | solution.py:184
  43.9 1.9 %collective-permute-start.5 = (bf16[4,128,128]{2,1,0:T(8,128)(2,1)S(1)}, bf16[4,128,128]{2,1,0:T(8,128)(2,1)S(1)}, u32[]{:S(2)}, u32[]{:S(2)}) collective-permute-start(bf16[4,128,128]{2,1,0:T(8,128)(2,1)S(1)} %get-tuple-element.23.up), channel_id=1, source_target_pairs={{0,16},{8,24},{16,32},{24,40},{32,48},{40,56},{48,64},{56,72},{64,... | collective-permute-start | bytes 393224 | tf_op jit(solution)/shard_map/ppermute | solution.py:208
  45.8 7.8 %collective-permute-start.6 = (bf16[4,128,128]{2,1,0:T(8,128)(2,1)S(1)}, bf16[4,128,128]{2,1,0:T(8,128)(2,1)S(1)}, u32[]{:S(2)}, u32[]{:S(2)}) collective-permute-start(bf16[4,128,128]{2,1,0:T(8,128)(2,1)S(1)} %get-tuple-element.24.down), channel_id=1, source_target_pairs={{0,496},{8,504},{16,0},{24,8},{32,16},{40,24},{48,32},{56,40},{64,... | collective-permute-start | bytes 393224 | tf_op jit(solution)/shard_map/ppermute | solution.py:208
  53.6 1.9 %collective-permute-done.5.from_low = bf16[4,128,128]{2,1,0:T(8,128)(2,1)S(1)} collective-permute-done((bf16[4,128,128]{2,1,0:T(8,128)(2,1)S(1)}, bf16[4,128,128]{2,1,0:T(8,128)(2,1)S(1)}, u32[]{:S(2)}, u32[]{:S(2)}) %collective-permute-start.5) | collective-permute-done | bytes 131104 | tf_op jit(solution)/shard_map/ppermute | solution.py:208
  55.5 1.2 %collective-permute-done.6.from_high = bf16[4,128,128]{2,1,0:T(8,128)(2,1)S(1)} collective-permute-done((bf16[4,128,128]{2,1,0:T(8,128)(2,1)S(1)}, bf16[4,128,128]{2,1,0:T(8,128)(2,1)S(1)}, u32[]{:S(2)}, u32[]{:S(2)}) %collective-permute-start.6) | collective-permute-done | bytes 131104 | tf_op jit(solution)/shard_map/ppermute | solution.py:208
  56.7 0.0 copy-done.3
  56.7 0.0 copy-done.8
  56.7 3.2 %shard_map.68 = f32[8,16,2048]{2,1,0:T(8,128)} custom-call(s32[8,8]{1,0:T(8,128)S(1)} %copy-done.8, bf16[8,128,128]{2,1,0:T(8,128)(2,1)S(1)} %get-tuple-element.22.smooth, bf16[4,128,128]{2,1,0:T(8,128)(2,1)S(1)} %get-tuple-element.23.up, bf16[4,128,128]{2,1,0:T(8,128)(2,1)S(1)} %get-tuple-element.24.down, ...), custom_call_target="tpu_custom_call" | custom-call | flops 16777216 | bytes 1048576 | tf_op jit(solution)/shard_map/pallas_call | solution.py:184
  (2 shorter events, 0.1 us)
Async XLA Ops:
  0.0 14.8 %copy-start = (bf16[8,8,128,128]{3,2,1,0:T(8,128)(2,1)S(1)}, bf16[8,8,128,128]{3,2,1,0:T(8,128)(2,1)}, u32[]{:S(2)}) copy-start(bf16[8,8,128,128]{3,2,1,0:T(8,128)(2,1)} %conv.3) | copy-start | bytes 6291460
  1.3 10.9 %collective-permute-start = (bf16[32,2048]{1,0:T(8,128)(2,1)S(1)}, bf16[32,2048]{1,0:T(8,128)(2,1)S(1)}, u32[]{:S(2)}, u32[]{:S(2)}) collective-permute-start(bf16[32,2048]{1,0:T(8,128)(2,1)S(1)} %reshape.6), channel_id=1, source_target_pairs={{0,1},{1,2},{2,3},{3,4},{4,5},{5,6},{6,7},{8,9},{9,10},{10,11},{11... | collective-permute-start | bytes 393224 | tf_op jit(solution)/shard_map/ppermute | solution.py:214
  6.1 8.1 %collective-permute-start.1 = (bf16[32,2048]{1,0:T(8,128)(2,1)S(1)}, bf16[32,2048]{1,0:T(8,128)(2,1)S(1)}, u32[]{:S(2)}, u32[]{:S(2)}) collective-permute-start(bf16[32,2048]{1,0:T(8,128)(2,1)S(1)} %reshape.7), channel_id=1, source_target_pairs={{1,0},{2,1},{3,2},{4,3},{5,4},{6,5},{7,6},{9,8},{10,9},{11,10},{12... | collective-permute-start | bytes 393224 | tf_op jit(solution)/shard_map/ppermute | solution.py:217
  8.8 1.0 %copy-start.1 = (bf16[8,128,256]{2,1,0:T(8,128)(2,1)S(1)}, bf16[8,128,256]{2,1,0:T(8,128)(2,1)}, u32[]{:S(2)}) copy-start(bf16[8,128,256]{2,1,0:T(8,128)(2,1)} %interp.3) | copy-start | bytes 1572868
  9.9 1.0 %copy-start.4 = (bf16[8,16,2048]{2,1,0:T(8,128)(2,1)S(1)}, bf16[8,16,2048]{2,1,0:T(8,128)(2,1)}, u32[]{:S(2)}) copy-start(bf16[8,16,2048]{2,1,0:T(8,128)(2,1)} %refs_0_.1) | copy-start | bytes 1572868
  10.9 25.2 %copy-start.9 = (s32[1,4,2]{1,2,0:T(2,128)S(1)}, s32[1,4,2]{1,2,0:T(2,128)}, u32[]{:S(2)}) copy-start(s32[1,4,2]{1,2,0:T(2,128)} %param.10) | copy-start | bytes 100
  14.2 0.7 %copy-start.5 = (bf16[32,2048]{1,0:T(8,128)(2,1)}, bf16[32,2048]{1,0:T(8,128)(2,1)S(1)}, u32[]{:S(2)}) copy-start(bf16[32,2048]{1,0:T(8,128)(2,1)S(1)} %collective-permute-done.1.high) | copy-start | bytes 393220
  14.8 1.0 %copy-start.2 = (bf16[8,128,256]{2,1,0:T(8,128)(2,1)S(1)}, bf16[8,128,256]{2,1,0:T(8,128)(2,1)}, u32[]{:S(2)}) copy-start(bf16[8,128,256]{2,1,0:T(8,128)(2,1)} %interp.3) | copy-start | bytes 1572868
  15.9 0.9 %copy-start.6 = (bf16[32,2048]{1,0:T(8,128)(2,1)S(1)}, bf16[32,2048]{1,0:T(8,128)(2,1)}, u32[]{:S(2)}) copy-start(bf16[32,2048]{1,0:T(8,128)(2,1)} %copy-done.5) | copy-start | bytes 393220
  16.8 0.7 %copy-start.7 = (s32[8,8]{1,0:T(8,128)S(1)}, s32[8,8]{1,0:T(8,128)}, u32[]{:S(2)}) copy-start(s32[8,8]{1,0:T(8,128)} %pattern.3) | copy-start | bytes 772
  17.5 39.2 %copy-start.3 = (bf16[8,128,256]{2,1,0:T(8,128)(2,1)S(1)}, bf16[8,128,256]{2,1,0:T(8,128)(2,1)}, u32[]{:S(2)}) copy-start(bf16[8,128,256]{2,1,0:T(8,128)(2,1)} %interp.3) | copy-start | bytes 1572868
  17.5 39.2 %copy-start.8 = (s32[8,8]{1,0:T(8,128)S(1)}, s32[8,8]{1,0:T(8,128)}, u32[]{:S(2)}) copy-start(s32[8,8]{1,0:T(8,128)} %pattern.3) | copy-start | bytes 772
  21.1 16.1 %collective-permute-start.2 = (bf16[4,128,128]{2,1,0:T(8,128)(2,1)S(1)}, bf16[4,128,128]{2,1,0:T(8,128)(2,1)S(1)}, u32[]{:S(2)}, u32[]{:S(2)}) collective-permute-start(bf16[4,128,128]{2,1,0:T(8,128)(2,1)S(1)} %get-tuple-element.18.up), channel_id=1, source_target_pairs={{0,16},{8,24},{16,32},{24,40},{32,48},{40,56},{48,64},{56,72},{64,... | collective-permute-start | bytes 393224 | tf_op jit(solution)/shard_map/ppermute | solution.py:208
  24.5 14.2 %collective-permute-start.3 = (bf16[4,128,128]{2,1,0:T(8,128)(2,1)S(1)}, bf16[4,128,128]{2,1,0:T(8,128)(2,1)}, u32[]{:S(2)}, u32[]{:S(2)}) collective-permute-start(bf16[4,128,128]{2,1,0:T(8,128)(2,1)S(1)} %get-tuple-element.19.down), channel_id=1, source_target_pairs={{0,496},{8,504},{16,0},{24,8},{32,16},{40,24},{48,32},{56,40},{64,... | collective-permute-start | bytes 393224 | tf_op jit(solution)/shard_map/ppermute | solution.py:208
  39.7 3.5 %collective-permute-start.4 = (bf16[9,128,128]{2,1,0:T(8,128)(2,1)S(1)}, bf16[9,128,128]{2,1,0:T(8,128)(2,1)S(1)}, u32[]{:S(2)}, u32[]{:S(2)}) collective-permute-start(bf16[9,128,128]{2,1,0:T(8,128)(2,1)S(1)} %get-tuple-element.21.payload), channel_id=1, source_target_pairs={{0,8},{8,0},{16,24},{24,16},{32,40},{40,32},{48,56},{56,48},{64,72... | collective-permute-start | bytes 884744 | tf_op jit(solution)/shard_map/ppermute | solution.py:249
  43.9 11.6 %collective-permute-start.5 = (bf16[4,128,128]{2,1,0:T(8,128)(2,1)S(1)}, bf16[4,128,128]{2,1,0:T(8,128)(2,1)S(1)}, u32[]{:S(2)}, u32[]{:S(2)}) collective-permute-start(bf16[4,128,128]{2,1,0:T(8,128)(2,1)S(1)} %get-tuple-element.23.up), channel_id=1, source_target_pairs={{0,16},{8,24},{16,32},{24,40},{32,48},{40,56},{48,64},{56,72},{64,... | collective-permute-start | bytes 393224 | tf_op jit(solution)/shard_map/ppermute | solution.py:208
  45.8 10.8 %collective-permute-start.6 = (bf16[4,128,128]{2,1,0:T(8,128)(2,1)S(1)}, bf16[4,128,128]{2,1,0:T(8,128)(2,1)S(1)}, u32[]{:S(2)}, u32[]{:S(2)}) collective-permute-start(bf16[4,128,128]{2,1,0:T(8,128)(2,1)S(1)} %get-tuple-element.24.down), channel_id=1, source_target_pairs={{0,496},{8,504},{16,0},{24,8},{32,16},{40,24},{48,32},{56,40},{64,... | collective-permute-start | bytes 393224 | tf_op jit(solution)/shard_map/ppermute | solution.py:208

commit v2 on v1

v2 whole, which is shorter than its diff:
```python
import functools

import jax
import jax.numpy as jnp
from jax import lax
from jax.experimental import pallas as pl
from jax.experimental.pallas import tpu as pltpu
from jax.sharding import PartitionSpec as P

BF16 = jnp.bfloat16
F32 = jnp.float32
HIGHEST = lax.Precision.HIGHEST


def nn(a, b):
    return lax.dot_general(a, b, (((1,), (0,)), ((), ())), preferred_element_type=F32)


def nt(a, b):
    return lax.dot_general(a, b, (((1,), (1,)), ((), ())), preferred_element_type=F32)


def iota(shape, dim):
    return lax.broadcasted_iota(jnp.int32, shape, dim)


def split(a):
    high = a.astype(BF16)
    return high, (a - high.astype(F32)).astype(BF16)


def restrict_kernel(halo, fields, interp, coarse, top, bottom, blocks, bases, sems):
    tiles, tile_len, fine = bases.shape
    members, level_len, _ = blocks.shape[1:]
    rows = members * level_len
    halo_rows = members * halo
    copies = []
    for t in range(tiles):
        pair = (
            pltpu.make_async_copy(
                fields.at[:, :, pl.ds(t * fine, fine)], blocks.at[t], sems.at[0, t]
            ),
            pltpu.make_async_copy(interp.at[t], bases.at[t], sems.at[1, t]),
        )
        for copy in pair:
            copy.start()
        copies.append(pair)
    place = iota((2 * halo_rows, rows), 0)
    level = jnp.where(place < halo_rows, place % halo, level_len - halo + place % halo)
    source = (place % halo_rows) // halo * level_len + level
    pick = (iota((2 * halo_rows, rows), 1) == source).astype(BF16)
    for t in range(tiles):
        for copy in copies[t]:
            copy.wait()
        value = nt(blocks[t].reshape(rows, fine), bases[t]).astype(BF16)
        coarse[t] = value
        edge = nn(pick, value).astype(BF16)
        bottom[t] = edge[:halo_rows]
        top[t] = edge[halo_rows:]


def vertical_kernel(
    level_len, halo, coarse, weights, pattern, conv, partial, halo_matrix, pattern_copy,
    conv_copy, sem
):
    fetch = pltpu.make_async_copy(conv, conv_copy, sem)
    fetch.start()
    tiles, rows, tile_len = coarse.shape
    halo_rows = rows // level_len * halo
    levels, taps = weights.shape
    half = taps // 2
    pattern_copy[...] = pattern[...]
    start = lax.axis_index("lev") * level_len
    distance = iota((levels, levels), 1) - iota((levels, levels), 0)
    table = weights[...]
    band = jnp.zeros((levels, levels), F32)
    for j in range(taps):
        band = band + jnp.where(distance == j - half, table[:, j : j + 1], 0.0)
    both = lax.dot_general(
        band, band, (((1,), (1,)), ((), ())), precision=HIGHEST, preferred_element_type=F32
    )
    pick = (
        iota((rows, levels), 1) == start + iota((rows, levels), 0) % level_len
    ).astype(BF16)
    place = iota((2 * halo_rows, levels), 0)
    level = jnp.where(
        place < halo_rows, start - halo + place % halo, start + level_len + place % halo
    )
    pick_halo = (iota((2 * halo_rows, levels), 1) == level).astype(BF16)
    same = iota((rows, rows), 0) // level_len == iota((rows, rows), 1) // level_len
    column = iota((rows, 2 * halo_rows), 1) % halo_rows
    same_halo = iota((rows, 2 * halo_rows), 0) // level_len == column // halo
    own_parts = []
    for i, part in enumerate(split(both)):
        chosen = nn(pick, part).astype(BF16)
        own_parts.append(jnp.where(same, nt(chosen, pick), 0.0).astype(BF16))
        halo_matrix[:, i * 2 * halo_rows : (i + 1) * 2 * halo_rows] = jnp.where(
            same_halo, nt(chosen, pick_halo), 0.0
        ).astype(BF16)
    own_matrix = jnp.concatenate(own_parts, axis=1)
    for t in range(tiles):
        value = coarse[t]
        partial[t] = nn(own_matrix, jnp.concatenate([value, value], axis=0))
    fetch.wait()


def by_chip(body, first, second):
    odd = lax.axis_index("patch") // 2 % 2

    @pl.when(odd == 0)
    def _():
        body(second, first)

    @pl.when(odd == 1)
    def _():
        body(first, second)


def adjoint_kernel(pattern, partial, halo_matrix, low, high, conv, own, second, first, entries):
    tiles, rows, tile_len = partial.shape
    count = conv.shape[1]
    entries[...] = jnp.zeros_like(entries)
    matrix = halo_matrix[...]
    for t in range(tiles):
        edge = jnp.concatenate([low[t], high[t]], axis=0)
        smooth = partial[t] + nn(matrix, jnp.concatenate([edge, edge], axis=0))
        products = nt(
            smooth.astype(BF16), conv[t].reshape(count * tile_len, tile_len)
        )
        for k in range(count):
            entry = pattern[t, k]
            entries[entry] += products[:, k * tile_len : (k + 1) * tile_len]
    own[...] = entries[:tiles]

    def sides(down, up):
        up[...] = entries[tiles : tiles + 4].astype(BF16)
        down[0:2] = entries[tiles + 6 : tiles + 8].astype(BF16)
        down[2:4] = entries[tiles + 4 : tiles + 6].astype(BF16)

    by_chip(sides, first, second)


def add_to(total, tile, piece):
    @pl.when(tile < total.shape[0])
    def _():
        total[tile] += piece.astype(F32)


def partner_kernel(send, own, first, second, from_first, from_second, payload):
    tiles = own.shape[0]
    core = lax.axis_index("patch") % 2

    def sides(low, high):
        (down, from_low), (up, from_high) = low, high

        @pl.when(core == 0)
        def _():
            payload[0:2] = up[2:4]
            payload[2:4] = from_high[2:4]

        @pl.when(core == 1)
        def _():
            payload[0:2] = from_low[2:4]
            payload[2:4] = down[2:4]

        for o in range(2):
            for s in range(2):
                tile = send[0, 1 + o, s]
                value = own[jnp.minimum(tile, tiles - 1)]
                for back in range(2):
                    value = value + jnp.where(
                        send[0, 0, back] == tile, from_low[back].astype(F32), 0.0
                    )
                    value = value + jnp.where(
                        send[0, 3, back] == tile, from_high[back].astype(F32), 0.0
                    )
                payload[4 + 2 * o + s] = value.astype(BF16)
                payload[8, 16 * (2 * o + s) : 16 * (2 * o + s) + 16, :] = jnp.full(
                    (16, payload.shape[2]), tile.astype(F32)
                ).astype(BF16)

    by_chip(sides, (first, from_first), (second, from_second))


def gather_kernel(send, own, from_first, from_second, total):
    total[...] = own[...]

    def sides(from_low, from_high):
        for s in range(2):
            add_to(total, send[0, 0, s], from_low[s])
            add_to(total, send[0, 3, s], from_high[s])

    by_chip(sides, from_first, from_second)


def complete_kernel(send, partial, payload, arrived, smooth, second, first, total):
    tiles = partial.shape[0]
    total[...] = partial[...]
    for o in range(2):
        for s in range(2):
            add_to(total, send[0, 1 + o, s], arrived[2 * o + s])
    smooth[...] = total[...].astype(BF16)

    def sides(down, up):
        for s in range(2):
            down[s] = smooth[jnp.minimum(send[0, 0, s], tiles - 1)]
            up[s] = smooth[jnp.minimum(send[0, 3, s], tiles - 1)]
        marks = [arrived[8, 16 * i : 16 * i + 1, :].astype(F32) for i in range(4)]
        for o in range(2):
            out = (down, up)[o]
            for s in range(2):
                mine = 2 * o + s
                tile = arrived[4 + mine].astype(F32) + payload[mine].astype(F32)
                for other in range(2):
                    theirs = 2 * (1 - o) + other
                    tile = tile + jnp.where(
                        marks[mine] == marks[theirs], payload[theirs].astype(F32), 0.0
                    )
                out[2 + s] = tile.astype(BF16)

    by_chip(sides, first, second)


def forward_kernel(
    pattern, smooth, first, second, from_first, from_second, interp, conv, out, entries
):
    tiles, tile_len, fine = interp.shape
    count = conv.shape[1]
    members, level_len, _ = out.shape
    core = lax.axis_index("patch") % 2
    entries[0:tiles] = smooth[...]

    def sides(low, high):
        (down, from_low), (up, from_high) = low, high
        entries[tiles : tiles + 2] = from_high[0:2]
        entries[tiles + 6 : tiles + 8] = from_low[0:2]

        @pl.when(core == 0)
        def _():
            entries[tiles + 2 : tiles + 4] = down[2:4]
            entries[tiles + 4 : tiles + 6] = from_low[2:4]

        @pl.when(core == 1)
        def _():
            entries[tiles + 2 : tiles + 4] = from_high[2:4]
            entries[tiles + 4 : tiles + 6] = up[2:4]

    by_chip(sides, (first, from_first), (second, from_second))
    for t in range(tiles):
        picked = jnp.concatenate([entries[pattern[t, k]] for k in range(count)], axis=1)
        mixed = nn(picked, conv[t].reshape(count * tile_len, tile_len)).astype(BF16)
        out[:, :, t * fine : (t + 1) * fine] = nn(mixed, interp[t]).reshape(
            members, level_len, fine
        )


VMEM = pl.BlockSpec(memory_space=pltpu.VMEM)
SMEM = pl.BlockSpec(memory_space=pltpu.SMEM)
HBM = pl.BlockSpec(memory_space=pltpu.HBM)


def in_hbm(array):
    return pltpu.with_memory_space_constraint(array, pltpu.HBM)


def call(kernel, outs, specs, ins, scratch=(), flops=1 << 24):
    return pl.pallas_call(
        kernel,
        out_shape=outs,
        in_specs=specs,
        out_specs=jax.tree.map(lambda _: VMEM, outs),
        scratch_shapes=list(scratch),
        compiler_params=pltpu.CompilerParams(vmem_limit_bytes=16 << 20),
        cost_estimate=pl.CostEstimate(flops=flops, bytes_accessed=1 << 20, transcendentals=0),
    )(*ins)


def shape(dims, dtype):
    return jax.ShapeDtypeStruct(dims, dtype)


def shards(fields, interp, conv_weight, vert_weight, send_tiles, tile_pattern):
    members, level_len, columns = fields.shape
    tiles, tile_len, fine = interp.shape
    halo = vert_weight.shape[1] - 1
    rows = members * level_len
    patches = lax.axis_size("patch")
    levs = lax.axis_size("lev")
    tile_shape = (rows, tile_len)
    tile_list = shape((tiles,) + tile_shape, F32)
    narrow_list = shape((tiles,) + tile_shape, BF16)
    edge_list = shape((tiles, members * halo, tile_len), BF16)
    four = shape((4,) + tile_shape, BF16)

    def swap(block, start):
        partner = [
            (i, (i + 2) % patches if (i - start) % 4 < 2 else (i - 2) % patches)
            for i in range(patches)
        ]
        return lax.ppermute(block, "patch", partner)

    coarse, top, bottom = call(
        functools.partial(restrict_kernel, halo),
        (narrow_list, edge_list, edge_list),
        [HBM, HBM],
        (in_hbm(fields), in_hbm(interp)),
        [
            pltpu.VMEM((tiles, members, level_len, fine), BF16),
            pltpu.VMEM((tiles, tile_len, fine), BF16),
            pltpu.SemaphoreType.DMA((2, tiles)),
        ],
    )
    low = lax.ppermute(top, "lev", [(i, i + 1) for i in range(levs - 1)])
    high = lax.ppermute(bottom, "lev", [(i + 1, i) for i in range(levs - 1)])
    partial, halo_matrix, pattern, conv = call(
        functools.partial(vertical_kernel, level_len, halo),
        (
            tile_list,
            shape((rows, 4 * members * halo), BF16),
            shape(tile_pattern.shape, jnp.int32),
            shape(conv_weight.shape, BF16),
        ),
        [VMEM] * 3 + [HBM],
        (coarse, vert_weight, tile_pattern, in_hbm(conv_weight)),
        [pltpu.SemaphoreType.DMA],
    )
    own, second, first = call(
        adjoint_kernel,
        (tile_list, four, four),
        [SMEM] + [VMEM] * 5,
        (pattern, partial, halo_matrix, low, high, conv),
        [pltpu.VMEM((tiles + 8,) + tile_shape, F32)],
    )
    from_second = swap(second, 2)
    from_first = swap(first, 0)
    payload = call(
        partner_kernel,
        shape((9,) + tile_shape, BF16),
        [SMEM] + [VMEM] * 5,
        (send_tiles, own, first, second, from_first, from_second),
    )
    arrived = lax.ppermute(payload, "patch", [(i, i ^ 1) for i in range(patches)])
    total = call(
        gather_kernel,
        tile_list,
        [SMEM] + [VMEM] * 3,
        (send_tiles, own, from_first, from_second),
    )
    smooth, second, first = call(
        complete_kernel,
        (narrow_list, four, four),
        [SMEM] + [VMEM] * 3,
        (send_tiles, total, payload, arrived),
        [pltpu.VMEM((tiles,) + tile_shape, F32)],
    )
    from_second = swap(second, 2)
    from_first = swap(first, 0)
    return call(
        forward_kernel,
        shape(fields.shape, F32),
        [SMEM] + [VMEM] * 7,
        (pattern, smooth, first, second, from_first, from_second, interp, conv),
        [pltpu.VMEM((tiles + 8,) + tile_shape, BF16)],
    )


def solution(mesh):
    in_specs = (
        P(None, "lev", "patch"),
        P("patch", None, None),
        P("patch", None, None, None),
        P(),
        P("patch", None, None),
        P("patch", None),
    )
    out_specs = P(None, "lev", "patch")
    return jax.shard_map(shards, mesh=mesh, in_specs=in_specs, out_specs=out_specs, check_vma=False)
```

time: 60.4 us -> 59.6 us (0.987)
  local copies, waits for them, and re-layouts: 7.64 us -> 1.58 us
  Pallas kernels: 9.99 us -> 14.9 us
    pallas_call x5 -> x7, Pallas kernels: 9.99 us -> 14.9 us  [call(): pl.pallas_call(kernel, out_shape=outs, in_specs=specs, out_specs=jax.tree...]
    unnamed x22 -> x8, local copies, waits for them, and re-layouts: 6.27 us -> 1.58 us
    slice x1 -> x0, local copies, waits for them, and re-layouts: 1.3 us -> none  [shards(): fields[:, :halo, :].reshape(members * halo, columns)]
    ppermute x1, waiting for transfers between devices: 1.55 us -> 0.89 us  [shards(): lax.ppermute(payload, 'patch', [(i, i ^ 1) for i in range(patches)])]
    ppermute x6, waiting for transfers between devices: 7.31 us -> 7.95 us  [the longest x4 6.6 us: swap(): return lax.ppermute(block, 'patch', partner)]
  transfers between devices with their start and end apart: 7 -> 7, of which waited for: 6 -> 4; matrix products, arithmetic and copies ran while one was open for 2% -> 2% of each run, Pallas kernels for 2% -> 5%
where the time goes in v2:
time: 59.6 us; the launch traced here: 59.2 us
  starting transfers between devices  33.7 us (57%)
  Pallas kernels  14.9 us (25%)
  waiting for transfers between devices  8.84 us (15%)
  local copies, waits for them, and re-layouts  1.58 us (3%)
    ppermute x4, starting transfers between devices, swap(): return lax.ppermute(block, 'patch', partner)  25.2 us
    pallas_call x7, Pallas kernels, call(): pl.pallas_call(kernel, out_shape=outs, in_specs=specs, out_specs=jax.tree...  14.9 us
    ppermute x4, waiting for transfers between devices, swap(): return lax.ppermute(block, 'patch', partner)  6.6 us
    ppermute x1, starting transfers between devices, shards(): low = lax.ppermute(top, 'lev', [(i, i + 1) for i in range(levs - 1)])  4.69 us
    ppermute x1, starting transfers between devices, shards(): high = lax.ppermute(bottom, 'lev', [(i + 1, i) for i in range(levs - 1)])  1.92 us
    ppermute x1, starting transfers between devices, shards(): lax.ppermute(payload, 'patch', [(i, i ^ 1) for i in range(patches)])  1.92 us
    unnamed x8, local copies, waits for them, and re-layouts  1.58 us
    ppermute x1, waiting for transfers between devices, shards(): high = lax.ppermute(bottom, 'lev', [(i + 1, i) for i in range(levs - 1)])  1.35 us
  transfers between devices with their start and end apart: 7, of which 4 were waited for; matrix products, arithmetic and copies ran while one was open for 2% of the time, Pallas kernels for 5%

profile of v2, /device:TPU:24, one launch (start us, length us, event | category | flops | bytes accessed | tf_op | source)
XLA Modules:
  0.0 59.2 jit_solution(6284053772261708208)
XLA Ops:
  0.0 3.5 %shard_map.64 = (bf16[8,128,128]{2,1,0:T(8,128)(2,1)S(1)}, bf16[8,32,128]{2,1,0:T(8,128)(2,1)S(1)}, bf16[8,32,128]{2,1,0:T(8,128)(2,1)S(1)}) custom-call(bf16[8,16,2048]{2,1,0:T(8,128)(2,1)} %fields.1, bf16[8,128,256]{2,1,0:T(8,128)(2,1)} %interp.3), custom_call_target="tpu_custom_call" | custom-call | flops 16777216 | bytes 1048576 | tf_op jit(solution)/shard_map/pallas_call | solution.py:267
  3.5 4.7 %collective-permute-start = (bf16[8,32,128]{2,1,0:T(8,128)(2,1)S(1)}, bf16[8,32,128]{2,1,0:T(8,128)(2,1)S(1)}, u32[]{:S(2)}, u32[]{:S(2)}) collective-permute-start(bf16[8,32,128]{2,1,0:T(8,128)(2,1)S(1)} %get-tuple-element.22), channel_id=1, source_target_pairs={{0,1},{1,2},{2,3},{3,4},{4,5},{5,6},{6,7},{8,9},{9,10},{10,11},{11... | collective-permute-start | bytes 196616 | tf_op jit(solution)/shard_map/ppermute | solution.py:313
  8.2 1.9 %collective-permute-start.1 = (bf16[8,32,128]{2,1,0:T(8,128)(2,1)S(1)}, bf16[8,32,128]{2,1,0:T(8,128)(2,1)S(1)}, u32[]{:S(2)}, u32[]{:S(2)}) collective-permute-start(bf16[8,32,128]{2,1,0:T(8,128)(2,1)S(1)} %get-tuple-element.23), channel_id=1, source_target_pairs={{1,0},{2,1},{3,2},{4,3},{5,4},{6,5},{7,6},{9,8},{10,9},{11,10},{12... | collective-permute-start | bytes 196616 | tf_op jit(solution)/shard_map/ppermute | solution.py:314
  10.1 0.8 %copy.7.weights = f32[128,5]{1,0:T(8,128)S(1)} copy(f32[128,5]{0,1:T(8,128)} %param.9) | data formatting | bytes 5120 | tf_op args[3]
  10.9 0.0 copy-start.1
  10.9 0.7 %copy-done.1 = s32[8,8]{1,0:T(8,128)S(1)} copy-done((s32[8,8]{1,0:T(8,128)S(1)}, s32[8,8]{1,0:T(8,128)}, u32[]{:S(2)}) %copy-start.1) | copy-done | bytes 280
  11.6 0.0 copy-start.2
  11.6 2.6 %shard_map.65 = (f32[8,128,128]{2,1,0:T(8,128)S(1)}, bf16[128,128]{1,0:T(8,128)(2,1)S(1)}, s32[8,8]{1,0:T(8,128)S(1)}, bf16[8,8,128,128]{3,2,1,0:T(8,128)(2,1)S(1)}) custom-call(bf16[8,128,128]{2,1,0:T(8,128)(2,1)S(1)} %get-tuple-element.18.coarse, f32[128,5]{1,0:T(8,128)S(1)} %copy.7.weights, s32[8,8]{1,0:T(8,128)S(1)} %copy-done.1, ...), custom_call_target="tpu_custom_call" | custom-call | flops 16777216 | bytes 1048576 | tf_op jit(solution)/shard_map/pallas_call | solution.py:267
  14.2 0.0 collective-permute-done.low
  14.2 1.3 %collective-permute-done.1.high = bf16[8,32,128]{2,1,0:T(8,128)(2,1)S(1)} collective-permute-done((bf16[8,32,128]{2,1,0:T(8,128)(2,1)S(1)}, bf16[8,32,128]{2,1,0:T(8,128)(2,1)S(1)}, u32[]{:S(2)}, u32[]{:S(2)}) %collective-permute-start.1) | collective-permute-done | bytes 65568 | tf_op jit(solution)/shard_map/ppermute | solution.py:314
  15.5 3.2 %shard_map.66 = (f32[8,128,128]{2,1,0:T(8,128)S(1)}, bf16[4,128,128]{2,1,0:T(8,128)(2,1)S(1)}, bf16[4,128,128]{2,1,0:T(8,128)(2,1)}) custom-call(s32[8,8]{1,0:T(8,128)S(1)} %get-tuple-element.19.pattern, f32[8,128,128]{2,1,0:T(8,128)S(1)} %get-tuple-element.20.partial, bf16[128,128]{1,0:T(8,128)(2,1)S(1)} %get-tuple-element.21.halo_matrix, ...), custom_call_target="tpu_custom_call" | custom-call | flops 16777216 | bytes 1048576 | tf_op jit(solution)/shard_map/pallas_call | solution.py:267
  18.7 0.0 copy-start
  18.7 3.5 %collective-permute-start.2 = (bf16[4,128,128]{2,1,0:T(8,128)(2,1)}, bf16[4,128,128]{2,1,0:T(8,128)(2,1)S(1)}, u32[]{:S(2)}, u32[]{:S(2)}) collective-permute-start(bf16[4,128,128]{2,1,0:T(8,128)(2,1)} %get-tuple-element.26.first), channel_id=1, source_target_pairs={{0,16},{8,24},{16,0},{24,8},{32,48},{40,56},{48,32},{56,40},{64,80... | collective-permute-start | bytes 393224 | tf_op jit(solution)/shard_map/ppermute | solution.py:300
  22.2 12.5 %collective-permute-start.3 = (bf16[4,128,128]{2,1,0:T(8,128)(2,1)S(1)}, bf16[4,128,128]{2,1,0:T(8,128)(2,1)S(1)}, u32[]{:S(2)}, u32[]{:S(2)}) collective-permute-start(bf16[4,128,128]{2,1,0:T(8,128)(2,1)S(1)} %get-tuple-element.27.second), channel_id=1, source_target_pairs={{0,496},{8,504},{16,32},{24,40},{32,16},{40,24},{48,64},{56,72},{6... | collective-permute-start | bytes 393224 | tf_op jit(solution)/shard_map/ppermute | solution.py:300
  34.7 0.0 copy-done.2
  34.7 0.1 copy.10.send
  34.8 0.0 collective-permute-done.2.from_first
  34.8 2.8 %collective-permute-done.3.from_second = bf16[4,128,128]{2,1,0:T(8,128)(2,1)S(1)} collective-permute-done((bf16[4,128,128]{2,1,0:T(8,128)(2,1)S(1)}, bf16[4,128,128]{2,1,0:T(8,128)(2,1)S(1)}, u32[]{:S(2)}, u32[]{:S(2)}) %collective-permute-start.3) | collective-permute-done | bytes 131104 | tf_op jit(solution)/shard_map/ppermute | solution.py:300
  37.7 1.1 %shard_map.68.payload = bf16[9,128,128]{2,1,0:T(8,128)(2,1)S(1)} custom-call(s32[1,4,2]{2,1,0:T(4,128)S(1)} %copy.10.send, f32[8,128,128]{2,1,0:T(8,128)S(1)} %get-tuple-element.25.own, bf16[4,128,128]{2,1,0:T(8,128)(2,1)} %get-tuple-element.26.first, bf16[4,128,128]{2,1,0:T(8,128)(2,1)S(1)} %get-tuple-element.27.second, ...), custom_call_target="tpu_custom_call" | custom-call | flops 16777216 | bytes 1048576 | tf_op jit(solution)/shard_map/pallas_call | solution.py:267
  38.7 1.9 %collective-permute-start.4 = (bf16[9,128,128]{2,1,0:T(8,128)(2,1)S(1)}, bf16[9,128,128]{2,1,0:T(8,128)(2,1)S(1)}, u32[]{:S(2)}, u32[]{:S(2)}) collective-permute-start(bf16[9,128,128]{2,1,0:T(8,128)(2,1)S(1)} %shard_map.68.payload), channel_id=1, source_target_pairs={{0,8},{8,0},{16,24},{24,16},{32,40},{40,32},{48,56},{56,48},{64,72... | collective-permute-start | bytes 884744 | tf_op jit(solution)/shard_map/ppermute | solution.py:342
  40.7 0.6 %shard_map.67.partial = f32[8,128,128]{2,1,0:T(8,128)S(1)} custom-call(s32[1,4,2]{2,1,0:T(4,128)S(1)} %copy.10.send, f32[8,128,128]{2,1,0:T(8,128)S(1)} %get-tuple-element.25.own, bf16[4,128,128]{2,1,0:T(8,128)(2,1)S(1)} %collective-permute-done.2.from_first, bf16[4,128,128]{2,1,0:T(8,128)(2,1)S(1)} %collective-permute-done.3.from_second), custom_call_target="tpu_custom_call" | custom-call | flops 16777216 | bytes 1048576 | tf_op jit(solution)/shard_map/pallas_call | solution.py:267
  41.3 0.9 %collective-permute-done.4.arrived = bf16[9,128,128]{2,1,0:T(8,128)(2,1)S(1)} collective-permute-done((bf16[9,128,128]{2,1,0:T(8,128)(2,1)S(1)}, bf16[9,128,128]{2,1,0:T(8,128)(2,1)S(1)}, u32[]{:S(2)}, u32[]{:S(2)}) %collective-permute-start.4) | collective-permute-done | bytes 294944 | tf_op jit(solution)/shard_map/ppermute | solution.py:342
  42.2 0.8 %shard_map.69 = (bf16[8,128,128]{2,1,0:T(8,128)(2,1)S(1)}, bf16[4,128,128]{2,1,0:T(8,128)(2,1)S(1)}, bf16[4,128,128]{2,1,0:T(8,128)(2,1)S(1)}) custom-call(s32[1,4,2]{2,1,0:T(4,128)S(1)} %copy.10.send, f32[8,128,128]{2,1,0:T(8,128)S(1)} %shard_map.67.partial, bf16[9,128,128]{2,1,0:T(8,128)(2,1)S(1)} %shard_map.68.payload, ...), custom_call_target="tpu_custom_call" | custom-call | flops 16777216 | bytes 1048576 | tf_op jit(solution)/shard_map/pallas_call | solution.py:267
  43.0 1.9 %collective-permute-start.5 = (bf16[4,128,128]{2,1,0:T(8,128)(2,1)S(1)}, bf16[4,128,128]{2,1,0:T(8,128)(2,1)S(1)}, u32[]{:S(2)}, u32[]{:S(2)}) collective-permute-start(bf16[4,128,128]{2,1,0:T(8,128)(2,1)S(1)} %get-tuple-element.29.first), channel_id=1, source_target_pairs={{0,16},{8,24},{16,0},{24,8},{32,48},{40,56},{48,32},{56,40},{64,80... | collective-permute-start | bytes 393224 | tf_op jit(solution)/shard_map/ppermute | solution.py:300
  44.9 7.2 %collective-permute-start.6 = (bf16[4,128,128]{2,1,0:T(8,128)(2,1)S(1)}, bf16[4,128,128]{2,1,0:T(8,128)(2,1)S(1)}, u32[]{:S(2)}, u32[]{:S(2)}) collective-permute-start(bf16[4,128,128]{2,1,0:T(8,128)(2,1)S(1)} %get-tuple-element.30.second), channel_id=1, source_target_pairs={{0,496},{8,504},{16,32},{24,40},{32,16},{40,24},{48,64},{56,72},{6... | collective-permute-start | bytes 393224 | tf_op jit(solution)/shard_map/ppermute | solution.py:300
  52.1 0.0 collective-permute-done.5.from_first
  52.2 3.8 %collective-permute-done.6.from_second = bf16[4,128,128]{2,1,0:T(8,128)(2,1)S(1)} collective-permute-done((bf16[4,128,128]{2,1,0:T(8,128)(2,1)S(1)}, bf16[4,128,128]{2,1,0:T(8,128)(2,1)S(1)}, u32[]{:S(2)}, u32[]{:S(2)}) %collective-permute-start.6) | collective-permute-done | bytes 131104 | tf_op jit(solution)/shard_map/ppermute | solution.py:300
  55.9 0.0 copy-done
  55.9 3.3 %shard_map.70 = f32[8,16,2048]{2,1,0:T(8,128)} custom-call(s32[8,8]{1,0:T(8,128)S(1)} %get-tuple-element.19.pattern, bf16[8,128,128]{2,1,0:T(8,128)(2,1)S(1)} %get-tuple-element.28.smooth, bf16[4,128,128]{2,1,0:T(8,128)(2,1)S(1)} %get-tuple-element.29.first, bf16[4,128,128]{2,1,0:T(8,128)(2,1)S(1)} %get-tuple-element.30.second, ...), custom_call_target="tpu_custom_call" | custom-call | flops 16777216 | bytes 1048576 | tf_op jit(solution)/shard_map/pallas_call | solution.py:267
Async XLA Ops:
  3.5 10.7 %collective-permute-start = (bf16[8,32,128]{2,1,0:T(8,128)(2,1)S(1)}, bf16[8,32,128]{2,1,0:T(8,128)(2,1)S(1)}, u32[]{:S(2)}, u32[]{:S(2)}) collective-permute-start(bf16[8,32,128]{2,1,0:T(8,128)(2,1)S(1)} %get-tuple-element.22), channel_id=1, source_target_pairs={{0,1},{1,2},{2,3},{3,4},{4,5},{5,6},{6,7},{8,9},{9,10},{10,11},{11... | collective-permute-start | bytes 196616 | tf_op jit(solution)/shard_map/ppermute | solution.py:313
  8.2 7.4 %collective-permute-start.1 = (bf16[8,32,128]{2,1,0:T(8,128)(2,1)S(1)}, bf16[8,32,128]{2,1,0:T(8,128)(2,1)S(1)}, u32[]{:S(2)}, u32[]{:S(2)}) collective-permute-start(bf16[8,32,128]{2,1,0:T(8,128)(2,1)S(1)} %get-tuple-element.23), channel_id=1, source_target_pairs={{1,0},{2,1},{3,2},{4,3},{5,4},{6,5},{7,6},{9,8},{10,9},{11,10},{12... | collective-permute-start | bytes 196616 | tf_op jit(solution)/shard_map/ppermute | solution.py:314
  10.9 0.7 %copy-start.1 = (s32[8,8]{1,0:T(8,128)S(1)}, s32[8,8]{1,0:T(8,128)}, u32[]{:S(2)}) copy-start(s32[8,8]{1,0:T(8,128)} %pattern.1) | copy-start | bytes 772
  11.6 23.1 %copy-start.2 = (s32[1,4,2]{1,2,0:T(2,128)S(1)}, s32[1,4,2]{1,2,0:T(2,128)}, u32[]{:S(2)}) copy-start(s32[1,4,2]{1,2,0:T(2,128)} %param.10) | copy-start | bytes 100
  18.7 37.2 %copy-start = (bf16[8,128,256]{2,1,0:T(8,128)(2,1)S(1)}, bf16[8,128,256]{2,1,0:T(8,128)(2,1)}, u32[]{:S(2)}) copy-start(bf16[8,128,256]{2,1,0:T(8,128)(2,1)} %interp.3) | copy-start | bytes 1572868
  18.7 16.1 %collective-permute-start.2 = (bf16[4,128,128]{2,1,0:T(8,128)(2,1)}, bf16[4,128,128]{2,1,0:T(8,128)(2,1)S(1)}, u32[]{:S(2)}, u32[]{:S(2)}) collective-permute-start(bf16[4,128,128]{2,1,0:T(8,128)(2,1)} %get-tuple-element.26.first), channel_id=1, source_target_pairs={{0,16},{8,24},{16,0},{24,8},{32,48},{40,56},{48,32},{56,40},{64,80... | collective-permute-start | bytes 393224 | tf_op jit(solution)/shard_map/ppermute | solution.py:300
  22.2 15.4 %collective-permute-start.3 = (bf16[4,128,128]{2,1,0:T(8,128)(2,1)S(1)}, bf16[4,128,128]{2,1,0:T(8,128)(2,1)S(1)}, u32[]{:S(2)}, u32[]{:S(2)}) collective-permute-start(bf16[4,128,128]{2,1,0:T(8,128)(2,1)S(1)} %get-tuple-element.27.second), channel_id=1, source_target_pairs={{0,496},{8,504},{16,32},{24,40},{32,16},{40,24},{48,64},{56,72},{6... | collective-permute-start | bytes 393224 | tf_op jit(solution)/shard_map/ppermute | solution.py:300
  38.7 3.5 %collective-permute-start.4 = (bf16[9,128,128]{2,1,0:T(8,128)(2,1)S(1)}, bf16[9,128,128]{2,1,0:T(8,128)(2,1)S(1)}, u32[]{:S(2)}, u32[]{:S(2)}) collective-permute-start(bf16[9,128,128]{2,1,0:T(8,128)(2,1)S(1)} %shard_map.68.payload), channel_id=1, source_target_pairs={{0,8},{8,0},{16,24},{24,16},{32,40},{40,32},{48,56},{56,48},{64,72... | collective-permute-start | bytes 884744 | tf_op jit(solution)/shard_map/ppermute | solution.py:342
  43.0 9.2 %collective-permute-start.5 = (bf16[4,128,128]{2,1,0:T(8,128)(2,1)S(1)}, bf16[4,128,128]{2,1,0:T(8,128)(2,1)S(1)}, u32[]{:S(2)}, u32[]{:S(2)}) collective-permute-start(bf16[4,128,128]{2,1,0:T(8,128)(2,1)S(1)} %get-tuple-element.29.first), channel_id=1, source_target_pairs={{0,16},{8,24},{16,0},{24,8},{32,48},{40,56},{48,32},{56,40},{64,80... | collective-permute-start | bytes 393224 | tf_op jit(solution)/shard_map/ppermute | solution.py:300
  44.9 11.0 %collective-permute-start.6 = (bf16[4,128,128]{2,1,0:T(8,128)(2,1)S(1)}, bf16[4,128,128]{2,1,0:T(8,128)(2,1)S(1)}, u32[]{:S(2)}, u32[]{:S(2)}) collective-permute-start(bf16[4,128,128]{2,1,0:T(8,128)(2,1)S(1)} %get-tuple-element.30.second), channel_id=1, source_target_pairs={{0,496},{8,504},{16,32},{24,40},{32,16},{40,24},{48,64},{56,72},{6... | collective-permute-start | bytes 393224 | tf_op jit(solution)/shard_map/ppermute | solution.py:300

commit v3 on v2

--- a/solution.py
+++ b/solution.py
@@ -29,55 +29,61 @@
     return high, (a - high.astype(F32)).astype(BF16)
 
 
-def restrict_kernel(halo, fields, interp, coarse, top, bottom, blocks, bases, sems):
+def restrict_kernel(
+    halo, fields, interp, weights, pattern, coarse, top, bottom, weights_copy, pattern_copy,
+    block, bases, sems
+):
     tiles, tile_len, fine = bases.shape
-    members, level_len, _ = blocks.shape[1:]
+    members, level_len, _ = block.shape
     rows = members * level_len
-    halo_rows = members * halo
-    copies = []
-    for t in range(tiles):
-        pair = (
-            pltpu.make_async_copy(
-                fields.at[:, :, pl.ds(t * fine, fine)], blocks.at[t], sems.at[0, t]
-            ),
-            pltpu.make_async_copy(interp.at[t], bases.at[t], sems.at[1, t]),
+    pairs = ((interp, bases), (fields, block), (weights, weights_copy), (pattern, pattern_copy))
+    copies = [
+        pltpu.make_async_copy(source, target, sems.at[i])
+        for i, (source, target) in enumerate(pairs)
+    ]
+    for copy in copies:
+        copy.start()
+    first_half = iota((members // 2, 2 * halo, tile_len), 1) < halo
+    for copy in copies[:2]:
+        copy.wait()
+    for t in range(tiles):
+        span = slice(t * fine, (t + 1) * fine)
+        value = nt(block[:, :, span].reshape(rows, fine), bases[t])
+        coarse[t] = value.astype(BF16)
+        group = value.reshape(members // 2, 2, level_len, tile_len)
+        even, odd = group[:, 0, : 2 * halo], group[:, 1, : 2 * halo]
+        bottom[t] = (
+            jnp.where(first_half, even, pltpu.roll(odd, halo, 1))
+            .reshape(members * halo, tile_len)
+            .astype(BF16)
         )
-        for copy in pair:
-            copy.start()
-        copies.append(pair)
-    place = iota((2 * halo_rows, rows), 0)
-    level = jnp.where(place < halo_rows, place % halo, level_len - halo + place % halo)
-    source = (place % halo_rows) // halo * level_len + level
-    pick = (iota((2 * halo_rows, rows), 1) == source).astype(BF16)
-    for t in range(tiles):
-        for copy in copies[t]:
-            copy.wait()
-        value = nt(blocks[t].reshape(rows, fine), bases[t]).astype(BF16)
-        coarse[t] = value
-        edge = nn(pick, value).astype(BF16)
-        bottom[t] = edge[:halo_rows]
-        top[t] = edge[halo_rows:]
+        even, odd = group[:, 0, level_len - 2 * halo :], group[:, 1, level_len - 2 * halo :]
+        top[t] = (
+            jnp.where(first_half, pltpu.roll(even, halo, 1), odd)
+            .reshape(members * halo, tile_len)
+            .astype(BF16)
+        )
+    for copy in copies[2:]:
+        copy.wait()
 
 
 def vertical_kernel(
-    level_len, halo, coarse, weights, pattern, conv, partial, halo_matrix, pattern_copy,
-    conv_copy, sem
+    level_len, halo, coarse, weights, conv, partial, halo_matrix, conv_copy, sem
 ):
     fetch = pltpu.make_async_copy(conv, conv_copy, sem)
     fetch.start()
     tiles, rows, tile_len = coarse.shape
     halo_rows = rows // level_len * halo
-    levels, taps = weights.shape
+    taps, levels = weights.shape
     half = taps // 2
-    pattern_copy[...] = pattern[...]
     start = lax.axis_index("lev") * level_len
-    distance = iota((levels, levels), 1) - iota((levels, levels), 0)
+    distance = iota((levels, levels), 0) - iota((levels, levels), 1)
     table = weights[...]
     band = jnp.zeros((levels, levels), F32)
     for j in range(taps):
-        band = band + jnp.where(distance == j - half, table[:, j : j + 1], 0.0)
+        band = band + jnp.where(distance == j - half, table[j : j + 1, :], 0.0)
     both = lax.dot_general(
-        band, band, (((1,), (1,)), ((), ())), precision=HIGHEST, preferred_element_type=F32
+        band, band, (((0,), (0,)), ((), ())), precision=HIGHEST, preferred_element_type=F32
     )
     pick = (
         iota((rows, levels), 1) == start + iota((rows, levels), 0) % level_len
@@ -116,20 +122,28 @@
         body(first, second)
 
 
-def adjoint_kernel(pattern, partial, halo_matrix, low, high, conv, own, second, first, entries):
+def adjoint_kernel(
+    pattern, partial, halo_matrix, low, high, conv, own, second, first,
+    smooth, products, entries, table, sem
+):
     tiles, rows, tile_len = partial.shape
     count = conv.shape[1]
+    fetch = pltpu.make_async_copy(pattern, table, sem)
+    fetch.start()
+    matrix = halo_matrix[...]
+    for t in range(tiles):
+        edge = jnp.concatenate([low[t], high[t]], axis=0)
+        smooth[t] = (
+            partial[t] + nn(matrix, jnp.concatenate([edge, edge], axis=0))
+        ).astype(BF16)
+    for t in range(tiles):
+        products[t] = nt(smooth[t], conv[t].reshape(count * tile_len, tile_len))
     entries[...] = jnp.zeros_like(entries)
-    matrix = halo_matrix[...]
-    for t in range(tiles):
-        edge = jnp.concatenate([low[t], high[t]], axis=0)
-        smooth = partial[t] + nn(matrix, jnp.concatenate([edge, edge], axis=0))
-        products = nt(
-            smooth.astype(BF16), conv[t].reshape(count * tile_len, tile_len)
-        )
+    fetch.wait()
+    for t in range(tiles):
         for k in range(count):
-            entry = pattern[t, k]
-            entries[entry] += products[:, k * tile_len : (k + 1) * tile_len]
+            entry = table[t, k]
+            entries[entry] += products[t, :, k * tile_len : (k + 1) * tile_len]
     own[...] = entries[:tiles]
 
     def sides(down, up):
@@ -146,7 +160,7 @@
         total[tile] += piece.astype(F32)
 
 
-def partner_kernel(send, own, first, second, from_first, from_second, payload):
+def partner_kernel(send, own, second, first, from_second, from_first, payload):
     tiles = own.shape[0]
     core = lax.axis_index("patch") % 2
 
@@ -182,7 +196,7 @@
     by_chip(sides, (first, from_first), (second, from_second))
 
 
-def gather_kernel(send, own, from_first, from_second, total):
+def gather_kernel(send, own, from_second, from_first, total):
     total[...] = own[...]
 
     def sides(from_low, from_high):
@@ -222,12 +236,15 @@
 
 
 def forward_kernel(
-    pattern, smooth, first, second, from_first, from_second, interp, conv, out, entries
+    pattern, smooth, second, first, from_second, from_first, interp, conv, out,
+    entries, mixed, table, sem
 ):
     tiles, tile_len, fine = interp.shape
     count = conv.shape[1]
     members, level_len, _ = out.shape
     core = lax.axis_index("patch") % 2
+    fetch = pltpu.make_async_copy(pattern, table, sem)
+    fetch.start()
     entries[0:tiles] = smooth[...]
 
     def sides(low, high):
@@ -246,10 +263,12 @@
             entries[tiles + 4 : tiles + 6] = up[2:4]
 
     by_chip(sides, (first, from_first), (second, from_second))
-    for t in range(tiles):
-        picked = jnp.concatenate([entries[pattern[t, k]] for k in range(count)], axis=1)
-        mixed = nn(picked, conv[t].reshape(count * tile_len, tile_len)).astype(BF16)
-        out[:, :, t * fine : (t + 1) * fine] = nn(mixed, interp[t]).reshape(
+    fetch.wait()
+    for t in range(tiles):
+        picked = jnp.concatenate([entries[table[t, k]] for k in range(count)], axis=1)
+        mixed[t] = nn(picked, conv[t].reshape(count * tile_len, tile_len)).astype(BF16)
+    for t in range(tiles):
+        out[:, :, t * fine : (t + 1) * fine] = nn(mixed[t], interp[t]).reshape(
             members, level_len, fine
         )
 
@@ -299,37 +318,49 @@
         ]
         return lax.ppermute(block, "patch", partner)
 
-    coarse, top, bottom = call(
+    table = pltpu.SMEM(tile_pattern.shape, jnp.int32)
+    coarse, top, bottom, weights, pattern = call(
         functools.partial(restrict_kernel, halo),
-        (narrow_list, edge_list, edge_list),
-        [HBM, HBM],
-        (in_hbm(fields), in_hbm(interp)),
+        (
+            narrow_list,
+            edge_list,
+            edge_list,
+            shape(vert_weight.shape[::-1], F32),
+            shape(tile_pattern.shape, jnp.int32),
+        ),
+        [HBM] * 4,
+        [in_hbm(array) for array in (fields, interp, vert_weight.T, tile_pattern)],
         [
-            pltpu.VMEM((tiles, members, level_len, fine), BF16),
+            pltpu.VMEM(fields.shape, BF16),
             pltpu.VMEM((tiles, tile_len, fine), BF16),
-            pltpu.SemaphoreType.DMA((2, tiles)),
+            pltpu.SemaphoreType.DMA((4,)),
         ],
     )
     low = lax.ppermute(top, "lev", [(i, i + 1) for i in range(levs - 1)])
     high = lax.ppermute(bottom, "lev", [(i + 1, i) for i in range(levs - 1)])
-    partial, halo_matrix, pattern, conv = call(
+    partial, halo_matrix, conv = call(
         functools.partial(vertical_kernel, level_len, halo),
         (
             tile_list,
             shape((rows, 4 * members * halo), BF16),
-            shape(tile_pattern.shape, jnp.int32),
             shape(conv_weight.shape, BF16),
         ),
-        [VMEM] * 3 + [HBM],
-        (coarse, vert_weight, tile_pattern, in_hbm(conv_weight)),
+        [VMEM] * 2 + [HBM],
+        (coarse, weights, in_hbm(conv_weight)),
         [pltpu.SemaphoreType.DMA],
     )
     own, second, first = call(
         adjoint_kernel,
         (tile_list, four, four),
-        [SMEM] + [VMEM] * 5,
+        [VMEM] * 6,
         (pattern, partial, halo_matrix, low, high, conv),
-        [pltpu.VMEM((tiles + 8,) + tile_shape, F32)],
+        [
+            pltpu.VMEM((tiles,) + tile_shape, BF16),
+            pltpu.VMEM((tiles, rows, conv_weight.shape[1] * tile_len), F32),
+            pltpu.VMEM((tiles + 8,) + tile_shape, F32),
+            table,
+            pltpu.SemaphoreType.DMA,
+        ],
     )
     from_second = swap(second, 2)
     from_first = swap(first, 0)
@@ -337,14 +368,14 @@
         partner_kernel,
         shape((9,) + tile_shape, BF16),
         [SMEM] + [VMEM] * 5,
-        (send_tiles, own, first, second, from_first, from_second),
+        (send_tiles, own, second, first, from_second, from_first),
     )
     arrived = lax.ppermute(payload, "patch", [(i, i ^ 1) for i in range(patches)])
     total = call(
         gather_kernel,
         tile_list,
         [SMEM] + [VMEM] * 3,
-        (send_tiles, own, from_first, from_second),
+        (send_tiles, own, from_second, from_first),
     )
     smooth, second, first = call(
         complete_kernel,
@@ -358,9 +389,14 @@
     return call(
         forward_kernel,
         shape(fields.shape, F32),
-        [SMEM] + [VMEM] * 7,
-        (pattern, smooth, first, second, from_first, from_second, interp, conv),
-        [pltpu.VMEM((tiles + 8,) + tile_shape, BF16)],
+        [VMEM] * 8,
+        (pattern, smooth, second, first, from_second, from_first, interp, conv),
+        [
+            pltpu.VMEM((tiles + 8,) + tile_shape, BF16),
+            pltpu.VMEM((tiles,) + tile_shape, BF16),
+            table,
+            pltpu.SemaphoreType.DMA,
+        ],
     )
 
 

time: 59.6 us -> 55.1 us (0.924)
  waiting for transfers between devices: 8.84 us -> 15.5 us
  starting transfers between devices: 33.7 us -> 28.8 us
  Pallas kernels: 14.9 us -> 10.3 us
  local copies, waits for them, and re-layouts: 1.58 us -> 0.11 us
    ppermute x4, starting transfers between devices: 25.2 us -> 20.2 us  [swap(): return lax.ppermute(block, 'patch', partner)]
    pallas_call x7, Pallas kernels: 14.9 us -> 10.3 us  [call(): pl.pallas_call(kernel, out_shape=outs, in_specs=specs, out_specs=jax.tree...]
    ppermute x4, waiting for transfers between devices: 6.6 us -> 10.8 us  [swap(): return lax.ppermute(block, 'patch', partner)]
    ppermute x1, waiting for transfers between devices: 1.35 us -> 3.81 us  [shards(): high = lax.ppermute(bottom, 'lev', [(i + 1, i) for i in range(levs - 1)])]
    unnamed x8 -> x5, local copies, waits for them, and re-layouts: 1.58 us -> 0.11 us
  transfers between devices with their start and end apart: 7 -> 7, of which waited for: 4 -> 5; matrix products, arithmetic and copies ran while one was open for 2% -> 0% of each run, Pallas kernels for 5% -> 4%
where the time goes in v3:
time: 55.1 us; the launch traced here: 54.8 us
  starting transfers between devices  28.8 us (52%)
  waiting for transfers between devices  15.5 us (28%)
  Pallas kernels  10.3 us (19%)
    ppermute x4, starting transfers between devices, swap(): return lax.ppermute(block, 'patch', partner)  20.2 us
    ppermute x4, waiting for transfers between devices, swap(): return lax.ppermute(block, 'patch', partner)  10.8 us
    pallas_call x7, Pallas kernels, call(): pl.pallas_call(kernel, out_shape=outs, in_specs=specs, out_specs=jax.tree...  10.3 us
    ppermute x1, starting transfers between devices, shards(): low = lax.ppermute(top, 'lev', [(i, i + 1) for i in range(levs - 1)])  4.7 us
    ppermute x1, waiting for transfers between devices, shards(): high = lax.ppermute(bottom, 'lev', [(i + 1, i) for i in range(levs - 1)])  3.81 us
    ppermute x1, starting transfers between devices, shards(): lax.ppermute(payload, 'patch', [(i, i ^ 1) for i in range(patches)])  1.92 us
    ppermute x1, starting transfers between devices, shards(): high = lax.ppermute(bottom, 'lev', [(i + 1, i) for i in range(levs - 1)])  1.92 us
  transfers between devices with their start and end apart: 7, of which 5 were waited for; matrix products, arithmetic and copies ran while one was open for 0% of the time, Pallas kernels for 4%

profile of v3, /device:TPU:24, one launch (start us, length us, event | category | flops | bytes accessed | tf_op | source)
XLA Modules:
  0.0 54.8 jit_solution(10546641161693260610)
XLA Ops:
  0.0 1.5 %shard_map.64 = (bf16[8,128,128]{2,1,0:T(8,128)(2,1)S(1)}, bf16[8,32,128]{2,1,0:T(8,128)(2,1)S(1)}, bf16[8,32,128]{2,1,0:T(8,128)(2,1)S(1)}, f32[5,128]{1,0:T(8,128)S(1)}, s32[8,8]{1,0:T(8,128)S(1)}) custom-call(bf16[8,16,2048]{2,1,0:T(8,128)(2,1)} %fields.1, bf16[8,128,256]{2,1,0:T(8,128)(2,1)} %interp.3, f32[5,128]{1,0:T(8,128)} %bitcast.1, s32[8,8]{1,0:T(8,128)} %pattern.1), custom_call_target="tpu_custom_call" | custom-call | flops 16777216 | bytes 1048576 | tf_op jit(solution)/shard_map/pallas_call | solution.py:286
  1.5 4.7 %collective-permute-start = (bf16[8,32,128]{2,1,0:T(8,128)(2,1)S(1)}, bf16[8,32,128]{2,1,0:T(8,128)(2,1)S(1)}, u32[]{:S(2)}, u32[]{:S(2)}) collective-permute-start(bf16[8,32,128]{2,1,0:T(8,128)(2,1)S(1)} %get-tuple-element.24), channel_id=1, source_target_pairs={{0,1},{1,2},{2,3},{3,4},{4,5},{5,6},{6,7},{8,9},{9,10},{10,11},{11... | collective-permute-start | bytes 196616 | tf_op jit(solution)/shard_map/ppermute | solution.py:339
  6.2 1.9 %collective-permute-start.1 = (bf16[8,32,128]{2,1,0:T(8,128)(2,1)S(1)}, bf16[8,32,128]{2,1,0:T(8,128)(2,1)S(1)}, u32[]{:S(2)}, u32[]{:S(2)}) collective-permute-start(bf16[8,32,128]{2,1,0:T(8,128)(2,1)S(1)} %get-tuple-element.25), channel_id=1, source_target_pairs={{1,0},{2,1},{3,2},{4,3},{5,4},{6,5},{7,6},{9,8},{10,9},{11,10},{12... | collective-permute-start | bytes 196616 | tf_op jit(solution)/shard_map/ppermute | solution.py:340
  8.2 0.0 copy-start.1
  8.2 1.6 %shard_map.65 = (f32[8,128,128]{2,1,0:T(8,128)S(1)}, bf16[128,128]{1,0:T(8,128)(2,1)S(1)}, bf16[8,8,128,128]{3,2,1,0:T(8,128)(2,1)S(1)}) custom-call(bf16[8,128,128]{2,1,0:T(8,128)(2,1)S(1)} %get-tuple-element.20.coarse, f32[5,128]{1,0:T(8,128)S(1)} %get-tuple-element.21.weights, bf16[8,8,128,128]{3,2,1,0:T(8,128)(2,1)} %conv.1), custom_call_target="tpu_custom_call" | custom-call | flops 16777216 | bytes 1048576 | tf_op jit(solution)/shard_map/pallas_call | solution.py:286
  9.8 0.0 collective-permute-done.low
  9.8 3.8 %collective-permute-done.1.high = bf16[8,32,128]{2,1,0:T(8,128)(2,1)S(1)} collective-permute-done((bf16[8,32,128]{2,1,0:T(8,128)(2,1)S(1)}, bf16[8,32,128]{2,1,0:T(8,128)(2,1)S(1)}, u32[]{:S(2)}, u32[]{:S(2)}) %collective-permute-start.1) | collective-permute-done | bytes 65568 | tf_op jit(solution)/shard_map/ppermute | solution.py:340
  13.6 2.3 %shard_map.66 = (f32[8,128,128]{2,1,0:T(8,128)S(1)}, bf16[4,128,128]{2,1,0:T(8,128)(2,1)S(1)}, bf16[4,128,128]{2,1,0:T(8,128)(2,1)}) custom-call(s32[8,8]{1,0:T(8,128)S(1)} %get-tuple-element.19.pattern, f32[8,128,128]{2,1,0:T(8,128)S(1)} %get-tuple-element.22.partial, bf16[128,128]{1,0:T(8,128)(2,1)S(1)} %get-tuple-element.23.halo_matrix, ...), custom_call_target="tpu_custom_call" | custom-call | flops 16777216 | bytes 1048576 | tf_op jit(solution)/shard_map/pallas_call | solution.py:286
  15.9 0.0 copy-start
  15.9 13.3 %collective-permute-start.2 = (bf16[4,128,128]{2,1,0:T(8,128)(2,1)S(1)}, bf16[4,128,128]{2,1,0:T(8,128)(2,1)S(1)}, u32[]{:S(2)}, u32[]{:S(2)}) collective-permute-start(bf16[4,128,128]{2,1,0:T(8,128)(2,1)S(1)} %get-tuple-element.28.second), channel_id=1, source_target_pairs={{0,496},{8,504},{16,32},{24,40},{32,16},{40,24},{48,64},{56,72},{6... | collective-permute-start | bytes 393224 | tf_op jit(solution)/shard_map/ppermute | solution.py:319
  29.2 1.9 %collective-permute-start.3 = (bf16[4,128,128]{2,1,0:T(8,128)(2,1)}, bf16[4,128,128]{2,1,0:T(8,128)(2,1)S(1)}, u32[]{:S(2)}, u32[]{:S(2)}) collective-permute-start(bf16[4,128,128]{2,1,0:T(8,128)(2,1)} %get-tuple-element.29.first), channel_id=1, source_target_pairs={{0,16},{8,24},{16,0},{24,8},{32,48},{40,56},{48,32},{56,40},{64,80... | collective-permute-start | bytes 393224 | tf_op jit(solution)/shard_map/ppermute | solution.py:319
  31.1 0.0 copy-done.1
  31.1 0.1 copy.9.send
  31.2 0.9 %collective-permute-done.2.from_second = bf16[4,128,128]{2,1,0:T(8,128)(2,1)S(1)} collective-permute-done((bf16[4,128,128]{2,1,0:T(8,128)(2,1)S(1)}, bf16[4,128,128]{2,1,0:T(8,128)(2,1)S(1)}, u32[]{:S(2)}, u32[]{:S(2)}) %collective-permute-start.2) | collective-permute-done | bytes 131104 | tf_op jit(solution)/shard_map/ppermute | solution.py:319
  32.1 4.1 %collective-permute-done.3.from_first = bf16[4,128,128]{2,1,0:T(8,128)(2,1)S(1)} collective-permute-done((bf16[4,128,128]{2,1,0:T(8,128)(2,1)}, bf16[4,128,128]{2,1,0:T(8,128)(2,1)S(1)}, u32[]{:S(2)}, u32[]{:S(2)}) %collective-permute-start.3) | collective-permute-done | bytes 131104 | tf_op jit(solution)/shard_map/ppermute | solution.py:319
  36.3 1.1 %shard_map.68.payload = bf16[9,128,128]{2,1,0:T(8,128)(2,1)S(1)} custom-call(s32[1,4,2]{2,1,0:T(4,128)S(1)} %copy.9.send, f32[8,128,128]{2,1,0:T(8,128)S(1)} %get-tuple-element.27.own, bf16[4,128,128]{2,1,0:T(8,128)(2,1)S(1)} %get-tuple-element.28.second, bf16[4,128,128]{2,1,0:T(8,128)(2,1)} %get-tuple-element.29.first, ...), custom_call_target="tpu_custom_call" | custom-call | flops 16777216 | bytes 1048576 | tf_op jit(solution)/shard_map/pallas_call | solution.py:286
  37.3 1.9 %collective-permute-start.4 = (bf16[9,128,128]{2,1,0:T(8,128)(2,1)S(1)}, bf16[9,128,128]{2,1,0:T(8,128)(2,1)S(1)}, u32[]{:S(2)}, u32[]{:S(2)}) collective-permute-start(bf16[9,128,128]{2,1,0:T(8,128)(2,1)S(1)} %shard_map.68.payload), channel_id=1, source_target_pairs={{0,8},{8,0},{16,24},{24,16},{32,40},{40,32},{48,56},{56,48},{64,72... | collective-permute-start | bytes 884744 | tf_op jit(solution)/shard_map/ppermute | solution.py:373
  39.3 0.6 %shard_map.67.partial = f32[8,128,128]{2,1,0:T(8,128)S(1)} custom-call(s32[1,4,2]{2,1,0:T(4,128)S(1)} %copy.9.send, f32[8,128,128]{2,1,0:T(8,128)S(1)} %get-tuple-element.27.own, bf16[4,128,128]{2,1,0:T(8,128)(2,1)S(1)} %collective-permute-done.2.from_second, bf16[4,128,128]{2,1,0:T(8,128)(2,1)S(1)} %collective-permute-done.3.from_first), custom_call_target="tpu_custom_call" | custom-call | flops 16777216 | bytes 1048576 | tf_op jit(solution)/shard_map/pallas_call | solution.py:286
  39.9 0.9 %collective-permute-done.4.arrived = bf16[9,128,128]{2,1,0:T(8,128)(2,1)S(1)} collective-permute-done((bf16[9,128,128]{2,1,0:T(8,128)(2,1)S(1)}, bf16[9,128,128]{2,1,0:T(8,128)(2,1)S(1)}, u32[]{:S(2)}, u32[]{:S(2)}) %collective-permute-start.4) | collective-permute-done | bytes 294944 | tf_op jit(solution)/shard_map/ppermute | solution.py:373
  40.8 0.8 %shard_map.69 = (bf16[8,128,128]{2,1,0:T(8,128)(2,1)S(1)}, bf16[4,128,128]{2,1,0:T(8,128)(2,1)S(1)}, bf16[4,128,128]{2,1,0:T(8,128)(2,1)S(1)}) custom-call(s32[1,4,2]{2,1,0:T(4,128)S(1)} %copy.9.send, f32[8,128,128]{2,1,0:T(8,128)S(1)} %shard_map.67.partial, bf16[9,128,128]{2,1,0:T(8,128)(2,1)S(1)} %shard_map.68.payload, ...), custom_call_target="tpu_custom_call" | custom-call | flops 16777216 | bytes 1048576 | tf_op jit(solution)/shard_map/pallas_call | solution.py:286
  41.6 3.1 %collective-permute-start.5 = (bf16[4,128,128]{2,1,0:T(8,128)(2,1)S(1)}, bf16[4,128,128]{2,1,0:T(8,128)(2,1)S(1)}, u32[]{:S(2)}, u32[]{:S(2)}) collective-permute-start(bf16[4,128,128]{2,1,0:T(8,128)(2,1)S(1)} %get-tuple-element.31.second), channel_id=1, source_target_pairs={{0,496},{8,504},{16,32},{24,40},{32,16},{40,24},{48,64},{56,72},{6... | collective-permute-start | bytes 393224 | tf_op jit(solution)/shard_map/ppermute | solution.py:319
  44.7 1.9 %collective-permute-start.6 = (bf16[4,128,128]{2,1,0:T(8,128)(2,1)S(1)}, bf16[4,128,128]{2,1,0:T(8,128)(2,1)S(1)}, u32[]{:S(2)}, u32[]{:S(2)}) collective-permute-start(bf16[4,128,128]{2,1,0:T(8,128)(2,1)S(1)} %get-tuple-element.32.first), channel_id=1, source_target_pairs={{0,16},{8,24},{16,0},{24,8},{32,48},{40,56},{48,32},{56,40},{64,80... | collective-permute-start | bytes 393224 | tf_op jit(solution)/shard_map/ppermute | solution.py:319
  46.6 5.7 %collective-permute-done.5.from_second = bf16[4,128,128]{2,1,0:T(8,128)(2,1)S(1)} collective-permute-done((bf16[4,128,128]{2,1,0:T(8,128)(2,1)S(1)}, bf16[4,128,128]{2,1,0:T(8,128)(2,1)S(1)}, u32[]{:S(2)}, u32[]{:S(2)}) %collective-permute-start.5) | collective-permute-done | bytes 131104 | tf_op jit(solution)/shard_map/ppermute | solution.py:319
  52.3 0.0 collective-permute-done.6.from_first
  52.3 0.0 copy-done
  52.3 2.4 %shard_map.70 = f32[8,16,2048]{2,1,0:T(8,128)} custom-call(s32[8,8]{1,0:T(8,128)S(1)} %get-tuple-element.19.pattern, bf16[8,128,128]{2,1,0:T(8,128)(2,1)S(1)} %get-tuple-element.30.smooth, bf16[4,128,128]{2,1,0:T(8,128)(2,1)S(1)} %get-tuple-element.31.second, bf16[4,128,128]{2,1,0:T(8,128)(2,1)S(1)} %get-tuple-element.32.first, ...), custom_call_target="tpu_custom_call" | custom-call | flops 16777216 | bytes 1048576 | tf_op jit(solution)/shard_map/pallas_call | solution.py:286
Async XLA Ops:
  1.5 8.3 %collective-permute-start = (bf16[8,32,128]{2,1,0:T(8,128)(2,1)S(1)}, bf16[8,32,128]{2,1,0:T(8,128)(2,1)S(1)}, u32[]{:S(2)}, u32[]{:S(2)}) collective-permute-start(bf16[8,32,128]{2,1,0:T(8,128)(2,1)S(1)} %get-tuple-element.24), channel_id=1, source_target_pairs={{0,1},{1,2},{2,3},{3,4},{4,5},{5,6},{6,7},{8,9},{9,10},{10,11},{11... | collective-permute-start | bytes 196616 | tf_op jit(solution)/shard_map/ppermute | solution.py:339
  6.2 7.4 %collective-permute-start.1 = (bf16[8,32,128]{2,1,0:T(8,128)(2,1)S(1)}, bf16[8,32,128]{2,1,0:T(8,128)(2,1)S(1)}, u32[]{:S(2)}, u32[]{:S(2)}) collective-permute-start(bf16[8,32,128]{2,1,0:T(8,128)(2,1)S(1)} %get-tuple-element.25), channel_id=1, source_target_pairs={{1,0},{2,1},{3,2},{4,3},{5,4},{6,5},{7,6},{9,8},{10,9},{11,10},{12... | collective-permute-start | bytes 196616 | tf_op jit(solution)/shard_map/ppermute | solution.py:340
  8.2 22.9 %copy-start.1 = (s32[1,4,2]{1,2,0:T(2,128)S(1)}, s32[1,4,2]{1,2,0:T(2,128)}, u32[]{:S(2)}) copy-start(s32[1,4,2]{1,2,0:T(2,128)} %param.10) | copy-start | bytes 100
  15.9 36.4 %copy-start = (bf16[8,128,256]{2,1,0:T(8,128)(2,1)S(1)}, bf16[8,128,256]{2,1,0:T(8,128)(2,1)}, u32[]{:S(2)}) copy-start(bf16[8,128,256]{2,1,0:T(8,128)(2,1)} %interp.3) | copy-start | bytes 1572868
  15.9 16.2 %collective-permute-start.2 = (bf16[4,128,128]{2,1,0:T(8,128)(2,1)S(1)}, bf16[4,128,128]{2,1,0:T(8,128)(2,1)S(1)}, u32[]{:S(2)}, u32[]{:S(2)}) collective-permute-start(bf16[4,128,128]{2,1,0:T(8,128)(2,1)S(1)} %get-tuple-element.28.second), channel_id=1, source_target_pairs={{0,496},{8,504},{16,32},{24,40},{32,16},{40,24},{48,64},{56,72},{6... | collective-permute-start | bytes 393224 | tf_op jit(solution)/shard_map/ppermute | solution.py:319
  29.2 7.1 %collective-permute-start.3 = (bf16[4,128,128]{2,1,0:T(8,128)(2,1)}, bf16[4,128,128]{2,1,0:T(8,128)(2,1)S(1)}, u32[]{:S(2)}, u32[]{:S(2)}) collective-permute-start(bf16[4,128,128]{2,1,0:T(8,128)(2,1)} %get-tuple-element.29.first), channel_id=1, source_target_pairs={{0,16},{8,24},{16,0},{24,8},{32,48},{40,56},{48,32},{56,40},{64,80... | collective-permute-start | bytes 393224 | tf_op jit(solution)/shard_map/ppermute | solution.py:319
  37.3 3.5 %collective-permute-start.4 = (bf16[9,128,128]{2,1,0:T(8,128)(2,1)S(1)}, bf16[9,128,128]{2,1,0:T(8,128)(2,1)S(1)}, u32[]{:S(2)}, u32[]{:S(2)}) collective-permute-start(bf16[9,128,128]{2,1,0:T(8,128)(2,1)S(1)} %shard_map.68.payload), channel_id=1, source_target_pairs={{0,8},{8,0},{16,24},{24,16},{32,40},{40,32},{48,56},{56,48},{64,72... | collective-permute-start | bytes 884744 | tf_op jit(solution)/shard_map/ppermute | solution.py:373
  41.6 10.8 %collective-permute-start.5 = (bf16[4,128,128]{2,1,0:T(8,128)(2,1)S(1)}, bf16[4,128,128]{2,1,0:T(8,128)(2,1)S(1)}, u32[]{:S(2)}, u32[]{:S(2)}) collective-permute-start(bf16[4,128,128]{2,1,0:T(8,128)(2,1)S(1)} %get-tuple-element.31.second), channel_id=1, source_target_pairs={{0,496},{8,504},{16,32},{24,40},{32,16},{40,24},{48,64},{56,72},{6... | collective-permute-start | bytes 393224 | tf_op jit(solution)/shard_map/ppermute | solution.py:319
  44.7 7.6 %collective-permute-start.6 = (bf16[4,128,128]{2,1,0:T(8,128)(2,1)S(1)}, bf16[4,128,128]{2,1,0:T(8,128)(2,1)S(1)}, u32[]{:S(2)}, u32[]{:S(2)}) collective-permute-start(bf16[4,128,128]{2,1,0:T(8,128)(2,1)S(1)} %get-tuple-element.32.first), channel_id=1, source_target_pairs={{0,16},{8,24},{16,0},{24,8},{32,48},{40,56},{48,32},{56,40},{64,80... | collective-permute-start | bytes 393224 | tf_op jit(solution)/shard_map/ppermute | solution.py:319

commit v4 on v3

--- a/solution.py
+++ b/solution.py
@@ -122,12 +122,36 @@
         body(first, second)
 
 
+def find_terms(table, place, tiles):
+    _, count = table.shape
+    for i in range(place.shape[0]):
+        place[i] = tiles * count
+    for t in range(tiles):
+        for k in range(count):
+            place[table[t, k] * tiles + t] = t * count + k
+
+
+def form_products(smooth, conv, products):
+    tiles, count, tile_len, _ = conv.shape
+    products[tiles * count] = jnp.zeros(products.shape[1:], F32)
+    for t in range(tiles):
+        value = nt(smooth[t], conv[t].reshape(count * tile_len, tile_len))
+        for k in range(count):
+            products[t * count + k] = value[:, k * tile_len : (k + 1) * tile_len]
+
+
+def entry_sum(products, place, entry, tiles):
+    terms = [products[place[entry * tiles + t]] for t in range(tiles)]
+    while len(terms) > 1:
+        terms = [terms[i] + terms[i + 1] for i in range(0, len(terms), 2)]
+    return terms[0]
+
+
 def adjoint_kernel(
-    pattern, partial, halo_matrix, low, high, conv, own, second, first,
-    smooth, products, entries, table, sem
+    pattern, partial, halo_matrix, low, high, conv, smooth, second, first,
+    products, table, place, sem
 ):
-    tiles, rows, tile_len = partial.shape
-    count = conv.shape[1]
+    tiles = partial.shape[0]
     fetch = pltpu.make_async_copy(pattern, table, sem)
     fetch.start()
     matrix = halo_matrix[...]
@@ -136,35 +160,41 @@
         smooth[t] = (
             partial[t] + nn(matrix, jnp.concatenate([edge, edge], axis=0))
         ).astype(BF16)
-    for t in range(tiles):
-        products[t] = nt(smooth[t], conv[t].reshape(count * tile_len, tile_len))
-    entries[...] = jnp.zeros_like(entries)
-    fetch.wait()
-    for t in range(tiles):
-        for k in range(count):
-            entry = table[t, k]
-            entries[entry] += products[t, :, k * tile_len : (k + 1) * tile_len]
-    own[...] = entries[:tiles]
+    form_products(smooth, conv, products)
+    fetch.wait()
+    find_terms(table, place, tiles)
 
     def sides(down, up):
-        up[...] = entries[tiles : tiles + 4].astype(BF16)
-        down[0:2] = entries[tiles + 6 : tiles + 8].astype(BF16)
-        down[2:4] = entries[tiles + 4 : tiles + 6].astype(BF16)
+        for i in range(4):
+            up[i] = entry_sum(products, place, tiles + i, tiles).astype(BF16)
+            down[i] = entry_sum(products, place, tiles + 4 + (i + 2) % 4, tiles).astype(BF16)
 
     by_chip(sides, first, second)
 
 
+def own_kernel(pattern, smooth, conv, own, products, table, place, sem):
+    tiles = own.shape[0]
+    fetch = pltpu.make_async_copy(pattern, table, sem)
+    fetch.start()
+    form_products(smooth, conv, products)
+    fetch.wait()
+    find_terms(table, place, tiles)
+    for t in range(tiles):
+        own[t] = entry_sum(products, place, t, tiles)
+
+
 def add_to(total, tile, piece):
-    @pl.when(tile < total.shape[0])
-    def _():
-        total[tile] += piece.astype(F32)
-
-
-def partner_kernel(send, own, second, first, from_second, from_first, payload):
+    last = total.shape[0] - 1
+    total[jnp.minimum(tile, last)] += jnp.where(tile <= last, piece.astype(F32), 0.0)
+
+
+def partner_kernel(send, own, second, first, from_second, from_first, payload, table, sem):
     tiles = own.shape[0]
     core = lax.axis_index("patch") % 2
-
-    def sides(low, high):
+    fetch = pltpu.make_async_copy(send, table, sem)
+    fetch.start()
+
+    def copies(low, high):
         (down, from_low), (up, from_high) = low, high
 
         @pl.when(core == 0)
@@ -177,23 +207,26 @@
             payload[0:2] = from_low[2:4]
             payload[2:4] = down[2:4]
 
-        for o in range(2):
-            for s in range(2):
-                tile = send[0, 1 + o, s]
-                value = own[jnp.minimum(tile, tiles - 1)]
-                for back in range(2):
+    by_chip(copies, (first, from_first), (second, from_second))
+    fetch.wait()
+    for i in range(4):
+        tile = table[0, 1 + i // 2, i % 2]
+        payload[8, 16 * i : 16 * i + 16, :] = jnp.full(
+            (16, payload.shape[2]), tile.astype(F32)
+        ).astype(BF16)
+
+    def sums(from_low, from_high):
+        for i in range(4):
+            tile = table[0, 1 + i // 2, i % 2]
+            value = own[jnp.minimum(tile, tiles - 1)]
+            for back in range(2):
+                for link, source in ((0, from_low), (3, from_high)):
                     value = value + jnp.where(
-                        send[0, 0, back] == tile, from_low[back].astype(F32), 0.0
+                        table[0, link, back] == tile, source[back].astype(F32), 0.0
                     )
-                    value = value + jnp.where(
-                        send[0, 3, back] == tile, from_high[back].astype(F32), 0.0
-                    )
-                payload[4 + 2 * o + s] = value.astype(BF16)
-                payload[8, 16 * (2 * o + s) : 16 * (2 * o + s) + 16, :] = jnp.full(
-                    (16, payload.shape[2]), tile.astype(F32)
-                ).astype(BF16)
-
-    by_chip(sides, (first, from_first), (second, from_second))
+            payload[4 + i] = value.astype(BF16)
+
+    by_chip(sums, from_first, from_second)
 
 
 def gather_kernel(send, own, from_second, from_first, total):
@@ -207,30 +240,37 @@
     by_chip(sides, from_first, from_second)
 
 
-def complete_kernel(send, partial, payload, arrived, smooth, second, first, total):
+def complete_kernel(
+    send, partial, payload, arrived, smooth, second, first, total, table, sem
+):
     tiles = partial.shape[0]
+    fetch = pltpu.make_async_copy(send, table, sem)
+    fetch.start()
     total[...] = partial[...]
-    for o in range(2):
+    marks = [arrived[8, 16 * i : 16 * i + 1, :].astype(F32) for i in range(4)]
+    pieces = [payload[i].astype(F32) for i in range(4)]
+    theirs = []
+    for i in range(4):
+        tile = arrived[4 + i].astype(F32) + pieces[i]
+        for j in (2, 3) if i < 2 else (0, 1):
+            tile = tile + jnp.where(marks[i] == marks[j], pieces[j], 0.0)
+        theirs.append(tile.astype(BF16))
+
+    def forwarded(down, up):
         for s in range(2):
-            add_to(total, send[0, 1 + o, s], arrived[2 * o + s])
+            down[2 + s] = theirs[s]
+            up[2 + s] = theirs[2 + s]
+
+    by_chip(forwarded, first, second)
+    fetch.wait()
+    for i in range(4):
+        add_to(total, table[0, 1 + i // 2, i % 2], arrived[i])
     smooth[...] = total[...].astype(BF16)
 
     def sides(down, up):
         for s in range(2):
-            down[s] = smooth[jnp.minimum(send[0, 0, s], tiles - 1)]
-            up[s] = smooth[jnp.minimum(send[0, 3, s], tiles - 1)]
-        marks = [arrived[8, 16 * i : 16 * i + 1, :].astype(F32) for i in range(4)]
-        for o in range(2):
-            out = (down, up)[o]
-            for s in range(2):
-                mine = 2 * o + s
-                tile = arrived[4 + mine].astype(F32) + payload[mine].astype(F32)
-                for other in range(2):
-                    theirs = 2 * (1 - o) + other
-                    tile = tile + jnp.where(
-                        marks[mine] == marks[theirs], payload[theirs].astype(F32), 0.0
-                    )
-                out[2 + s] = tile.astype(BF16)
+            down[s] = smooth[jnp.minimum(table[0, 0, s], tiles - 1)]
+            up[s] = smooth[jnp.minimum(table[0, 3, s], tiles - 1)]
 
     by_chip(sides, first, second)
 
@@ -349,26 +389,33 @@
         (coarse, weights, in_hbm(conv_weight)),
         [pltpu.SemaphoreType.DMA],
     )
-    own, second, first = call(
+    place = pltpu.SMEM((2 * tiles * tiles,), jnp.int32)
+    sem = pltpu.SemaphoreType.DMA
+    count = conv_weight.shape[1]
+    products = pltpu.VMEM((tiles * count + 1,) + tile_shape, F32)
+    vertical, second, first = call(
         adjoint_kernel,
-        (tile_list, four, four),
+        (narrow_list, four, four),
         [VMEM] * 6,
         (pattern, partial, halo_matrix, low, high, conv),
-        [
-            pltpu.VMEM((tiles,) + tile_shape, BF16),
-            pltpu.VMEM((tiles, rows, conv_weight.shape[1] * tile_len), F32),
-            pltpu.VMEM((tiles + 8,) + tile_shape, F32),
-            table,
-            pltpu.SemaphoreType.DMA,
-        ],
+        [products, table, place, sem],
     )
     from_second = swap(second, 2)
     from_first = swap(first, 0)
+    own = call(
+        own_kernel,
+        tile_list,
+        [VMEM] * 3,
+        (pattern, vertical, conv),
+        [products, table, place, sem],
+    )
+    links = pltpu.SMEM(send_tiles.shape, jnp.int32)
     payload = call(
         partner_kernel,
         shape((9,) + tile_shape, BF16),
-        [SMEM] + [VMEM] * 5,
+        [VMEM] * 6,
         (send_tiles, own, second, first, from_second, from_first),
+        [links, sem],
     )
     arrived = lax.ppermute(payload, "patch", [(i, i ^ 1) for i in range(patches)])
     total = call(
@@ -380,9 +427,9 @@
     smooth, second, first = call(
         complete_kernel,
         (narrow_list, four, four),
-        [SMEM] + [VMEM] * 3,
+        [VMEM] * 4,
         (send_tiles, total, payload, arrived),
-        [pltpu.VMEM((tiles,) + tile_shape, F32)],
+        [pltpu.VMEM((tiles,) + tile_shape, F32), links, sem],
     )
     from_second = swap(second, 2)
     from_first = swap(first, 0)

time: 55.1 us -> 53.2 us (0.966)
  waiting for transfers between devices: 15.5 us -> 13.9 us
    ppermute x4, waiting for transfers between devices: 10.8 us -> 9.23 us  [swap(): return lax.ppermute(block, 'patch', partner)]
    pallas_call x7 -> x8, Pallas kernels: 10.3 us -> 9.82 us  [call(): pl.pallas_call(kernel, out_shape=outs, in_specs=specs, out_specs=jax.tree...]
  transfers between devices with their start and end apart: 7 -> 7, of which waited for: 5 -> 4; matrix products, arithmetic and copies ran while one was open for 0% -> 0% of each run, Pallas kernels for 4% -> 6%
where the time goes in v4:
time: 53.2 us; the launch traced here: 52.9 us
  starting transfers between devices  28.8 us (54%)
  waiting for transfers between devices  13.9 us (26%)
  Pallas kernels  9.82 us (18%)
    ppermute x4, starting transfers between devices, swap(): return lax.ppermute(block, 'patch', partner)  20.3 us
    pallas_call x8, Pallas kernels, call(): pl.pallas_call(kernel, out_shape=outs, in_specs=specs, out_specs=jax.tree...  9.82 us
    ppermute x4, waiting for transfers between devices, swap(): return lax.ppermute(block, 'patch', partner)  9.23 us
    ppermute x1, starting transfers between devices, shards(): low = lax.ppermute(top, 'lev', [(i, i + 1) for i in range(levs - 1)])  4.7 us
    ppermute x1, waiting for transfers between devices, shards(): high = lax.ppermute(bottom, 'lev', [(i + 1, i) for i in range(levs - 1)])  3.81 us
    ppermute x1, starting transfers between devices, shards(): lax.ppermute(payload, 'patch', [(i, i ^ 1) for i in range(patches)])  1.92 us
    ppermute x1, starting transfers between devices, shards(): high = lax.ppermute(bottom, 'lev', [(i + 1, i) for i in range(levs - 1)])  1.92 us
  transfers between devices with their start and end apart: 7, of which 4 were waited for; matrix products, arithmetic and copies ran while one was open for 0% of the time, Pallas kernels for 6%

profile of v4, /device:TPU:24, one launch (start us, length us, event | category | flops | bytes accessed | tf_op | source)
XLA Modules:
  0.0 52.9 jit_solution(7898516600316722290)
XLA Ops:
  0.0 1.5 %shard_map.64 = (bf16[8,128,128]{2,1,0:T(8,128)(2,1)S(1)}, bf16[8,32,128]{2,1,0:T(8,128)(2,1)S(1)}, bf16[8,32,128]{2,1,0:T(8,128)(2,1)S(1)}, f32[5,128]{1,0:T(8,128)S(1)}, s32[8,8]{1,0:T(8,128)S(1)}) custom-call(bf16[8,16,2048]{2,1,0:T(8,128)(2,1)} %fields.1, bf16[8,128,256]{2,1,0:T(8,128)(2,1)} %interp.3, f32[5,128]{1,0:T(8,128)} %bitcast.1, s32[8,8]{1,0:T(8,128)} %pattern.1), custom_call_target="tpu_custom_call" | custom-call | flops 16777216 | bytes 1048576 | tf_op jit(solution)/shard_map/pallas_call | solution.py:326
  1.5 4.7 %collective-permute-start = (bf16[8,32,128]{2,1,0:T(8,128)(2,1)S(1)}, bf16[8,32,128]{2,1,0:T(8,128)(2,1)S(1)}, u32[]{:S(2)}, u32[]{:S(2)}) collective-permute-start(bf16[8,32,128]{2,1,0:T(8,128)(2,1)S(1)} %get-tuple-element.24), channel_id=1, source_target_pairs={{0,1},{1,2},{2,3},{3,4},{4,5},{5,6},{6,7},{8,9},{9,10},{10,11},{11... | collective-permute-start | bytes 196616 | tf_op jit(solution)/shard_map/ppermute | solution.py:379
  6.2 1.9 %collective-permute-start.1 = (bf16[8,32,128]{2,1,0:T(8,128)(2,1)S(1)}, bf16[8,32,128]{2,1,0:T(8,128)(2,1)S(1)}, u32[]{:S(2)}, u32[]{:S(2)}) collective-permute-start(bf16[8,32,128]{2,1,0:T(8,128)(2,1)S(1)} %get-tuple-element.25), channel_id=1, source_target_pairs={{1,0},{2,1},{3,2},{4,3},{5,4},{6,5},{7,6},{9,8},{10,9},{11,10},{12... | collective-permute-start | bytes 196616 | tf_op jit(solution)/shard_map/ppermute | solution.py:380
  8.2 0.0 copy-start.1
  8.2 1.6 %shard_map.65 = (f32[8,128,128]{2,1,0:T(8,128)S(1)}, bf16[128,128]{1,0:T(8,128)(2,1)S(1)}, bf16[8,8,128,128]{3,2,1,0:T(8,128)(2,1)S(1)}) custom-call(bf16[8,128,128]{2,1,0:T(8,128)(2,1)S(1)} %get-tuple-element.20.coarse, f32[5,128]{1,0:T(8,128)S(1)} %get-tuple-element.21.weights, bf16[8,8,128,128]{3,2,1,0:T(8,128)(2,1)} %conv.1), custom_call_target="tpu_custom_call" | custom-call | flops 16777216 | bytes 1048576 | tf_op jit(solution)/shard_map/pallas_call | solution.py:326
  9.8 0.0 collective-permute-done.low
  9.8 3.8 %collective-permute-done.1.high = bf16[8,32,128]{2,1,0:T(8,128)(2,1)S(1)} collective-permute-done((bf16[8,32,128]{2,1,0:T(8,128)(2,1)S(1)}, bf16[8,32,128]{2,1,0:T(8,128)(2,1)S(1)}, u32[]{:S(2)}, u32[]{:S(2)}) %collective-permute-start.1) | collective-permute-done | bytes 65568 | tf_op jit(solution)/shard_map/ppermute | solution.py:380
  13.6 1.2 %shard_map.66 = (bf16[8,128,128]{2,1,0:T(8,128)(2,1)S(1)}, bf16[4,128,128]{2,1,0:T(8,128)(2,1)S(1)}, bf16[4,128,128]{2,1,0:T(8,128)(2,1)S(1)}) custom-call(s32[8,8]{1,0:T(8,128)S(1)} %get-tuple-element.19.pattern, f32[8,128,128]{2,1,0:T(8,128)S(1)} %get-tuple-element.22.partial, bf16[128,128]{1,0:T(8,128)(2,1)S(1)} %get-tuple-element.23.halo_matrix, ...), custom_call_target="tpu_custom_call" | custom-call | flops 16777216 | bytes 1048576 | tf_op jit(solution)/shard_map/pallas_call | solution.py:326
  14.8 13.1 %collective-permute-start.2 = (bf16[4,128,128]{2,1,0:T(8,128)(2,1)S(1)}, bf16[4,128,128]{2,1,0:T(8,128)(2,1)S(1)}, u32[]{:S(2)}, u32[]{:S(2)}) collective-permute-start(bf16[4,128,128]{2,1,0:T(8,128)(2,1)S(1)} %get-tuple-element.28.second), channel_id=1, source_target_pairs={{0,496},{8,504},{16,32},{24,40},{32,16},{40,24},{48,64},{56,72},{6... | collective-permute-start | bytes 393224 | tf_op jit(solution)/shard_map/ppermute | solution.py:359
  28.0 1.9 %collective-permute-start.3 = (bf16[4,128,128]{2,1,0:T(8,128)(2,1)S(1)}, bf16[4,128,128]{2,1,0:T(8,128)(2,1)S(1)}, u32[]{:S(2)}, u32[]{:S(2)}) collective-permute-start(bf16[4,128,128]{2,1,0:T(8,128)(2,1)S(1)} %get-tuple-element.29.first), channel_id=1, source_target_pairs={{0,16},{8,24},{16,0},{24,8},{32,48},{40,56},{48,32},{56,40},{64,80... | collective-permute-start | bytes 393224 | tf_op jit(solution)/shard_map/ppermute | solution.py:359
  29.9 0.0 copy-done.1
  29.9 0.1 copy.9.send
  30.0 1.1 %shard_map.67.own = f32[8,128,128]{2,1,0:T(8,128)S(1)} custom-call(s32[8,8]{1,0:T(8,128)S(1)} %get-tuple-element.19.pattern, bf16[8,128,128]{2,1,0:T(8,128)(2,1)S(1)} %get-tuple-element.27.smooth, bf16[8,8,128,128]{3,2,1,0:T(8,128)(2,1)S(1)} %get-tuple-element.26.conv), custom_call_target="tpu_custom_call" | custom-call | flops 16777216 | bytes 1048576 | tf_op jit(solution)/shard_map/pallas_call | solution.py:326
  31.1 0.0 copy-start
  31.1 0.0 collective-permute-done.2.from_second
  31.1 3.7 %collective-permute-done.3.from_first = bf16[4,128,128]{2,1,0:T(8,128)(2,1)S(1)} collective-permute-done((bf16[4,128,128]{2,1,0:T(8,128)(2,1)S(1)}, bf16[4,128,128]{2,1,0:T(8,128)(2,1)S(1)}, u32[]{:S(2)}, u32[]{:S(2)}) %collective-permute-start.3) | collective-permute-done | bytes 131104 | tf_op jit(solution)/shard_map/ppermute | solution.py:359
  34.8 0.7 %shard_map.69.payload = bf16[9,128,128]{2,1,0:T(8,128)(2,1)S(1)} custom-call(s32[1,4,2]{2,1,0:T(4,128)S(1)} %copy.9.send, f32[8,128,128]{2,1,0:T(8,128)S(1)} %shard_map.67.own, bf16[4,128,128]{2,1,0:T(8,128)(2,1)S(1)} %get-tuple-element.28.second, bf16[4,128,128]{2,1,0:T(8,128)(2,1)S(1)} %get-tuple-element.29.first, ...), custom_call_target="tpu_custom_call" | custom-call | flops 16777216 | bytes 1048576 | tf_op jit(solution)/shard_map/pallas_call | solution.py:326
  35.5 1.9 %collective-permute-start.4 = (bf16[9,128,128]{2,1,0:T(8,128)(2,1)S(1)}, bf16[9,128,128]{2,1,0:T(8,128)(2,1)S(1)}, u32[]{:S(2)}, u32[]{:S(2)}) collective-permute-start(bf16[9,128,128]{2,1,0:T(8,128)(2,1)S(1)} %shard_map.69.payload), channel_id=1, source_target_pairs={{0,8},{8,0},{16,24},{24,16},{32,40},{40,32},{48,56},{56,48},{64,72... | collective-permute-start | bytes 884744 | tf_op jit(solution)/shard_map/ppermute | solution.py:420
  37.5 0.6 %shard_map.68.partial = f32[8,128,128]{2,1,0:T(8,128)S(1)} custom-call(s32[1,4,2]{2,1,0:T(4,128)S(1)} %copy.9.send, f32[8,128,128]{2,1,0:T(8,128)S(1)} %shard_map.67.own, bf16[4,128,128]{2,1,0:T(8,128)(2,1)S(1)} %collective-permute-done.2.from_second, bf16[4,128,128]{2,1,0:T(8,128)(2,1)S(1)} %collective-permute-done.3.from_first), custom_call_target="tpu_custom_call" | custom-call | flops 16777216 | bytes 1048576 | tf_op jit(solution)/shard_map/pallas_call | solution.py:326
  38.1 0.9 %collective-permute-done.4.arrived = bf16[9,128,128]{2,1,0:T(8,128)(2,1)S(1)} collective-permute-done((bf16[9,128,128]{2,1,0:T(8,128)(2,1)S(1)}, bf16[9,128,128]{2,1,0:T(8,128)(2,1)S(1)}, u32[]{:S(2)}, u32[]{:S(2)}) %collective-permute-start.4) | collective-permute-done | bytes 294944 | tf_op jit(solution)/shard_map/ppermute | solution.py:420
  39.0 0.7 %shard_map.70 = (bf16[8,128,128]{2,1,0:T(8,128)(2,1)S(1)}, bf16[4,128,128]{2,1,0:T(8,128)(2,1)S(1)}, bf16[4,128,128]{2,1,0:T(8,128)(2,1)S(1)}) custom-call(s32[1,4,2]{2,1,0:T(4,128)S(1)} %copy.9.send, f32[8,128,128]{2,1,0:T(8,128)S(1)} %shard_map.68.partial, bf16[9,128,128]{2,1,0:T(8,128)(2,1)S(1)} %shard_map.69.payload, ...), custom_call_target="tpu_custom_call" | custom-call | flops 16777216 | bytes 1048576 | tf_op jit(solution)/shard_map/pallas_call | solution.py:326
  39.7 3.3 %collective-permute-start.5 = (bf16[4,128,128]{2,1,0:T(8,128)(2,1)S(1)}, bf16[4,128,128]{2,1,0:T(8,128)(2,1)S(1)}, u32[]{:S(2)}, u32[]{:S(2)}) collective-permute-start(bf16[4,128,128]{2,1,0:T(8,128)(2,1)S(1)} %get-tuple-element.31.second), channel_id=1, source_target_pairs={{0,496},{8,504},{16,32},{24,40},{32,16},{40,24},{48,64},{56,72},{6... | collective-permute-start | bytes 393224 | tf_op jit(solution)/shard_map/ppermute | solution.py:359
  43.0 1.9 %collective-permute-start.6 = (bf16[4,128,128]{2,1,0:T(8,128)(2,1)S(1)}, bf16[4,128,128]{2,1,0:T(8,128)(2,1)S(1)}, u32[]{:S(2)}, u32[]{:S(2)}) collective-permute-start(bf16[4,128,128]{2,1,0:T(8,128)(2,1)S(1)} %get-tuple-element.32.first), channel_id=1, source_target_pairs={{0,16},{8,24},{16,0},{24,8},{32,48},{40,56},{48,32},{56,40},{64,80... | collective-permute-start | bytes 393224 | tf_op jit(solution)/shard_map/ppermute | solution.py:359
  44.9 5.5 %collective-permute-done.5.from_second = bf16[4,128,128]{2,1,0:T(8,128)(2,1)S(1)} collective-permute-done((bf16[4,128,128]{2,1,0:T(8,128)(2,1)S(1)}, bf16[4,128,128]{2,1,0:T(8,128)(2,1)S(1)}, u32[]{:S(2)}, u32[]{:S(2)}) %collective-permute-start.5) | collective-permute-done | bytes 131104 | tf_op jit(solution)/shard_map/ppermute | solution.py:359
  50.4 0.0 collective-permute-done.6.from_first
  50.4 0.0 copy-done
  50.4 2.4 %shard_map.71 = f32[8,16,2048]{2,1,0:T(8,128)} custom-call(s32[8,8]{1,0:T(8,128)S(1)} %get-tuple-element.19.pattern, bf16[8,128,128]{2,1,0:T(8,128)(2,1)S(1)} %get-tuple-element.30.smooth, bf16[4,128,128]{2,1,0:T(8,128)(2,1)S(1)} %get-tuple-element.31.second, bf16[4,128,128]{2,1,0:T(8,128)(2,1)S(1)} %get-tuple-element.32.first, ...), custom_call_target="tpu_custom_call" | custom-call | flops 16777216 | bytes 1048576 | tf_op jit(solution)/shard_map/pallas_call | solution.py:326
Async XLA Ops:
  1.5 8.3 %collective-permute-start = (bf16[8,32,128]{2,1,0:T(8,128)(2,1)S(1)}, bf16[8,32,128]{2,1,0:T(8,128)(2,1)S(1)}, u32[]{:S(2)}, u32[]{:S(2)}) collective-permute-start(bf16[8,32,128]{2,1,0:T(8,128)(2,1)S(1)} %get-tuple-element.24), channel_id=1, source_target_pairs={{0,1},{1,2},{2,3},{3,4},{4,5},{5,6},{6,7},{8,9},{9,10},{10,11},{11... | collective-permute-start | bytes 196616 | tf_op jit(solution)/shard_map/ppermute | solution.py:379
  6.2 7.4 %collective-permute-start.1 = (bf16[8,32,128]{2,1,0:T(8,128)(2,1)S(1)}, bf16[8,32,128]{2,1,0:T(8,128)(2,1)S(1)}, u32[]{:S(2)}, u32[]{:S(2)}) collective-permute-start(bf16[8,32,128]{2,1,0:T(8,128)(2,1)S(1)} %get-tuple-element.25), channel_id=1, source_target_pairs={{1,0},{2,1},{3,2},{4,3},{5,4},{6,5},{7,6},{9,8},{10,9},{11,10},{12... | collective-permute-start | bytes 196616 | tf_op jit(solution)/shard_map/ppermute | solution.py:380
  8.2 21.7 %copy-start.1 = (s32[1,4,2]{1,2,0:T(2,128)S(1)}, s32[1,4,2]{1,2,0:T(2,128)}, u32[]{:S(2)}) copy-start(s32[1,4,2]{1,2,0:T(2,128)} %param.10) | copy-start | bytes 100
  14.8 16.3 %collective-permute-start.2 = (bf16[4,128,128]{2,1,0:T(8,128)(2,1)S(1)}, bf16[4,128,128]{2,1,0:T(8,128)(2,1)S(1)}, u32[]{:S(2)}, u32[]{:S(2)}) collective-permute-start(bf16[4,128,128]{2,1,0:T(8,128)(2,1)S(1)} %get-tuple-element.28.second), channel_id=1, source_target_pairs={{0,496},{8,504},{16,32},{24,40},{32,16},{40,24},{48,64},{56,72},{6... | collective-permute-start | bytes 393224 | tf_op jit(solution)/shard_map/ppermute | solution.py:359
  28.0 6.9 %collective-permute-start.3 = (bf16[4,128,128]{2,1,0:T(8,128)(2,1)S(1)}, bf16[4,128,128]{2,1,0:T(8,128)(2,1)S(1)}, u32[]{:S(2)}, u32[]{:S(2)}) collective-permute-start(bf16[4,128,128]{2,1,0:T(8,128)(2,1)S(1)} %get-tuple-element.29.first), channel_id=1, source_target_pairs={{0,16},{8,24},{16,0},{24,8},{32,48},{40,56},{48,32},{56,40},{64,80... | collective-permute-start | bytes 393224 | tf_op jit(solution)/shard_map/ppermute | solution.py:359
  31.1 19.4 %copy-start = (bf16[8,128,256]{2,1,0:T(8,128)(2,1)S(1)}, bf16[8,128,256]{2,1,0:T(8,128)(2,1)}, u32[]{:S(2)}) copy-start(bf16[8,128,256]{2,1,0:T(8,128)(2,1)} %interp.3) | copy-start | bytes 1572868
  35.5 3.5 %collective-permute-start.4 = (bf16[9,128,128]{2,1,0:T(8,128)(2,1)S(1)}, bf16[9,128,128]{2,1,0:T(8,128)(2,1)S(1)}, u32[]{:S(2)}, u32[]{:S(2)}) collective-permute-start(bf16[9,128,128]{2,1,0:T(8,128)(2,1)S(1)} %shard_map.69.payload), channel_id=1, source_target_pairs={{0,8},{8,0},{16,24},{24,16},{32,40},{40,32},{48,56},{56,48},{64,72... | collective-permute-start | bytes 884744 | tf_op jit(solution)/shard_map/ppermute | solution.py:420
  39.7 10.8 %collective-permute-start.5 = (bf16[4,128,128]{2,1,0:T(8,128)(2,1)S(1)}, bf16[4,128,128]{2,1,0:T(8,128)(2,1)S(1)}, u32[]{:S(2)}, u32[]{:S(2)}) collective-permute-start(bf16[4,128,128]{2,1,0:T(8,128)(2,1)S(1)} %get-tuple-element.31.second), channel_id=1, source_target_pairs={{0,496},{8,504},{16,32},{24,40},{32,16},{40,24},{48,64},{56,72},{6... | collective-permute-start | bytes 393224 | tf_op jit(solution)/shard_map/ppermute | solution.py:359
  43.0 7.4 %collective-permute-start.6 = (bf16[4,128,128]{2,1,0:T(8,128)(2,1)S(1)}, bf16[4,128,128]{2,1,0:T(8,128)(2,1)S(1)}, u32[]{:S(2)}, u32[]{:S(2)}) collective-permute-start(bf16[4,128,128]{2,1,0:T(8,128)(2,1)S(1)} %get-tuple-element.32.first), channel_id=1, source_target_pairs={{0,16},{8,24},{16,0},{24,8},{32,48},{40,56},{48,32},{56,40},{64,80... | collective-permute-start | bytes 393224 | tf_op jit(solution)/shard_map/ppermute | solution.py:359

commit v5 on v4

--- a/solution.py
+++ b/solution.py
@@ -20,6 +20,10 @@
     return lax.dot_general(a, b, (((1,), (1,)), ((), ())), preferred_element_type=F32)
 
 
+def lanes(t, width):
+    return slice(t * width, (t + 1) * width)
+
+
 def iota(shape, dim):
     return lax.broadcasted_iota(jnp.int32, shape, dim)
 
@@ -30,13 +34,13 @@
 
 
 def restrict_kernel(
-    halo, fields, interp, weights, pattern, coarse, top, bottom, weights_copy, pattern_copy,
+    halo, fields, interp, weights, coarse, top, bottom, weights_copy,
     block, bases, sems
 ):
     tiles, tile_len, fine = bases.shape
     members, level_len, _ = block.shape
     rows = members * level_len
-    pairs = ((interp, bases), (fields, block), (weights, weights_copy), (pattern, pattern_copy))
+    pairs = ((interp, bases), (fields, block), (weights, weights_copy))
     copies = [
         pltpu.make_async_copy(source, target, sems.at[i])
         for i, (source, target) in enumerate(pairs)
@@ -49,16 +53,16 @@
     for t in range(tiles):
         span = slice(t * fine, (t + 1) * fine)
         value = nt(block[:, :, span].reshape(rows, fine), bases[t])
-        coarse[t] = value.astype(BF16)
+        coarse[:, lanes(t, tile_len)] = value.astype(BF16)
         group = value.reshape(members // 2, 2, level_len, tile_len)
         even, odd = group[:, 0, : 2 * halo], group[:, 1, : 2 * halo]
-        bottom[t] = (
+        bottom[:, lanes(t, tile_len)] = (
             jnp.where(first_half, even, pltpu.roll(odd, halo, 1))
             .reshape(members * halo, tile_len)
             .astype(BF16)
         )
         even, odd = group[:, 0, level_len - 2 * halo :], group[:, 1, level_len - 2 * halo :]
-        top[t] = (
+        top[:, lanes(t, tile_len)] = (
             jnp.where(first_half, pltpu.roll(even, halo, 1), odd)
             .reshape(members * halo, tile_len)
             .astype(BF16)
@@ -68,20 +72,26 @@
 
 
 def vertical_kernel(
-    level_len, halo, coarse, weights, conv, partial, halo_matrix, conv_copy, sem
+    level_len, halo, coarse, weights, pattern, conv, partial, halo_matrix, own_blocks,
+    received_blocks, conv_copy, table, sems
 ):
-    fetch = pltpu.make_async_copy(conv, conv_copy, sem)
-    fetch.start()
-    tiles, rows, tile_len = coarse.shape
+    fetches = (
+        pltpu.make_async_copy(pattern, table, sems.at[0]),
+        pltpu.make_async_copy(conv, conv_copy, sems.at[1]),
+    )
+    for fetch in fetches:
+        fetch.start()
+    tiles, count, tile_len, _ = conv.shape
+    rows = coarse.shape[0]
     halo_rows = rows // level_len * halo
     taps, levels = weights.shape
     half = taps // 2
     start = lax.axis_index("lev") * level_len
     distance = iota((levels, levels), 0) - iota((levels, levels), 1)
-    table = weights[...]
+    taken = weights[...]
     band = jnp.zeros((levels, levels), F32)
     for j in range(taps):
-        band = band + jnp.where(distance == j - half, table[j : j + 1, :], 0.0)
+        band = band + jnp.where(distance == j - half, taken[j : j + 1, :], 0.0)
     both = lax.dot_general(
         band, band, (((0,), (0,)), ((), ())), precision=HIGHEST, preferred_element_type=F32
     )
@@ -104,10 +114,23 @@
             same_halo, nt(chosen, pick_halo), 0.0
         ).astype(BF16)
     own_matrix = jnp.concatenate(own_parts, axis=1)
+    value = coarse[...]
+    partial[...] = nn(own_matrix, jnp.concatenate([value, value], axis=0))
+    own_blocks[...] = jnp.zeros_like(own_blocks)
+    received_blocks[...] = jnp.zeros_like(received_blocks)
+    for fetch in fetches:
+        fetch.wait()
     for t in range(tiles):
-        value = coarse[t]
-        partial[t] = nn(own_matrix, jnp.concatenate([value, value], axis=0))
-    fetch.wait()
+        for k in range(count):
+            entry = table[t, k]
+
+            @pl.when(entry < tiles)
+            def _():
+                own_blocks[entry, :, lanes(t, tile_len)] = conv_copy[t, k]
+
+            @pl.when(entry >= tiles)
+            def _():
+                received_blocks[entry - tiles, :, lanes(t, tile_len)] = conv_copy[t, k]
 
 
 def by_chip(body, first, second):
@@ -122,65 +145,31 @@
         body(first, second)
 
 
-def find_terms(table, place, tiles):
-    _, count = table.shape
-    for i in range(place.shape[0]):
-        place[i] = tiles * count
-    for t in range(tiles):
-        for k in range(count):
-            place[table[t, k] * tiles + t] = t * count + k
-
-
-def form_products(smooth, conv, products):
-    tiles, count, tile_len, _ = conv.shape
-    products[tiles * count] = jnp.zeros(products.shape[1:], F32)
-    for t in range(tiles):
-        value = nt(smooth[t], conv[t].reshape(count * tile_len, tile_len))
-        for k in range(count):
-            products[t * count + k] = value[:, k * tile_len : (k + 1) * tile_len]
-
-
-def entry_sum(products, place, entry, tiles):
-    terms = [products[place[entry * tiles + t]] for t in range(tiles)]
-    while len(terms) > 1:
-        terms = [terms[i] + terms[i + 1] for i in range(0, len(terms), 2)]
-    return terms[0]
-
-
-def adjoint_kernel(
-    pattern, partial, halo_matrix, low, high, conv, smooth, second, first,
-    products, table, place, sem
-):
-    tiles = partial.shape[0]
-    fetch = pltpu.make_async_copy(pattern, table, sem)
-    fetch.start()
-    matrix = halo_matrix[...]
-    for t in range(tiles):
-        edge = jnp.concatenate([low[t], high[t]], axis=0)
-        smooth[t] = (
-            partial[t] + nn(matrix, jnp.concatenate([edge, edge], axis=0))
-        ).astype(BF16)
-    form_products(smooth, conv, products)
-    fetch.wait()
-    find_terms(table, place, tiles)
+def flat(blocks):
+    return blocks[...].reshape(-1, blocks.shape[-1])
+
+
+def adjoint_kernel(partial, halo_matrix, low, high, received_blocks, smooth, second, first):
+    tile_len = received_blocks.shape[1]
+    edge = jnp.concatenate([low[...], high[...]], axis=0)
+    value = (
+        partial[...] + nn(halo_matrix[...], jnp.concatenate([edge, edge], axis=0))
+    ).astype(BF16)
+    smooth[...] = value
+    returning = nt(value, flat(received_blocks)).astype(BF16)
 
     def sides(down, up):
         for i in range(4):
-            up[i] = entry_sum(products, place, tiles + i, tiles).astype(BF16)
-            down[i] = entry_sum(products, place, tiles + 4 + (i + 2) % 4, tiles).astype(BF16)
+            up[i] = returning[:, lanes(i, tile_len)]
+            down[i] = returning[:, lanes(4 + (i + 2) % 4, tile_len)]
 
     by_chip(sides, first, second)
 
 
-def own_kernel(pattern, smooth, conv, own, products, table, place, sem):
-    tiles = own.shape[0]
-    fetch = pltpu.make_async_copy(pattern, table, sem)
-    fetch.start()
-    form_products(smooth, conv, products)
-    fetch.wait()
-    find_terms(table, place, tiles)
-    for t in range(tiles):
-        own[t] = entry_sum(products, place, t, tiles)
+def own_kernel(smooth, own_blocks, own):
+    value = nt(smooth[...], flat(own_blocks))
+    for t in range(own.shape[0]):
+        own[t] = value[:, lanes(t, own.shape[2])]
 
 
 def add_to(total, tile, piece):
@@ -275,40 +264,42 @@
     by_chip(sides, first, second)
 
 
+def own_forward_kernel(smooth, own_blocks, partial):
+    tiles = smooth.shape[0]
+    picked = jnp.concatenate([smooth[t] for t in range(tiles)], axis=1)
+    partial[...] = nn(picked, flat(own_blocks))
+
+
 def forward_kernel(
-    pattern, smooth, second, first, from_second, from_first, interp, conv, out,
-    entries, mixed, table, sem
+    partial, second, first, from_second, from_first, received_blocks, interp, out, entries, mixed
 ):
     tiles, tile_len, fine = interp.shape
-    count = conv.shape[1]
     members, level_len, _ = out.shape
     core = lax.axis_index("patch") % 2
-    fetch = pltpu.make_async_copy(pattern, table, sem)
-    fetch.start()
-    entries[0:tiles] = smooth[...]
+
+    def put(place, source):
+        for i in range(2):
+            entries[:, lanes(place + i, tile_len)] = source[i]
 
     def sides(low, high):
         (down, from_low), (up, from_high) = low, high
-        entries[tiles : tiles + 2] = from_high[0:2]
-        entries[tiles + 6 : tiles + 8] = from_low[0:2]
+        put(0, from_high.at[0:2])
+        put(6, from_low.at[0:2])
 
         @pl.when(core == 0)
         def _():
-            entries[tiles + 2 : tiles + 4] = down[2:4]
-            entries[tiles + 4 : tiles + 6] = from_low[2:4]
+            put(2, down.at[2:4])
+            put(4, from_low.at[2:4])
 
         @pl.when(core == 1)
         def _():
-            entries[tiles + 2 : tiles + 4] = from_high[2:4]
-            entries[tiles + 4 : tiles + 6] = up[2:4]
+            put(2, from_high.at[2:4])
+            put(4, up.at[2:4])
 
     by_chip(sides, (first, from_first), (second, from_second))
-    fetch.wait()
+    mixed[...] = (partial[...] + nn(entries[...], flat(received_blocks))).astype(BF16)
     for t in range(tiles):
-        picked = jnp.concatenate([entries[table[t, k]] for k in range(count)], axis=1)
-        mixed[t] = nn(picked, conv[t].reshape(count * tile_len, tile_len)).astype(BF16)
-    for t in range(tiles):
-        out[:, :, t * fine : (t + 1) * fine] = nn(mixed[t], interp[t]).reshape(
+        out[:, :, lanes(t, fine)] = nn(mixed[:, lanes(t, tile_len)], interp[t]).reshape(
             members, level_len, fine
         )
 
@@ -346,9 +337,11 @@
     patches = lax.axis_size("patch")
     levs = lax.axis_size("lev")
     tile_shape = (rows, tile_len)
+    wide = tiles * tile_len
     tile_list = shape((tiles,) + tile_shape, F32)
     narrow_list = shape((tiles,) + tile_shape, BF16)
-    edge_list = shape((tiles, members * halo, tile_len), BF16)
+    edge_list = shape((members * halo, wide), BF16)
+    block_list = shape((tiles, tile_len, wide), BF16)
     four = shape((4,) + tile_shape, BF16)
 
     def swap(block, start):
@@ -358,57 +351,50 @@
         ]
         return lax.ppermute(block, "patch", partner)
 
-    table = pltpu.SMEM(tile_pattern.shape, jnp.int32)
-    coarse, top, bottom, weights, pattern = call(
+    coarse, top, bottom, weights = call(
         functools.partial(restrict_kernel, halo),
         (
-            narrow_list,
+            shape((rows, wide), BF16),
             edge_list,
             edge_list,
             shape(vert_weight.shape[::-1], F32),
-            shape(tile_pattern.shape, jnp.int32),
         ),
-        [HBM] * 4,
-        [in_hbm(array) for array in (fields, interp, vert_weight.T, tile_pattern)],
+        [HBM] * 3,
+        [in_hbm(array) for array in (fields, interp, vert_weight.T)],
         [
             pltpu.VMEM(fields.shape, BF16),
             pltpu.VMEM((tiles, tile_len, fine), BF16),
-            pltpu.SemaphoreType.DMA((4,)),
+            pltpu.SemaphoreType.DMA((3,)),
         ],
     )
     low = lax.ppermute(top, "lev", [(i, i + 1) for i in range(levs - 1)])
     high = lax.ppermute(bottom, "lev", [(i + 1, i) for i in range(levs - 1)])
-    partial, halo_matrix, conv = call(
+    partial, halo_matrix, own_blocks, received_blocks = call(
         functools.partial(vertical_kernel, level_len, halo),
         (
-            tile_list,
+            shape((rows, wide), F32),
             shape((rows, 4 * members * halo), BF16),
-            shape(conv_weight.shape, BF16),
+            block_list,
+            block_list,
         ),
-        [VMEM] * 2 + [HBM],
-        (coarse, weights, in_hbm(conv_weight)),
-        [pltpu.SemaphoreType.DMA],
-    )
-    place = pltpu.SMEM((2 * tiles * tiles,), jnp.int32)
+        [VMEM] * 2 + [HBM] * 2,
+        (coarse, weights, in_hbm(tile_pattern), in_hbm(conv_weight)),
+        [
+            pltpu.VMEM(conv_weight.shape, BF16),
+            pltpu.SMEM(tile_pattern.shape, jnp.int32),
+            pltpu.SemaphoreType.DMA((2,)),
+        ],
+    )
     sem = pltpu.SemaphoreType.DMA
-    count = conv_weight.shape[1]
-    products = pltpu.VMEM((tiles * count + 1,) + tile_shape, F32)
     vertical, second, first = call(
         adjoint_kernel,
-        (narrow_list, four, four),
-        [VMEM] * 6,
-        (pattern, partial, halo_matrix, low, high, conv),
-        [products, table, place, sem],
+        (shape((rows, wide), BF16), four, four),
+        [VMEM] * 5,
+        (partial, halo_matrix, low, high, received_blocks),
     )
     from_second = swap(second, 2)
     from_first = swap(first, 0)
-    own = call(
-        own_kernel,
-        tile_list,
-        [VMEM] * 3,
-        (pattern, vertical, conv),
-        [products, table, place, sem],
-    )
+    own = call(own_kernel, tile_list, [VMEM] * 2, (vertical, own_blocks))
     links = pltpu.SMEM(send_tiles.shape, jnp.int32)
     payload = call(
         partner_kernel,
@@ -433,17 +419,15 @@
     )
     from_second = swap(second, 2)
     from_first = swap(first, 0)
+    partial = call(
+        own_forward_kernel, shape((rows, wide), F32), [VMEM] * 2, (smooth, own_blocks)
+    )
     return call(
         forward_kernel,
         shape(fields.shape, F32),
-        [VMEM] * 8,
-        (pattern, smooth, second, first, from_second, from_first, interp, conv),
-        [
-            pltpu.VMEM((tiles + 8,) + tile_shape, BF16),
-            pltpu.VMEM((tiles,) + tile_shape, BF16),
-            table,
-            pltpu.SemaphoreType.DMA,
-        ],
+        [VMEM] * 7,
+        (partial, second, first, from_second, from_first, received_blocks, interp),
+        [pltpu.VMEM((rows, wide), BF16), pltpu.VMEM((rows, wide), BF16)],
     )
 
 

time: 53.2 us -> 52.2 us (0.981)
  waiting for transfers between devices: 13.9 us -> 9.77 us
  local copies, waits for them, and re-layouts: 0.11 us -> 3.03 us
    unnamed x5 -> x11, local copies, waits for them, and re-layouts: 0.11 us -> 3.03 us
    ppermute x1, waiting for transfers between devices: 3.81 us -> 1.47 us  [shards(): high = lax.ppermute(bottom, 'lev', [(i + 1, i) for i in range(levs - 1)])]
    ppermute x4, waiting for transfers between devices: 9.23 us -> 7.41 us  [swap(): return lax.ppermute(block, 'patch', partner)]
    pallas_call x8 -> x9, Pallas kernels: 9.82 us -> 10 us  [call(): pl.pallas_call(kernel, out_shape=outs, in_specs=specs, out_specs=jax.tree...]
  transfers between devices with their start and end apart: 7 -> 7, of which waited for: 4 -> 4; matrix products, arithmetic and copies ran while one was open for 0% -> 0% of each run, Pallas kernels for 6% -> 9%
where the time goes in v5:
time: 52.2 us; the launch traced here: 51.8 us
  starting transfers between devices  28.8 us (55%)
  Pallas kernels  10 us (19%)
  waiting for transfers between devices  9.77 us (19%)
  local copies, waits for them, and re-layouts  3.03 us (6%)
    ppermute x4, starting transfers between devices, swap(): return lax.ppermute(block, 'patch', partner)  20.3 us
    pallas_call x9, Pallas kernels, call(): pl.pallas_call(kernel, out_shape=outs, in_specs=specs, out_specs=jax.tree...  10 us
    ppermute x4, waiting for transfers between devices, swap(): return lax.ppermute(block, 'patch', partner)  7.41 us
    ppermute x1, starting transfers between devices, shards(): low = lax.ppermute(top, 'lev', [(i, i + 1) for i in range(levs - 1)])  4.7 us
    unnamed x11, local copies, waits for them, and re-layouts  3.03 us
    ppermute x1, starting transfers between devices, shards(): high = lax.ppermute(bottom, 'lev', [(i + 1, i) for i in range(levs - 1)])  1.92 us
    ppermute x1, starting transfers between devices, shards(): lax.ppermute(payload, 'patch', [(i, i ^ 1) for i in range(patches)])  1.92 us
    ppermute x1, waiting for transfers between devices, shards(): high = lax.ppermute(bottom, 'lev', [(i + 1, i) for i in range(levs - 1)])  1.47 us
  transfers between devices with their start and end apart: 7, of which 4 were waited for; matrix products, arithmetic and copies ran while one was open for 0% of the time, Pallas kernels for 9%

profile of v5, /device:TPU:24, one launch (start us, length us, event | category | flops | bytes accessed | tf_op | source)
XLA Modules:
  0.0 51.8 jit_solution(2768984388409545183)
XLA Ops:
  0.0 1.5 %shard_map.64 = (bf16[128,1024]{1,0:T(8,128)(2,1)S(1)}, bf16[32,1024]{1,0:T(8,128)(2,1)S(1)}, bf16[32,1024]{1,0:T(8,128)(2,1)S(1)}, f32[5,128]{1,0:T(8,128)S(1)}) custom-call(bf16[8,16,2048]{2,1,0:T(8,128)(2,1)} %fields.1, bf16[8,128,256]{2,1,0:T(8,128)(2,1)} %interp.3, f32[5,128]{1,0:T(8,128)} %bitcast.1), custom_call_target="tpu_custom_call" | custom-call | flops 16777216 | bytes 1048576 | tf_op jit(solution)/shard_map/pallas_call | solution.py:317
  1.5 4.7 %collective-permute-start = (bf16[32,1024]{1,0:T(8,128)(2,1)S(1)}, bf16[32,1024]{1,0:T(8,128)(2,1)S(1)}, u32[]{:S(2)}, u32[]{:S(2)}) collective-permute-start(bf16[32,1024]{1,0:T(8,128)(2,1)S(1)} %get-tuple-element.23), channel_id=1, source_target_pairs={{0,1},{1,2},{2,3},{3,4},{4,5},{5,6},{6,7},{8,9},{9,10},{10,11},{11... | collective-permute-start | bytes 196616 | tf_op jit(solution)/shard_map/ppermute | solution.py:370
  6.2 1.9 %collective-permute-start.1 = (bf16[32,1024]{1,0:T(8,128)(2,1)S(1)}, bf16[32,1024]{1,0:T(8,128)(2,1)S(1)}, u32[]{:S(2)}, u32[]{:S(2)}) collective-permute-start(bf16[32,1024]{1,0:T(8,128)(2,1)S(1)} %get-tuple-element.24), channel_id=1, source_target_pairs={{1,0},{2,1},{3,2},{4,3},{5,4},{6,5},{7,6},{9,8},{10,9},{11,10},{12... | collective-permute-start | bytes 196616 | tf_op jit(solution)/shard_map/ppermute | solution.py:371
  8.2 0.0 copy-start.4
  8.2 2.6 %shard_map.65 = (f32[128,1024]{1,0:T(8,128)S(1)}, bf16[128,128]{1,0:T(8,128)(2,1)S(1)}, bf16[8,128,1024]{2,1,0:T(8,128)(2,1)S(1)}, bf16[8,128,1024]{2,1,0:T(8,128)(2,1)S(1)}) custom-call(bf16[128,1024]{1,0:T(8,128)(2,1)S(1)} %get-tuple-element.19.coarse, f32[5,128]{1,0:T(8,128)S(1)} %get-tuple-element.20.weights, s32[8,8]{1,0:T(8,128)} %pattern.1, ...), custom_call_target="tpu_custom_call" | custom-call | flops 16777216 | bytes 1048576 | tf_op jit(solution)/shard_map/pallas_call | solution.py:317
  10.8 0.0 copy-start
  10.8 1.3 %copy-done = bf16[8,128,1024]{2,1,0:T(8,128)(2,1)} copy-done((bf16[8,128,1024]{2,1,0:T(8,128)(2,1)}, bf16[8,128,1024]{2,1,0:T(8,128)(2,1)S(1)}, u32[]{:S(2)}) %copy-start) | copy-done | bytes 2097176
  12.1 0.0 collective-permute-done.low
  12.1 1.5 %collective-permute-done.1.high = bf16[32,1024]{1,0:T(8,128)(2,1)S(1)} collective-permute-done((bf16[32,1024]{1,0:T(8,128)(2,1)S(1)}, bf16[32,1024]{1,0:T(8,128)(2,1)S(1)}, u32[]{:S(2)}, u32[]{:S(2)}) %collective-permute-start.1) | collective-permute-done | bytes 65568 | tf_op jit(solution)/shard_map/ppermute | solution.py:371
  13.6 0.9 %shard_map.66 = (bf16[128,1024]{1,0:T(8,128)(2,1)S(1)}, bf16[4,128,128]{2,1,0:T(8,128)(2,1)S(1)}, bf16[4,128,128]{2,1,0:T(8,128)(2,1)S(1)}) custom-call(f32[128,1024]{1,0:T(8,128)S(1)} %get-tuple-element.21.partial, bf16[128,128]{1,0:T(8,128)(2,1)S(1)} %get-tuple-element.22.halo_matrix, bf16[32,1024]{1,0:T(8,128)(2,1)S(1)} %collective-permute-done.low, ...), custom_call_target="tpu_custom_call" | custom-call | flops 16777216 | bytes 1048576 | tf_op jit(solution)/shard_map/pallas_call | solution.py:317
  14.5 13.1 %collective-permute-start.2 = (bf16[4,128,128]{2,1,0:T(8,128)(2,1)S(1)}, bf16[4,128,128]{2,1,0:T(8,128)(2,1)S(1)}, u32[]{:S(2)}, u32[]{:S(2)}) collective-permute-start(bf16[4,128,128]{2,1,0:T(8,128)(2,1)S(1)} %get-tuple-element.28.second), channel_id=1, source_target_pairs={{0,496},{8,504},{16,32},{24,40},{32,16},{40,24},{48,64},{56,72},{6... | collective-permute-start | bytes 393224 | tf_op jit(solution)/shard_map/ppermute | solution.py:352
  27.7 1.9 %collective-permute-start.3 = (bf16[4,128,128]{2,1,0:T(8,128)(2,1)S(1)}, bf16[4,128,128]{2,1,0:T(8,128)(2,1)S(1)}, u32[]{:S(2)}, u32[]{:S(2)}) collective-permute-start(bf16[4,128,128]{2,1,0:T(8,128)(2,1)S(1)} %get-tuple-element.29.first), channel_id=1, source_target_pairs={{0,16},{8,24},{16,0},{24,8},{32,48},{40,56},{48,32},{56,40},{64,80... | collective-permute-start | bytes 393224 | tf_op jit(solution)/shard_map/ppermute | solution.py:352
  29.6 0.0 copy-done.4
  29.6 0.1 copy.9.send
  29.7 0.0 copy-start.1
  29.7 1.6 %copy-done.1 = bf16[8,128,1024]{2,1,0:T(8,128)(2,1)S(1)} copy-done((bf16[8,128,1024]{2,1,0:T(8,128)(2,1)S(1)}, bf16[8,128,1024]{2,1,0:T(8,128)(2,1)}, u32[]{:S(2)}) %copy-start.1) | copy-done | bytes 2097176
  31.3 0.8 %shard_map.67.own = f32[8,128,128]{2,1,0:T(8,128)S(1)} custom-call(bf16[128,1024]{1,0:T(8,128)(2,1)S(1)} %get-tuple-element.26.smooth, bf16[8,128,1024]{2,1,0:T(8,128)(2,1)S(1)} %copy-done.1), custom_call_target="tpu_custom_call" | custom-call | flops 16777216 | bytes 1048576 | tf_op jit(solution)/shard_map/pallas_call | solution.py:317
  32.1 0.0 copy-start.2
  32.1 0.0 collective-permute-done.2.from_second
  32.2 2.4 %collective-permute-done.3.from_first = bf16[4,128,128]{2,1,0:T(8,128)(2,1)S(1)} collective-permute-done((bf16[4,128,128]{2,1,0:T(8,128)(2,1)S(1)}, bf16[4,128,128]{2,1,0:T(8,128)(2,1)S(1)}, u32[]{:S(2)}, u32[]{:S(2)}) %collective-permute-start.3) | collective-permute-done | bytes 131104 | tf_op jit(solution)/shard_map/ppermute | solution.py:352
  34.5 0.7 %shard_map.69.payload = bf16[9,128,128]{2,1,0:T(8,128)(2,1)S(1)} custom-call(s32[1,4,2]{2,1,0:T(4,128)S(1)} %copy.9.send, f32[8,128,128]{2,1,0:T(8,128)S(1)} %shard_map.67.own, bf16[4,128,128]{2,1,0:T(8,128)(2,1)S(1)} %get-tuple-element.28.second, bf16[4,128,128]{2,1,0:T(8,128)(2,1)S(1)} %get-tuple-element.29.first, ...), custom_call_target="tpu_custom_call" | custom-call | flops 16777216 | bytes 1048576 | tf_op jit(solution)/shard_map/pallas_call | solution.py:317
  35.2 1.9 %collective-permute-start.4 = (bf16[9,128,128]{2,1,0:T(8,128)(2,1)S(1)}, bf16[9,128,128]{2,1,0:T(8,128)(2,1)S(1)}, u32[]{:S(2)}, u32[]{:S(2)}) collective-permute-start(bf16[9,128,128]{2,1,0:T(8,128)(2,1)S(1)} %shard_map.69.payload), channel_id=1, source_target_pairs={{0,8},{8,0},{16,24},{24,16},{32,40},{40,32},{48,56},{56,48},{64,72... | collective-permute-start | bytes 884744 | tf_op jit(solution)/shard_map/ppermute | solution.py:406
  37.2 0.6 %shard_map.68.partial = f32[8,128,128]{2,1,0:T(8,128)S(1)} custom-call(s32[1,4,2]{2,1,0:T(4,128)S(1)} %copy.9.send, f32[8,128,128]{2,1,0:T(8,128)S(1)} %shard_map.67.own, bf16[4,128,128]{2,1,0:T(8,128)(2,1)S(1)} %collective-permute-done.2.from_second, bf16[4,128,128]{2,1,0:T(8,128)(2,1)S(1)} %collective-permute-done.3.from_first), custom_call_target="tpu_custom_call" | custom-call | flops 16777216 | bytes 1048576 | tf_op jit(solution)/shard_map/pallas_call | solution.py:317
  37.8 0.0 copy-start.3
  37.8 0.9 %collective-permute-done.4.arrived = bf16[9,128,128]{2,1,0:T(8,128)(2,1)S(1)} collective-permute-done((bf16[9,128,128]{2,1,0:T(8,128)(2,1)S(1)}, bf16[9,128,128]{2,1,0:T(8,128)(2,1)S(1)}, u32[]{:S(2)}, u32[]{:S(2)}) %collective-permute-start.4) | collective-permute-done | bytes 294944 | tf_op jit(solution)/shard_map/ppermute | solution.py:406
  38.7 0.7 %shard_map.70 = (bf16[8,128,128]{2,1,0:T(8,128)(2,1)S(1)}, bf16[4,128,128]{2,1,0:T(8,128)(2,1)S(1)}, bf16[4,128,128]{2,1,0:T(8,128)(2,1)S(1)}) custom-call(s32[1,4,2]{2,1,0:T(4,128)S(1)} %copy.9.send, f32[8,128,128]{2,1,0:T(8,128)S(1)} %shard_map.68.partial, bf16[9,128,128]{2,1,0:T(8,128)(2,1)S(1)} %shard_map.69.payload, ...), custom_call_target="tpu_custom_call" | custom-call | flops 16777216 | bytes 1048576 | tf_op jit(solution)/shard_map/pallas_call | solution.py:317
  39.4 3.3 %collective-permute-start.5 = (bf16[4,128,128]{2,1,0:T(8,128)(2,1)S(1)}, bf16[4,128,128]{2,1,0:T(8,128)(2,1)S(1)}, u32[]{:S(2)}, u32[]{:S(2)}) collective-permute-start(bf16[4,128,128]{2,1,0:T(8,128)(2,1)S(1)} %get-tuple-element.31.second), channel_id=1, source_target_pairs={{0,496},{8,504},{16,32},{24,40},{32,16},{40,24},{48,64},{56,72},{6... | collective-permute-start | bytes 393224 | tf_op jit(solution)/shard_map/ppermute | solution.py:352
  42.7 1.9 %collective-permute-start.6 = (bf16[4,128,128]{2,1,0:T(8,128)(2,1)S(1)}, bf16[4,128,128]{2,1,0:T(8,128)(2,1)S(1)}, u32[]{:S(2)}, u32[]{:S(2)}) collective-permute-start(bf16[4,128,128]{2,1,0:T(8,128)(2,1)S(1)} %get-tuple-element.32.first), channel_id=1, source_target_pairs={{0,16},{8,24},{16,0},{24,8},{32,48},{40,56},{48,32},{56,40},{64,80... | collective-permute-start | bytes 393224 | tf_op jit(solution)/shard_map/ppermute | solution.py:352
  44.6 0.0 copy-done.2
  44.6 0.5 shard_map.71.partial
  45.1 5.0 %collective-permute-done.5.from_second = bf16[4,128,128]{2,1,0:T(8,128)(2,1)S(1)} collective-permute-done((bf16[4,128,128]{2,1,0:T(8,128)(2,1)S(1)}, bf16[4,128,128]{2,1,0:T(8,128)(2,1)S(1)}, u32[]{:S(2)}, u32[]{:S(2)}) %collective-permute-start.5) | collective-permute-done | bytes 131104 | tf_op jit(solution)/shard_map/ppermute | solution.py:352
  50.1 0.0 collective-permute-done.6.from_first
  50.1 0.0 copy-done.3
  50.1 1.7 %shard_map.72 = f32[8,16,2048]{2,1,0:T(8,128)} custom-call(f32[128,1024]{1,0:T(8,128)S(1)} %shard_map.71.partial, bf16[4,128,128]{2,1,0:T(8,128)(2,1)S(1)} %get-tuple-element.31.second, bf16[4,128,128]{2,1,0:T(8,128)(2,1)S(1)} %get-tuple-element.32.first, bf16[4,128,128]{2,1,0:T(8,128)(2,1)S(1)} %collective-permute-done.5.from_second, ...), custom_call_target="tpu_custom_call" | custom-call | flops 16777216 | bytes 1048576 | tf_op jit(solution)/shard_map/pallas_call | solution.py:317
Async XLA Ops:
  1.5 10.6 %collective-permute-start = (bf16[32,1024]{1,0:T(8,128)(2,1)S(1)}, bf16[32,1024]{1,0:T(8,128)(2,1)S(1)}, u32[]{:S(2)}, u32[]{:S(2)}) collective-permute-start(bf16[32,1024]{1,0:T(8,128)(2,1)S(1)} %get-tuple-element.23), channel_id=1, source_target_pairs={{0,1},{1,2},{2,3},{3,4},{4,5},{5,6},{6,7},{8,9},{9,10},{10,11},{11... | collective-permute-start | bytes 196616 | tf_op jit(solution)/shard_map/ppermute | solution.py:370
  6.2 7.4 %collective-permute-start.1 = (bf16[32,1024]{1,0:T(8,128)(2,1)S(1)}, bf16[32,1024]{1,0:T(8,128)(2,1)S(1)}, u32[]{:S(2)}, u32[]{:S(2)}) collective-permute-start(bf16[32,1024]{1,0:T(8,128)(2,1)S(1)} %get-tuple-element.24), channel_id=1, source_target_pairs={{1,0},{2,1},{3,2},{4,3},{5,4},{6,5},{7,6},{9,8},{10,9},{11,10},{12... | collective-permute-start | bytes 196616 | tf_op jit(solution)/shard_map/ppermute | solution.py:371
  8.2 21.4 %copy-start.4 = (s32[1,4,2]{1,2,0:T(2,128)S(1)}, s32[1,4,2]{1,2,0:T(2,128)}, u32[]{:S(2)}) copy-start(s32[1,4,2]{1,2,0:T(2,128)} %param.10) | copy-start | bytes 100
  10.8 1.3 %copy-start = (bf16[8,128,1024]{2,1,0:T(8,128)(2,1)}, bf16[8,128,1024]{2,1,0:T(8,128)(2,1)S(1)}, u32[]{:S(2)}) copy-start(bf16[8,128,1024]{2,1,0:T(8,128)(2,1)S(1)} %get-tuple-element.27.own_blocks) | copy-start | bytes 6291460
  14.5 17.6 %collective-permute-start.2 = (bf16[4,128,128]{2,1,0:T(8,128)(2,1)S(1)}, bf16[4,128,128]{2,1,0:T(8,128)(2,1)S(1)}, u32[]{:S(2)}, u32[]{:S(2)}) collective-permute-start(bf16[4,128,128]{2,1,0:T(8,128)(2,1)S(1)} %get-tuple-element.28.second), channel_id=1, source_target_pairs={{0,496},{8,504},{16,32},{24,40},{32,16},{40,24},{48,64},{56,72},{6... | collective-permute-start | bytes 393224 | tf_op jit(solution)/shard_map/ppermute | solution.py:352
  27.7 6.9 %collective-permute-start.3 = (bf16[4,128,128]{2,1,0:T(8,128)(2,1)S(1)}, bf16[4,128,128]{2,1,0:T(8,128)(2,1)S(1)}, u32[]{:S(2)}, u32[]{:S(2)}) collective-permute-start(bf16[4,128,128]{2,1,0:T(8,128)(2,1)S(1)} %get-tuple-element.29.first), channel_id=1, source_target_pairs={{0,16},{8,24},{16,0},{24,8},{32,48},{40,56},{48,32},{56,40},{64,80... | collective-permute-start | bytes 393224 | tf_op jit(solution)/shard_map/ppermute | solution.py:352
  29.7 1.6 %copy-start.1 = (bf16[8,128,1024]{2,1,0:T(8,128)(2,1)S(1)}, bf16[8,128,1024]{2,1,0:T(8,128)(2,1)}, u32[]{:S(2)}) copy-start(bf16[8,128,1024]{2,1,0:T(8,128)(2,1)} %copy-done) | copy-start | bytes 6291460
  32.1 12.5 %copy-start.2 = (bf16[8,128,1024]{2,1,0:T(8,128)(2,1)S(1)}, bf16[8,128,1024]{2,1,0:T(8,128)(2,1)}, u32[]{:S(2)}) copy-start(bf16[8,128,1024]{2,1,0:T(8,128)(2,1)} %copy-done) | copy-start | bytes 6291460
  35.2 3.5 %collective-permute-start.4 = (bf16[9,128,128]{2,1,0:T(8,128)(2,1)S(1)}, bf16[9,128,128]{2,1,0:T(8,128)(2,1)S(1)}, u32[]{:S(2)}, u32[]{:S(2)}) collective-permute-start(bf16[9,128,128]{2,1,0:T(8,128)(2,1)S(1)} %shard_map.69.payload), channel_id=1, source_target_pairs={{0,8},{8,0},{16,24},{24,16},{32,40},{40,32},{48,56},{56,48},{64,72... | collective-permute-start | bytes 884744 | tf_op jit(solution)/shard_map/ppermute | solution.py:406
  37.8 12.3 %copy-start.3 = (bf16[8,128,256]{2,1,0:T(8,128)(2,1)S(1)}, bf16[8,128,256]{2,1,0:T(8,128)(2,1)}, u32[]{:S(2)}) copy-start(bf16[8,128,256]{2,1,0:T(8,128)(2,1)} %interp.3) | copy-start | bytes 1572868
  39.4 10.8 %collective-permute-start.5 = (bf16[4,128,128]{2,1,0:T(8,128)(2,1)S(1)}, bf16[4,128,128]{2,1,0:T(8,128)(2,1)S(1)}, u32[]{:S(2)}, u32[]{:S(2)}) collective-permute-start(bf16[4,128,128]{2,1,0:T(8,128)(2,1)S(1)} %get-tuple-element.31.second), channel_id=1, source_target_pairs={{0,496},{8,504},{16,32},{24,40},{32,16},{40,24},{48,64},{56,72},{6... | collective-permute-start | bytes 393224 | tf_op jit(solution)/shard_map/ppermute | solution.py:352
  42.7 7.4 %collective-permute-start.6 = (bf16[4,128,128]{2,1,0:T(8,128)(2,1)S(1)}, bf16[4,128,128]{2,1,0:T(8,128)(2,1)S(1)}, u32[]{:S(2)}, u32[]{:S(2)}) collective-permute-start(bf16[4,128,128]{2,1,0:T(8,128)(2,1)S(1)} %get-tuple-element.32.first), channel_id=1, source_target_pairs={{0,16},{8,24},{16,0},{24,8},{32,48},{40,56},{48,32},{56,40},{64,80... | collective-permute-start | bytes 393224 | tf_op jit(solution)/shard_map/ppermute | solution.py:352

commit v6 on v5

--- a/solution.py
+++ b/solution.py
@@ -71,17 +71,34 @@
         copy.wait()
 
 
-def vertical_kernel(
-    level_len, halo, coarse, weights, pattern, conv, partial, halo_matrix, own_blocks,
-    received_blocks, conv_copy, table, sems
-):
+def fetch_weights(pattern, conv, table, conv_copy, sems):
     fetches = (
         pltpu.make_async_copy(pattern, table, sems.at[0]),
         pltpu.make_async_copy(conv, conv_copy, sems.at[1]),
     )
     for fetch in fetches:
         fetch.start()
-    tiles, count, tile_len, _ = conv.shape
+    return fetches
+
+
+def lay_blocks(fetches, table, conv_copy, blocks, first_entry):
+    tiles, count, tile_len, _ = conv_copy.shape
+    spare = blocks.shape[0] - 1
+    for fetch in fetches:
+        fetch.wait()
+    for t in range(tiles):
+        for k in range(count):
+            entry = table[t, k] - first_entry
+            entry = jnp.where((entry >= 0) & (entry < spare), entry, spare)
+            blocks[entry, :, lanes(t, tile_len)] = conv_copy[t, k]
+
+
+def vertical_kernel(
+    level_len, halo, coarse, weights, pattern, conv, partial, halo_matrix, received_blocks,
+    conv_copy, table, sems
+):
+    fetches = fetch_weights(pattern, conv, table, conv_copy, sems)
+    received_blocks[...] = jnp.zeros_like(received_blocks)
     rows = coarse.shape[0]
     halo_rows = rows // level_len * halo
     taps, levels = weights.shape
@@ -116,21 +133,7 @@
     own_matrix = jnp.concatenate(own_parts, axis=1)
     value = coarse[...]
     partial[...] = nn(own_matrix, jnp.concatenate([value, value], axis=0))
-    own_blocks[...] = jnp.zeros_like(own_blocks)
-    received_blocks[...] = jnp.zeros_like(received_blocks)
-    for fetch in fetches:
-        fetch.wait()
-    for t in range(tiles):
-        for k in range(count):
-            entry = table[t, k]
-
-            @pl.when(entry < tiles)
-            def _():
-                own_blocks[entry, :, lanes(t, tile_len)] = conv_copy[t, k]
-
-            @pl.when(entry >= tiles)
-            def _():
-                received_blocks[entry - tiles, :, lanes(t, tile_len)] = conv_copy[t, k]
+    lay_blocks(fetches, table, conv_copy, received_blocks, conv.shape[0])
 
 
 def by_chip(body, first, second):
@@ -146,7 +149,8 @@
 
 
 def flat(blocks):
-    return blocks[...].reshape(-1, blocks.shape[-1])
+    entries = blocks.shape[0] - 1
+    return blocks[:entries].reshape(-1, blocks.shape[-1])
 
 
 def adjoint_kernel(partial, halo_matrix, low, high, received_blocks, smooth, second, first):
@@ -166,8 +170,11 @@
     by_chip(sides, first, second)
 
 
-def own_kernel(smooth, own_blocks, own):
-    value = nt(smooth[...], flat(own_blocks))
+def own_kernel(smooth, pattern, conv, own, blocks, conv_copy, table, sems):
+    fetches = fetch_weights(pattern, conv, table, conv_copy, sems)
+    blocks[...] = jnp.zeros_like(blocks)
+    lay_blocks(fetches, table, conv_copy, blocks, 0)
+    value = nt(smooth[...], flat(blocks))
     for t in range(own.shape[0]):
         own[t] = value[:, lanes(t, own.shape[2])]
 
@@ -341,7 +348,7 @@
     tile_list = shape((tiles,) + tile_shape, F32)
     narrow_list = shape((tiles,) + tile_shape, BF16)
     edge_list = shape((members * halo, wide), BF16)
-    block_list = shape((tiles, tile_len, wide), BF16)
+    block_list = shape((tiles + 1, tile_len, wide), BF16)
     four = shape((4,) + tile_shape, BF16)
 
     def swap(block, start):
@@ -369,21 +376,17 @@
     )
     low = lax.ppermute(top, "lev", [(i, i + 1) for i in range(levs - 1)])
     high = lax.ppermute(bottom, "lev", [(i + 1, i) for i in range(levs - 1)])
-    partial, halo_matrix, own_blocks, received_blocks = call(
+    weight_scratch = [
+        pltpu.VMEM(conv_weight.shape, BF16),
+        pltpu.SMEM(tile_pattern.shape, jnp.int32),
+        pltpu.SemaphoreType.DMA((2,)),
+    ]
+    partial, halo_matrix, received_blocks = call(
         functools.partial(vertical_kernel, level_len, halo),
-        (
-            shape((rows, wide), F32),
-            shape((rows, 4 * members * halo), BF16),
-            block_list,
-            block_list,
-        ),
+        (shape((rows, wide), F32), shape((rows, 4 * members * halo), BF16), block_list),
         [VMEM] * 2 + [HBM] * 2,
         (coarse, weights, in_hbm(tile_pattern), in_hbm(conv_weight)),
-        [
-            pltpu.VMEM(conv_weight.shape, BF16),
-            pltpu.SMEM(tile_pattern.shape, jnp.int32),
-            pltpu.SemaphoreType.DMA((2,)),
-        ],
+        weight_scratch,
     )
     sem = pltpu.SemaphoreType.DMA
     vertical, second, first = call(
@@ -394,7 +397,13 @@
     )
     from_second = swap(second, 2)
     from_first = swap(first, 0)
-    own = call(own_kernel, tile_list, [VMEM] * 2, (vertical, own_blocks))
+    own, own_blocks = call(
+        own_kernel,
+        (tile_list, block_list),
+        [VMEM] + [HBM] * 2,
+        (vertical, in_hbm(tile_pattern), in_hbm(conv_weight)),
+        weight_scratch,
+    )
     links = pltpu.SMEM(send_tiles.shape, jnp.int32)
     payload = call(
         partner_kernel,

time: 52.2 us -> 52.2 us (level)
  local copies, waits for them, and re-layouts: 3.03 us -> 0.11 us
  Pallas kernels: 10 us -> 12.6 us
    unnamed x11 -> x5, local copies, waits for them, and re-layouts: 3.03 us -> 0.11 us
    pallas_call x9, Pallas kernels: 10 us -> 12.6 us  [call(): pl.pallas_call(kernel, out_shape=outs, in_specs=specs, out_specs=jax.tree...]
    ppermute x1, waiting for transfers between devices: 1.47 us -> 2.36 us  [shards(): high = lax.ppermute(bottom, 'lev', [(i + 1, i) for i in range(levs - 1)])]
    ppermute x4, waiting for transfers between devices: 7.41 us -> 6.82 us  [swap(): return lax.ppermute(block, 'patch', partner)]
  transfers between devices with their start and end apart: 7 -> 7, of which waited for: 4 -> 4; matrix products, arithmetic and copies ran while one was open for 0% -> 0% of each run, Pallas kernels for 9% -> 14%
where the time goes in v6:
time: 52.2 us; the launch traced here: 51.8 us
  starting transfers between devices  28.8 us (55%)
  Pallas kernels  12.6 us (24%)
  waiting for transfers between devices  10.1 us (19%)
    ppermute x4, starting transfers between devices, swap(): return lax.ppermute(block, 'patch', partner)  20.3 us
    pallas_call x9, Pallas kernels, call(): pl.pallas_call(kernel, out_shape=outs, in_specs=specs, out_specs=jax.tree...  12.6 us
    ppermute x4, waiting for transfers between devices, swap(): return lax.ppermute(block, 'patch', partner)  6.82 us
    ppermute x1, starting transfers between devices, shards(): low = lax.ppermute(top, 'lev', [(i, i + 1) for i in range(levs - 1)])  4.7 us
    ppermute x1, waiting for transfers between devices, shards(): high = lax.ppermute(bottom, 'lev', [(i + 1, i) for i in range(levs - 1)])  2.36 us
    ppermute x1, starting transfers between devices, shards(): high = lax.ppermute(bottom, 'lev', [(i + 1, i) for i in range(levs - 1)])  1.92 us
    ppermute x1, starting transfers between devices, shards(): lax.ppermute(payload, 'patch', [(i, i ^ 1) for i in range(patches)])  1.92 us
  transfers between devices with their start and end apart: 7, of which 4 were waited for; matrix products, arithmetic and copies ran while one was open for 0% of the time, Pallas kernels for 14%

profile of v6, /device:TPU:24, one launch (start us, length us, event | category | flops | bytes accessed | tf_op | source)
XLA Modules:
  0.0 51.8 jit_solution(17674971767238220752)
XLA Ops:
  0.0 1.5 %shard_map.64 = (bf16[128,1024]{1,0:T(8,128)(2,1)S(1)}, bf16[32,1024]{1,0:T(8,128)(2,1)S(1)}, bf16[32,1024]{1,0:T(8,128)(2,1)S(1)}, f32[5,128]{1,0:T(8,128)S(1)}) custom-call(bf16[8,16,2048]{2,1,0:T(8,128)(2,1)} %fields.1, bf16[8,128,256]{2,1,0:T(8,128)(2,1)} %interp.3, f32[5,128]{1,0:T(8,128)} %bitcast.1), custom_call_target="tpu_custom_call" | custom-call | flops 16777216 | bytes 1048576 | tf_op jit(solution)/shard_map/pallas_call | solution.py:324
  1.5 4.7 %collective-permute-start = (bf16[32,1024]{1,0:T(8,128)(2,1)S(1)}, bf16[32,1024]{1,0:T(8,128)(2,1)S(1)}, u32[]{:S(2)}, u32[]{:S(2)}) collective-permute-start(bf16[32,1024]{1,0:T(8,128)(2,1)S(1)} %get-tuple-element.24), channel_id=1, source_target_pairs={{0,1},{1,2},{2,3},{3,4},{4,5},{5,6},{6,7},{8,9},{9,10},{10,11},{11... | collective-permute-start | bytes 196616 | tf_op jit(solution)/shard_map/ppermute | solution.py:377
  6.2 1.9 %collective-permute-start.1 = (bf16[32,1024]{1,0:T(8,128)(2,1)S(1)}, bf16[32,1024]{1,0:T(8,128)(2,1)S(1)}, u32[]{:S(2)}, u32[]{:S(2)}) collective-permute-start(bf16[32,1024]{1,0:T(8,128)(2,1)S(1)} %get-tuple-element.25), channel_id=1, source_target_pairs={{1,0},{2,1},{3,2},{4,3},{5,4},{6,5},{7,6},{9,8},{10,9},{11,10},{12... | collective-permute-start | bytes 196616 | tf_op jit(solution)/shard_map/ppermute | solution.py:378
  8.2 0.0 copy-start.1
  8.2 3.0 %shard_map.65 = (f32[128,1024]{1,0:T(8,128)S(1)}, bf16[128,128]{1,0:T(8,128)(2,1)S(1)}, bf16[9,128,1024]{2,1,0:T(8,128)(2,1)S(1)}) custom-call(bf16[128,1024]{1,0:T(8,128)(2,1)S(1)} %get-tuple-element.20.coarse, f32[5,128]{1,0:T(8,128)S(1)} %get-tuple-element.21.weights, s32[8,8]{1,0:T(8,128)} %pattern.3, bf16[8,8,128,128]{3,2,1,0:T(8,128)(2,1)} %conv.3), custom_call_target="tpu_custom_call" | custom-call | flops 16777216 | bytes 1048576 | tf_op jit(solution)/shard_map/pallas_call | solution.py:324
  11.2 0.0 collective-permute-done.low
  11.2 2.4 %collective-permute-done.1.high = bf16[32,1024]{1,0:T(8,128)(2,1)S(1)} collective-permute-done((bf16[32,1024]{1,0:T(8,128)(2,1)S(1)}, bf16[32,1024]{1,0:T(8,128)(2,1)S(1)}, u32[]{:S(2)}, u32[]{:S(2)}) %collective-permute-start.1) | collective-permute-done | bytes 65568 | tf_op jit(solution)/shard_map/ppermute | solution.py:378
  13.6 0.9 %shard_map.66 = (bf16[128,1024]{1,0:T(8,128)(2,1)S(1)}, bf16[4,128,128]{2,1,0:T(8,128)(2,1)S(1)}, bf16[4,128,128]{2,1,0:T(8,128)(2,1)S(1)}) custom-call(f32[128,1024]{1,0:T(8,128)S(1)} %get-tuple-element.22.partial, bf16[128,128]{1,0:T(8,128)(2,1)S(1)} %get-tuple-element.23.halo_matrix, bf16[32,1024]{1,0:T(8,128)(2,1)S(1)} %collective-permute-done.low, ...), custom_call_target="tpu_custom_call" | custom-call | flops 16777216 | bytes 1048576 | tf_op jit(solution)/shard_map/pallas_call | solution.py:324
  14.5 13.1 %collective-permute-start.2 = (bf16[4,128,128]{2,1,0:T(8,128)(2,1)S(1)}, bf16[4,128,128]{2,1,0:T(8,128)(2,1)S(1)}, u32[]{:S(2)}, u32[]{:S(2)}) collective-permute-start(bf16[4,128,128]{2,1,0:T(8,128)(2,1)S(1)} %get-tuple-element.29.second), channel_id=1, source_target_pairs={{0,496},{8,504},{16,32},{24,40},{32,16},{40,24},{48,64},{56,72},{6... | collective-permute-start | bytes 393224 | tf_op jit(solution)/shard_map/ppermute | solution.py:359
  27.7 1.9 %collective-permute-start.3 = (bf16[4,128,128]{2,1,0:T(8,128)(2,1)S(1)}, bf16[4,128,128]{2,1,0:T(8,128)(2,1)S(1)}, u32[]{:S(2)}, u32[]{:S(2)}) collective-permute-start(bf16[4,128,128]{2,1,0:T(8,128)(2,1)S(1)} %get-tuple-element.30.first), channel_id=1, source_target_pairs={{0,16},{8,24},{16,0},{24,8},{32,48},{40,56},{48,32},{56,40},{64,80... | collective-permute-start | bytes 393224 | tf_op jit(solution)/shard_map/ppermute | solution.py:359
  29.6 0.0 copy-done.1
  29.6 0.1 copy.9.send
  29.7 3.0 %shard_map.67 = (f32[8,128,128]{2,1,0:T(8,128)S(1)}, bf16[9,128,1024]{2,1,0:T(8,128)(2,1)S(1)}) custom-call(bf16[128,1024]{1,0:T(8,128)(2,1)S(1)} %get-tuple-element.27.smooth, s32[8,8]{1,0:T(8,128)} %pattern.3, bf16[8,8,128,128]{3,2,1,0:T(8,128)(2,1)} %conv.3), custom_call_target="tpu_custom_call" | custom-call | flops 16777216 | bytes 1048576 | tf_op jit(solution)/shard_map/pallas_call | solution.py:324
  32.8 0.0 collective-permute-done.2.from_second
  32.8 1.8 %collective-permute-done.3.from_first = bf16[4,128,128]{2,1,0:T(8,128)(2,1)S(1)} collective-permute-done((bf16[4,128,128]{2,1,0:T(8,128)(2,1)S(1)}, bf16[4,128,128]{2,1,0:T(8,128)(2,1)S(1)}, u32[]{:S(2)}, u32[]{:S(2)}) %collective-permute-start.3) | collective-permute-done | bytes 131104 | tf_op jit(solution)/shard_map/ppermute | solution.py:359
  34.5 0.7 %shard_map.69.payload = bf16[9,128,128]{2,1,0:T(8,128)(2,1)S(1)} custom-call(s32[1,4,2]{2,1,0:T(4,128)S(1)} %copy.9.send, f32[8,128,128]{2,1,0:T(8,128)S(1)} %get-tuple-element.28.own, bf16[4,128,128]{2,1,0:T(8,128)(2,1)S(1)} %get-tuple-element.29.second, bf16[4,128,128]{2,1,0:T(8,128)(2,1)S(1)} %get-tuple-element.30.first, ...), custom_call_target="tpu_custom_call" | custom-call | flops 16777216 | bytes 1048576 | tf_op jit(solution)/shard_map/pallas_call | solution.py:324
  35.2 1.9 %collective-permute-start.4 = (bf16[9,128,128]{2,1,0:T(8,128)(2,1)S(1)}, bf16[9,128,128]{2,1,0:T(8,128)(2,1)S(1)}, u32[]{:S(2)}, u32[]{:S(2)}) collective-permute-start(bf16[9,128,128]{2,1,0:T(8,128)(2,1)S(1)} %shard_map.69.payload), channel_id=1, source_target_pairs={{0,8},{8,0},{16,24},{24,16},{32,40},{40,32},{48,56},{56,48},{64,72... | collective-permute-start | bytes 884744 | tf_op jit(solution)/shard_map/ppermute | solution.py:415
  37.2 0.6 %shard_map.68.partial = f32[8,128,128]{2,1,0:T(8,128)S(1)} custom-call(s32[1,4,2]{2,1,0:T(4,128)S(1)} %copy.9.send, f32[8,128,128]{2,1,0:T(8,128)S(1)} %get-tuple-element.28.own, bf16[4,128,128]{2,1,0:T(8,128)(2,1)S(1)} %collective-permute-done.2.from_second, bf16[4,128,128]{2,1,0:T(8,128)(2,1)S(1)} %collective-permute-done.3.from_first), custom_call_target="tpu_custom_call" | custom-call | flops 16777216 | bytes 1048576 | tf_op jit(solution)/shard_map/pallas_call | solution.py:324
  37.8 0.0 copy-start
  37.8 0.9 %collective-permute-done.4.arrived = bf16[9,128,128]{2,1,0:T(8,128)(2,1)S(1)} collective-permute-done((bf16[9,128,128]{2,1,0:T(8,128)(2,1)S(1)}, bf16[9,128,128]{2,1,0:T(8,128)(2,1)S(1)}, u32[]{:S(2)}, u32[]{:S(2)}) %collective-permute-start.4) | collective-permute-done | bytes 294944 | tf_op jit(solution)/shard_map/ppermute | solution.py:415
  38.7 0.7 %shard_map.70 = (bf16[8,128,128]{2,1,0:T(8,128)(2,1)S(1)}, bf16[4,128,128]{2,1,0:T(8,128)(2,1)S(1)}, bf16[4,128,128]{2,1,0:T(8,128)(2,1)S(1)}) custom-call(s32[1,4,2]{2,1,0:T(4,128)S(1)} %copy.9.send, f32[8,128,128]{2,1,0:T(8,128)S(1)} %shard_map.68.partial, bf16[9,128,128]{2,1,0:T(8,128)(2,1)S(1)} %shard_map.69.payload, ...), custom_call_target="tpu_custom_call" | custom-call | flops 16777216 | bytes 1048576 | tf_op jit(solution)/shard_map/pallas_call | solution.py:324
  39.4 3.3 %collective-permute-start.5 = (bf16[4,128,128]{2,1,0:T(8,128)(2,1)S(1)}, bf16[4,128,128]{2,1,0:T(8,128)(2,1)S(1)}, u32[]{:S(2)}, u32[]{:S(2)}) collective-permute-start(bf16[4,128,128]{2,1,0:T(8,128)(2,1)S(1)} %get-tuple-element.33.second), channel_id=1, source_target_pairs={{0,496},{8,504},{16,32},{24,40},{32,16},{40,24},{48,64},{56,72},{6... | collective-permute-start | bytes 393224 | tf_op jit(solution)/shard_map/ppermute | solution.py:359
  42.7 1.9 %collective-permute-start.6 = (bf16[4,128,128]{2,1,0:T(8,128)(2,1)S(1)}, bf16[4,128,128]{2,1,0:T(8,128)(2,1)S(1)}, u32[]{:S(2)}, u32[]{:S(2)}) collective-permute-start(bf16[4,128,128]{2,1,0:T(8,128)(2,1)S(1)} %get-tuple-element.34.first), channel_id=1, source_target_pairs={{0,16},{8,24},{16,0},{24,8},{32,48},{40,56},{48,32},{56,40},{64,80... | collective-permute-start | bytes 393224 | tf_op jit(solution)/shard_map/ppermute | solution.py:359
  44.6 0.5 shard_map.71.partial
  45.1 5.0 %collective-permute-done.5.from_second = bf16[4,128,128]{2,1,0:T(8,128)(2,1)S(1)} collective-permute-done((bf16[4,128,128]{2,1,0:T(8,128)(2,1)S(1)}, bf16[4,128,128]{2,1,0:T(8,128)(2,1)S(1)}, u32[]{:S(2)}, u32[]{:S(2)}) %collective-permute-start.5) | collective-permute-done | bytes 131104 | tf_op jit(solution)/shard_map/ppermute | solution.py:359
  50.1 0.0 collective-permute-done.6.from_first
  50.1 0.0 copy-done
  50.1 1.7 %shard_map.72 = f32[8,16,2048]{2,1,0:T(8,128)} custom-call(f32[128,1024]{1,0:T(8,128)S(1)} %shard_map.71.partial, bf16[4,128,128]{2,1,0:T(8,128)(2,1)S(1)} %get-tuple-element.33.second, bf16[4,128,128]{2,1,0:T(8,128)(2,1)S(1)} %get-tuple-element.34.first, bf16[4,128,128]{2,1,0:T(8,128)(2,1)S(1)} %collective-permute-done.5.from_second, ...), custom_call_target="tpu_custom_call" | custom-call | flops 16777216 | bytes 1048576 | tf_op jit(solution)/shard_map/pallas_call | solution.py:324
Async XLA Ops:
  1.5 9.7 %collective-permute-start = (bf16[32,1024]{1,0:T(8,128)(2,1)S(1)}, bf16[32,1024]{1,0:T(8,128)(2,1)S(1)}, u32[]{:S(2)}, u32[]{:S(2)}) collective-permute-start(bf16[32,1024]{1,0:T(8,128)(2,1)S(1)} %get-tuple-element.24), channel_id=1, source_target_pairs={{0,1},{1,2},{2,3},{3,4},{4,5},{5,6},{6,7},{8,9},{9,10},{10,11},{11... | collective-permute-start | bytes 196616 | tf_op jit(solution)/shard_map/ppermute | solution.py:377
  6.2 7.4 %collective-permute-start.1 = (bf16[32,1024]{1,0:T(8,128)(2,1)S(1)}, bf16[32,1024]{1,0:T(8,128)(2,1)S(1)}, u32[]{:S(2)}, u32[]{:S(2)}) collective-permute-start(bf16[32,1024]{1,0:T(8,128)(2,1)S(1)} %get-tuple-element.25), channel_id=1, source_target_pairs={{1,0},{2,1},{3,2},{4,3},{5,4},{6,5},{7,6},{9,8},{10,9},{11,10},{12... | collective-permute-start | bytes 196616 | tf_op jit(solution)/shard_map/ppermute | solution.py:378
  8.2 21.4 %copy-start.1 = (s32[1,4,2]{1,2,0:T(2,128)S(1)}, s32[1,4,2]{1,2,0:T(2,128)}, u32[]{:S(2)}) copy-start(s32[1,4,2]{1,2,0:T(2,128)} %param.10) | copy-start | bytes 100
  14.5 18.2 %collective-permute-start.2 = (bf16[4,128,128]{2,1,0:T(8,128)(2,1)S(1)}, bf16[4,128,128]{2,1,0:T(8,128)(2,1)S(1)}, u32[]{:S(2)}, u32[]{:S(2)}) collective-permute-start(bf16[4,128,128]{2,1,0:T(8,128)(2,1)S(1)} %get-tuple-element.29.second), channel_id=1, source_target_pairs={{0,496},{8,504},{16,32},{24,40},{32,16},{40,24},{48,64},{56,72},{6... | collective-permute-start | bytes 393224 | tf_op jit(solution)/shard_map/ppermute | solution.py:359
  27.7 6.9 %collective-permute-start.3 = (bf16[4,128,128]{2,1,0:T(8,128)(2,1)S(1)}, bf16[4,128,128]{2,1,0:T(8,128)(2,1)S(1)}, u32[]{:S(2)}, u32[]{:S(2)}) collective-permute-start(bf16[4,128,128]{2,1,0:T(8,128)(2,1)S(1)} %get-tuple-element.30.first), channel_id=1, source_target_pairs={{0,16},{8,24},{16,0},{24,8},{32,48},{40,56},{48,32},{56,40},{64,80... | collective-permute-start | bytes 393224 | tf_op jit(solution)/shard_map/ppermute | solution.py:359
  35.2 3.5 %collective-permute-start.4 = (bf16[9,128,128]{2,1,0:T(8,128)(2,1)S(1)}, bf16[9,128,128]{2,1,0:T(8,128)(2,1)S(1)}, u32[]{:S(2)}, u32[]{:S(2)}) collective-permute-start(bf16[9,128,128]{2,1,0:T(8,128)(2,1)S(1)} %shard_map.69.payload), channel_id=1, source_target_pairs={{0,8},{8,0},{16,24},{24,16},{32,40},{40,32},{48,56},{56,48},{64,72... | collective-permute-start | bytes 884744 | tf_op jit(solution)/shard_map/ppermute | solution.py:415
  37.8 12.3 %copy-start = (bf16[8,128,256]{2,1,0:T(8,128)(2,1)S(1)}, bf16[8,128,256]{2,1,0:T(8,128)(2,1)}, u32[]{:S(2)}) copy-start(bf16[8,128,256]{2,1,0:T(8,128)(2,1)} %interp.3) | copy-start | bytes 1572868
  39.4 10.8 %collective-permute-start.5 = (bf16[4,128,128]{2,1,0:T(8,128)(2,1)S(1)}, bf16[4,128,128]{2,1,0:T(8,128)(2,1)S(1)}, u32[]{:S(2)}, u32[]{:S(2)}) collective-permute-start(bf16[4,128,128]{2,1,0:T(8,128)(2,1)S(1)} %get-tuple-element.33.second), channel_id=1, source_target_pairs={{0,496},{8,504},{16,32},{24,40},{32,16},{40,24},{48,64},{56,72},{6... | collective-permute-start | bytes 393224 | tf_op jit(solution)/shard_map/ppermute | solution.py:359
  42.7 7.4 %collective-permute-start.6 = (bf16[4,128,128]{2,1,0:T(8,128)(2,1)S(1)}, bf16[4,128,128]{2,1,0:T(8,128)(2,1)S(1)}, u32[]{:S(2)}, u32[]{:S(2)}) collective-permute-start(bf16[4,128,128]{2,1,0:T(8,128)(2,1)S(1)} %get-tuple-element.34.first), channel_id=1, source_target_pairs={{0,16},{8,24},{16,0},{24,8},{32,48},{40,56},{48,32},{56,40},{64,80... | collective-permute-start | bytes 393224 | tf_op jit(solution)/shard_map/ppermute | solution.py:359

commit v7 on v6

--- a/solution.py
+++ b/solution.py
@@ -40,7 +40,14 @@
     tiles, tile_len, fine = bases.shape
     members, level_len, _ = block.shape
     rows = members * level_len
-    pairs = ((interp, bases), (fields, block), (weights, weights_copy))
+    half = tiles // 2
+    parts = [pl.ds(i * half, half) for i in range(2)]
+    columns = [pl.ds(i * half * fine, half * fine) for i in range(2)]
+    pairs = [(interp.at[parts[0]], bases.at[parts[0]])]
+    pairs += [(fields.at[:, :, columns[0]], block.at[:, :, columns[0]])]
+    pairs += [(interp.at[parts[1]], bases.at[parts[1]])]
+    pairs += [(fields.at[:, :, columns[1]], block.at[:, :, columns[1]])]
+    pairs += [(weights, weights_copy)]
     copies = [
         pltpu.make_async_copy(source, target, sems.at[i])
         for i, (source, target) in enumerate(pairs)
@@ -48,9 +55,10 @@
     for copy in copies:
         copy.start()
     first_half = iota((members // 2, 2 * halo, tile_len), 1) < halo
-    for copy in copies[:2]:
-        copy.wait()
     for t in range(tiles):
+        if t % half == 0:
+            for copy in copies[2 * (t // half) : 2 * (t // half) + 2]:
+                copy.wait()
         span = slice(t * fine, (t + 1) * fine)
         value = nt(block[:, :, span].reshape(rows, fine), bases[t])
         coarse[:, lanes(t, tile_len)] = value.astype(BF16)
@@ -67,8 +75,7 @@
             .reshape(members * halo, tile_len)
             .astype(BF16)
         )
-    for copy in copies[2:]:
-        copy.wait()
+    copies[4].wait()
 
 
 def fetch_weights(pattern, conv, table, conv_copy, sems):
@@ -89,8 +96,10 @@
     for t in range(tiles):
         for k in range(count):
             entry = table[t, k] - first_entry
-            entry = jnp.where((entry >= 0) & (entry < spare), entry, spare)
-            blocks[entry, :, lanes(t, tile_len)] = conv_copy[t, k]
+
+            @pl.when((entry >= 0) & (entry < spare))
+            def _():
+                blocks[entry, :, lanes(t, tile_len)] = conv_copy[t, k]
 
 
 def vertical_kernel(
@@ -153,7 +162,7 @@
     return blocks[:entries].reshape(-1, blocks.shape[-1])
 
 
-def adjoint_kernel(partial, halo_matrix, low, high, received_blocks, smooth, second, first):
+def adjoint_kernel(partial, halo_matrix, high, low, received_blocks, smooth, second, first):
     tile_len = received_blocks.shape[1]
     edge = jnp.concatenate([low[...], high[...]], axis=0)
     value = (
@@ -371,7 +380,7 @@
         [
             pltpu.VMEM(fields.shape, BF16),
             pltpu.VMEM((tiles, tile_len, fine), BF16),
-            pltpu.SemaphoreType.DMA((3,)),
+            pltpu.SemaphoreType.DMA((5,)),
         ],
     )
     low = lax.ppermute(top, "lev", [(i, i + 1) for i in range(levs - 1)])
@@ -393,7 +402,7 @@
         adjoint_kernel,
         (shape((rows, wide), BF16), four, four),
         [VMEM] * 5,
-        (partial, halo_matrix, low, high, received_blocks),
+        (partial, halo_matrix, high, low, received_blocks),
     )
     from_second = swap(second, 2)
     from_first = swap(first, 0)

time: 52.2 us -> 50.3 us (0.964)
  waiting for transfers between devices: 10.1 us -> 7.69 us
    ppermute x1, waiting for transfers between devices: 2.36 us -> 0.01 us  [shards(): high = lax.ppermute(bottom, 'lev', [(i + 1, i) for i in range(levs - 1)])]
  transfers between devices with their start and end apart: 7 -> 7, of which waited for: 4 -> 3; matrix products, arithmetic and copies ran while one was open for 0% -> 0% of each run, Pallas kernels for 14% -> 14%
where the time goes in v7:
time: 50.3 us; the launch traced here: 50 us
  starting transfers between devices  29.3 us (58%)
  Pallas kernels  12.7 us (25%)
  waiting for transfers between devices  7.69 us (15%)
    ppermute x4, starting transfers between devices, swap(): return lax.ppermute(block, 'patch', partner)  20.3 us
    pallas_call x9, Pallas kernels, call(): pl.pallas_call(kernel, out_shape=outs, in_specs=specs, out_specs=jax.tree...  12.7 us
    ppermute x4, waiting for transfers between devices, swap(): return lax.ppermute(block, 'patch', partner)  6.79 us
    ppermute x1, starting transfers between devices, shards(): low = lax.ppermute(top, 'lev', [(i, i + 1) for i in range(levs - 1)])  4.7 us
    ppermute x1, starting transfers between devices, shards(): high = lax.ppermute(bottom, 'lev', [(i + 1, i) for i in range(levs - 1)])  2.36 us
    ppermute x1, starting transfers between devices, shards(): lax.ppermute(payload, 'patch', [(i, i ^ 1) for i in range(patches)])  1.92 us
  transfers between devices with their start and end apart: 7, of which 3 were waited for; matrix products, arithmetic and copies ran while one was open for 0% of the time, Pallas kernels for 14%

profile of v7, /device:TPU:24, one launch (start us, length us, event | category | flops | bytes accessed | tf_op | source)
XLA Modules:
  0.0 50.0 jit_solution(17722329499667788597)
XLA Ops:
  0.0 1.5 %shard_map.64 = (bf16[128,1024]{1,0:T(8,128)(2,1)S(1)}, bf16[32,1024]{1,0:T(8,128)(2,1)S(1)}, bf16[32,1024]{1,0:T(8,128)(2,1)S(1)}, f32[5,128]{1,0:T(8,128)S(1)}) custom-call(bf16[8,16,2048]{2,1,0:T(8,128)(2,1)} %fields.1, bf16[8,128,256]{2,1,0:T(8,128)(2,1)} %interp.3, f32[5,128]{1,0:T(8,128)} %bitcast.1), custom_call_target="tpu_custom_call" | custom-call | flops 16777216 | bytes 1048576 | tf_op jit(solution)/shard_map/pallas_call | solution.py:333
  1.6 2.4 %collective-permute-start = (bf16[32,1024]{1,0:T(8,128)(2,1)S(1)}, bf16[32,1024]{1,0:T(8,128)(2,1)S(1)}, u32[]{:S(2)}, u32[]{:S(2)}) collective-permute-start(bf16[32,1024]{1,0:T(8,128)(2,1)S(1)} %get-tuple-element.24), channel_id=1, source_target_pairs={{1,0},{2,1},{3,2},{4,3},{5,4},{6,5},{7,6},{9,8},{10,9},{11,10},{12... | collective-permute-start | bytes 196616 | tf_op jit(solution)/shard_map/ppermute | solution.py:387
  3.9 4.7 %collective-permute-start.1 = (bf16[32,1024]{1,0:T(8,128)(2,1)S(1)}, bf16[32,1024]{1,0:T(8,128)(2,1)S(1)}, u32[]{:S(2)}, u32[]{:S(2)}) collective-permute-start(bf16[32,1024]{1,0:T(8,128)(2,1)S(1)} %get-tuple-element.25), channel_id=1, source_target_pairs={{0,1},{1,2},{2,3},{3,4},{4,5},{5,6},{6,7},{8,9},{9,10},{10,11},{11... | collective-permute-start | bytes 196616 | tf_op jit(solution)/shard_map/ppermute | solution.py:386
  8.6 0.0 copy-start.1
  8.6 3.1 %shard_map.65 = (f32[128,1024]{1,0:T(8,128)S(1)}, bf16[128,128]{1,0:T(8,128)(2,1)S(1)}, bf16[9,128,1024]{2,1,0:T(8,128)(2,1)S(1)}) custom-call(bf16[128,1024]{1,0:T(8,128)(2,1)S(1)} %get-tuple-element.20.coarse, f32[5,128]{1,0:T(8,128)S(1)} %get-tuple-element.21.weights, s32[8,8]{1,0:T(8,128)} %pattern.3, bf16[8,8,128,128]{3,2,1,0:T(8,128)(2,1)} %conv.3), custom_call_target="tpu_custom_call" | custom-call | flops 16777216 | bytes 1048576 | tf_op jit(solution)/shard_map/pallas_call | solution.py:333
  11.7 0.0 collective-permute-done.high
  11.7 0.0 collective-permute-done.1.low
  11.8 0.9 %shard_map.66 = (bf16[128,1024]{1,0:T(8,128)(2,1)S(1)}, bf16[4,128,128]{2,1,0:T(8,128)(2,1)S(1)}, bf16[4,128,128]{2,1,0:T(8,128)(2,1)S(1)}) custom-call(f32[128,1024]{1,0:T(8,128)S(1)} %get-tuple-element.22.partial, bf16[128,128]{1,0:T(8,128)(2,1)S(1)} %get-tuple-element.23.halo_matrix, bf16[32,1024]{1,0:T(8,128)(2,1)S(1)} %collective-permute-done.high, ...), custom_call_target="tpu_custom_call" | custom-call | flops 16777216 | bytes 1048576 | tf_op jit(solution)/shard_map/pallas_call | solution.py:333
  12.7 13.1 %collective-permute-start.2 = (bf16[4,128,128]{2,1,0:T(8,128)(2,1)S(1)}, bf16[4,128,128]{2,1,0:T(8,128)(2,1)S(1)}, u32[]{:S(2)}, u32[]{:S(2)}) collective-permute-start(bf16[4,128,128]{2,1,0:T(8,128)(2,1)S(1)} %get-tuple-element.29.second), channel_id=1, source_target_pairs={{0,496},{8,504},{16,32},{24,40},{32,16},{40,24},{48,64},{56,72},{6... | collective-permute-start | bytes 393224 | tf_op jit(solution)/shard_map/ppermute | solution.py:368
  25.8 1.9 %collective-permute-start.3 = (bf16[4,128,128]{2,1,0:T(8,128)(2,1)S(1)}, bf16[4,128,128]{2,1,0:T(8,128)(2,1)S(1)}, u32[]{:S(2)}, u32[]{:S(2)}) collective-permute-start(bf16[4,128,128]{2,1,0:T(8,128)(2,1)S(1)} %get-tuple-element.30.first), channel_id=1, source_target_pairs={{0,16},{8,24},{16,0},{24,8},{32,48},{40,56},{48,32},{56,40},{64,80... | collective-permute-start | bytes 393224 | tf_op jit(solution)/shard_map/ppermute | solution.py:368
  27.8 0.0 copy-done.1
  27.8 0.1 copy.9.send
  27.9 3.0 %shard_map.67 = (f32[8,128,128]{2,1,0:T(8,128)S(1)}, bf16[9,128,1024]{2,1,0:T(8,128)(2,1)S(1)}) custom-call(bf16[128,1024]{1,0:T(8,128)(2,1)S(1)} %get-tuple-element.27.smooth, s32[8,8]{1,0:T(8,128)} %pattern.3, bf16[8,8,128,128]{3,2,1,0:T(8,128)(2,1)} %conv.3), custom_call_target="tpu_custom_call" | custom-call | flops 16777216 | bytes 1048576 | tf_op jit(solution)/shard_map/pallas_call | solution.py:333
  30.9 0.0 collective-permute-done.2.from_second
  30.9 1.8 %collective-permute-done.3.from_first = bf16[4,128,128]{2,1,0:T(8,128)(2,1)S(1)} collective-permute-done((bf16[4,128,128]{2,1,0:T(8,128)(2,1)S(1)}, bf16[4,128,128]{2,1,0:T(8,128)(2,1)S(1)}, u32[]{:S(2)}, u32[]{:S(2)}) %collective-permute-start.3) | collective-permute-done | bytes 131104 | tf_op jit(solution)/shard_map/ppermute | solution.py:368
  32.7 0.7 %shard_map.69.payload = bf16[9,128,128]{2,1,0:T(8,128)(2,1)S(1)} custom-call(s32[1,4,2]{2,1,0:T(4,128)S(1)} %copy.9.send, f32[8,128,128]{2,1,0:T(8,128)S(1)} %get-tuple-element.28.own, bf16[4,128,128]{2,1,0:T(8,128)(2,1)S(1)} %get-tuple-element.29.second, bf16[4,128,128]{2,1,0:T(8,128)(2,1)S(1)} %get-tuple-element.30.first, ...), custom_call_target="tpu_custom_call" | custom-call | flops 16777216 | bytes 1048576 | tf_op jit(solution)/shard_map/pallas_call | solution.py:333
  33.4 1.9 %collective-permute-start.4 = (bf16[9,128,128]{2,1,0:T(8,128)(2,1)S(1)}, bf16[9,128,128]{2,1,0:T(8,128)(2,1)S(1)}, u32[]{:S(2)}, u32[]{:S(2)}) collective-permute-start(bf16[9,128,128]{2,1,0:T(8,128)(2,1)S(1)} %shard_map.69.payload), channel_id=1, source_target_pairs={{0,8},{8,0},{16,24},{24,16},{32,40},{40,32},{48,56},{56,48},{64,72... | collective-permute-start | bytes 884744 | tf_op jit(solution)/shard_map/ppermute | solution.py:424
  35.3 0.6 %shard_map.68.partial = f32[8,128,128]{2,1,0:T(8,128)S(1)} custom-call(s32[1,4,2]{2,1,0:T(4,128)S(1)} %copy.9.send, f32[8,128,128]{2,1,0:T(8,128)S(1)} %get-tuple-element.28.own, bf16[4,128,128]{2,1,0:T(8,128)(2,1)S(1)} %collective-permute-done.2.from_second, bf16[4,128,128]{2,1,0:T(8,128)(2,1)S(1)} %collective-permute-done.3.from_first), custom_call_target="tpu_custom_call" | custom-call | flops 16777216 | bytes 1048576 | tf_op jit(solution)/shard_map/pallas_call | solution.py:333
  36.0 0.0 copy-start
  36.0 0.9 %collective-permute-done.4.arrived = bf16[9,128,128]{2,1,0:T(8,128)(2,1)S(1)} collective-permute-done((bf16[9,128,128]{2,1,0:T(8,128)(2,1)S(1)}, bf16[9,128,128]{2,1,0:T(8,128)(2,1)S(1)}, u32[]{:S(2)}, u32[]{:S(2)}) %collective-permute-start.4) | collective-permute-done | bytes 294944 | tf_op jit(solution)/shard_map/ppermute | solution.py:424
  36.9 0.7 %shard_map.70 = (bf16[8,128,128]{2,1,0:T(8,128)(2,1)S(1)}, bf16[4,128,128]{2,1,0:T(8,128)(2,1)S(1)}, bf16[4,128,128]{2,1,0:T(8,128)(2,1)S(1)}) custom-call(s32[1,4,2]{2,1,0:T(4,128)S(1)} %copy.9.send, f32[8,128,128]{2,1,0:T(8,128)S(1)} %shard_map.68.partial, bf16[9,128,128]{2,1,0:T(8,128)(2,1)S(1)} %shard_map.69.payload, ...), custom_call_target="tpu_custom_call" | custom-call | flops 16777216 | bytes 1048576 | tf_op jit(solution)/shard_map/pallas_call | solution.py:333
  37.5 3.3 %collective-permute-start.5 = (bf16[4,128,128]{2,1,0:T(8,128)(2,1)S(1)}, bf16[4,128,128]{2,1,0:T(8,128)(2,1)S(1)}, u32[]{:S(2)}, u32[]{:S(2)}) collective-permute-start(bf16[4,128,128]{2,1,0:T(8,128)(2,1)S(1)} %get-tuple-element.33.second), channel_id=1, source_target_pairs={{0,496},{8,504},{16,32},{24,40},{32,16},{40,24},{48,64},{56,72},{6... | collective-permute-start | bytes 393224 | tf_op jit(solution)/shard_map/ppermute | solution.py:368
  40.9 1.9 %collective-permute-start.6 = (bf16[4,128,128]{2,1,0:T(8,128)(2,1)S(1)}, bf16[4,128,128]{2,1,0:T(8,128)(2,1)S(1)}, u32[]{:S(2)}, u32[]{:S(2)}) collective-permute-start(bf16[4,128,128]{2,1,0:T(8,128)(2,1)S(1)} %get-tuple-element.34.first), channel_id=1, source_target_pairs={{0,16},{8,24},{16,0},{24,8},{32,48},{40,56},{48,32},{56,40},{64,80... | collective-permute-start | bytes 393224 | tf_op jit(solution)/shard_map/ppermute | solution.py:368
  42.8 0.5 shard_map.71.partial
  43.3 5.0 %collective-permute-done.5.from_second = bf16[4,128,128]{2,1,0:T(8,128)(2,1)S(1)} collective-permute-done((bf16[4,128,128]{2,1,0:T(8,128)(2,1)S(1)}, bf16[4,128,128]{2,1,0:T(8,128)(2,1)S(1)}, u32[]{:S(2)}, u32[]{:S(2)}) %collective-permute-start.5) | collective-permute-done | bytes 131104 | tf_op jit(solution)/shard_map/ppermute | solution.py:368
  48.3 0.0 collective-permute-done.6.from_first
  48.3 0.0 copy-done
  48.3 1.7 %shard_map.72 = f32[8,16,2048]{2,1,0:T(8,128)} custom-call(f32[128,1024]{1,0:T(8,128)S(1)} %shard_map.71.partial, bf16[4,128,128]{2,1,0:T(8,128)(2,1)S(1)} %get-tuple-element.33.second, bf16[4,128,128]{2,1,0:T(8,128)(2,1)S(1)} %get-tuple-element.34.first, bf16[4,128,128]{2,1,0:T(8,128)(2,1)S(1)} %collective-permute-done.5.from_second, ...), custom_call_target="tpu_custom_call" | custom-call | flops 16777216 | bytes 1048576 | tf_op jit(solution)/shard_map/pallas_call | solution.py:333
Async XLA Ops:
  1.6 10.2 %collective-permute-start = (bf16[32,1024]{1,0:T(8,128)(2,1)S(1)}, bf16[32,1024]{1,0:T(8,128)(2,1)S(1)}, u32[]{:S(2)}, u32[]{:S(2)}) collective-permute-start(bf16[32,1024]{1,0:T(8,128)(2,1)S(1)} %get-tuple-element.24), channel_id=1, source_target_pairs={{1,0},{2,1},{3,2},{4,3},{5,4},{6,5},{7,6},{9,8},{10,9},{11,10},{12... | collective-permute-start | bytes 196616 | tf_op jit(solution)/shard_map/ppermute | solution.py:387
  3.9 7.8 %collective-permute-start.1 = (bf16[32,1024]{1,0:T(8,128)(2,1)S(1)}, bf16[32,1024]{1,0:T(8,128)(2,1)S(1)}, u32[]{:S(2)}, u32[]{:S(2)}) collective-permute-start(bf16[32,1024]{1,0:T(8,128)(2,1)S(1)} %get-tuple-element.25), channel_id=1, source_target_pairs={{0,1},{1,2},{2,3},{3,4},{4,5},{5,6},{6,7},{8,9},{9,10},{10,11},{11... | collective-permute-start | bytes 196616 | tf_op jit(solution)/shard_map/ppermute | solution.py:386
  8.6 19.2 %copy-start.1 = (s32[1,4,2]{1,2,0:T(2,128)S(1)}, s32[1,4,2]{1,2,0:T(2,128)}, u32[]{:S(2)}) copy-start(s32[1,4,2]{1,2,0:T(2,128)} %param.10) | copy-start | bytes 100
  12.7 18.2 %collective-permute-start.2 = (bf16[4,128,128]{2,1,0:T(8,128)(2,1)S(1)}, bf16[4,128,128]{2,1,0:T(8,128)(2,1)S(1)}, u32[]{:S(2)}, u32[]{:S(2)}) collective-permute-start(bf16[4,128,128]{2,1,0:T(8,128)(2,1)S(1)} %get-tuple-element.29.second), channel_id=1, source_target_pairs={{0,496},{8,504},{16,32},{24,40},{32,16},{40,24},{48,64},{56,72},{6... | collective-permute-start | bytes 393224 | tf_op jit(solution)/shard_map/ppermute | solution.py:368
  25.8 6.9 %collective-permute-start.3 = (bf16[4,128,128]{2,1,0:T(8,128)(2,1)S(1)}, bf16[4,128,128]{2,1,0:T(8,128)(2,1)S(1)}, u32[]{:S(2)}, u32[]{:S(2)}) collective-permute-start(bf16[4,128,128]{2,1,0:T(8,128)(2,1)S(1)} %get-tuple-element.30.first), channel_id=1, source_target_pairs={{0,16},{8,24},{16,0},{24,8},{32,48},{40,56},{48,32},{56,40},{64,80... | collective-permute-start | bytes 393224 | tf_op jit(solution)/shard_map/ppermute | solution.py:368
  33.4 3.5 %collective-permute-start.4 = (bf16[9,128,128]{2,1,0:T(8,128)(2,1)S(1)}, bf16[9,128,128]{2,1,0:T(8,128)(2,1)S(1)}, u32[]{:S(2)}, u32[]{:S(2)}) collective-permute-start(bf16[9,128,128]{2,1,0:T(8,128)(2,1)S(1)} %shard_map.69.payload), channel_id=1, source_target_pairs={{0,8},{8,0},{16,24},{24,16},{32,40},{40,32},{48,56},{56,48},{64,72... | collective-permute-start | bytes 884744 | tf_op jit(solution)/shard_map/ppermute | solution.py:424
  36.0 12.3 %copy-start = (bf16[8,128,256]{2,1,0:T(8,128)(2,1)S(1)}, bf16[8,128,256]{2,1,0:T(8,128)(2,1)}, u32[]{:S(2)}) copy-start(bf16[8,128,256]{2,1,0:T(8,128)(2,1)} %interp.3) | copy-start | bytes 1572868
  37.5 10.8 %collective-permute-start.5 = (bf16[4,128,128]{2,1,0:T(8,128)(2,1)S(1)}, bf16[4,128,128]{2,1,0:T(8,128)(2,1)S(1)}, u32[]{:S(2)}, u32[]{:S(2)}) collective-permute-start(bf16[4,128,128]{2,1,0:T(8,128)(2,1)S(1)} %get-tuple-element.33.second), channel_id=1, source_target_pairs={{0,496},{8,504},{16,32},{24,40},{32,16},{40,24},{48,64},{56,72},{6... | collective-permute-start | bytes 393224 | tf_op jit(solution)/shard_map/ppermute | solution.py:368
  40.9 7.4 %collective-permute-start.6 = (bf16[4,128,128]{2,1,0:T(8,128)(2,1)S(1)}, bf16[4,128,128]{2,1,0:T(8,128)(2,1)S(1)}, u32[]{:S(2)}, u32[]{:S(2)}) collective-permute-start(bf16[4,128,128]{2,1,0:T(8,128)(2,1)S(1)} %get-tuple-element.34.first), channel_id=1, source_target_pairs={{0,16},{8,24},{16,0},{24,8},{32,48},{40,56},{48,32},{56,40},{64,80... | collective-permute-start | bytes 393224 | tf_op jit(solution)/shard_map/ppermute | solution.py:368

commit v8 on v7

--- a/solution.py
+++ b/solution.py
@@ -107,7 +107,6 @@
     conv_copy, table, sems
 ):
     fetches = fetch_weights(pattern, conv, table, conv_copy, sems)
-    received_blocks[...] = jnp.zeros_like(received_blocks)
     rows = coarse.shape[0]
     halo_rows = rows // level_len * halo
     taps, levels = weights.shape
@@ -142,6 +141,7 @@
     own_matrix = jnp.concatenate(own_parts, axis=1)
     value = coarse[...]
     partial[...] = nn(own_matrix, jnp.concatenate([value, value], axis=0))
+    received_blocks[...] = jnp.zeros_like(received_blocks)
     lay_blocks(fetches, table, conv_copy, received_blocks, conv.shape[0])
 
 

time: 50.3 us -> 49.8 us (0.990)
  the two profiles are of different devices: /device:TPU:24 before, /device:TPU:32 now
where the time goes in v8:
time: 49.8 us; the launch traced here: 49.5 us
  starting transfers between devices  28.1 us (56%)
  Pallas kernels  11.9 us (24%)
  waiting for transfers between devices  9.27 us (19%)
    ppermute x4, starting transfers between devices, swap(): return lax.ppermute(block, 'patch', partner)  20.3 us
    pallas_call x9, Pallas kernels, call(): pl.pallas_call(kernel, out_shape=outs, in_specs=specs, out_specs=jax.tree...  11.9 us
    ppermute x4, waiting for transfers between devices, swap(): return lax.ppermute(block, 'patch', partner)  6.8 us
    ppermute x1, starting transfers between devices, shards(): low = lax.ppermute(top, 'lev', [(i, i + 1) for i in range(levs - 1)])  3.48 us
    ppermute x1, starting transfers between devices, shards(): high = lax.ppermute(bottom, 'lev', [(i + 1, i) for i in range(levs - 1)])  2.36 us
    ppermute x1, starting transfers between devices, shards(): lax.ppermute(payload, 'patch', [(i, i ^ 1) for i in range(patches)])  1.92 us
    ppermute x1, waiting for transfers between devices, shards(): low = lax.ppermute(top, 'lev', [(i, i + 1) for i in range(levs - 1)])  1.59 us
  transfers between devices with their start and end apart: 7, of which 4 were waited for; matrix products, arithmetic and copies ran while one was open for 0% of the time, Pallas kernels for 13%

profile of v8, /device:TPU:32, one launch (start us, length us, event | category | flops | bytes accessed | tf_op | source)
XLA Modules:
  0.0 49.5 jit_solution(97801311948160719)
XLA Ops:
  0.0 1.5 %shard_map.64 = (bf16[128,1024]{1,0:T(8,128)(2,1)S(1)}, bf16[32,1024]{1,0:T(8,128)(2,1)S(1)}, bf16[32,1024]{1,0:T(8,128)(2,1)S(1)}, f32[5,128]{1,0:T(8,128)S(1)}) custom-call(bf16[8,16,2048]{2,1,0:T(8,128)(2,1)} %fields.1, bf16[8,128,256]{2,1,0:T(8,128)(2,1)} %interp.3, f32[5,128]{1,0:T(8,128)} %bitcast.1), custom_call_target="tpu_custom_call" | custom-call | flops 16777216 | bytes 1048576 | tf_op jit(solution)/shard_map/pallas_call | solution.py:333
  1.5 2.4 %collective-permute-start = (bf16[32,1024]{1,0:T(8,128)(2,1)S(1)}, bf16[32,1024]{1,0:T(8,128)(2,1)S(1)}, u32[]{:S(2)}, u32[]{:S(2)}) collective-permute-start(bf16[32,1024]{1,0:T(8,128)(2,1)S(1)} %get-tuple-element.24), channel_id=1, source_target_pairs={{1,0},{2,1},{3,2},{4,3},{5,4},{6,5},{7,6},{9,8},{10,9},{11,10},{12... | collective-permute-start | bytes 196616 | tf_op jit(solution)/shard_map/ppermute | solution.py:387
  3.9 3.5 %collective-permute-start.1 = (bf16[32,1024]{1,0:T(8,128)(2,1)S(1)}, bf16[32,1024]{1,0:T(8,128)(2,1)S(1)}, u32[]{:S(2)}, u32[]{:S(2)}) collective-permute-start(bf16[32,1024]{1,0:T(8,128)(2,1)S(1)} %get-tuple-element.25), channel_id=1, source_target_pairs={{0,1},{1,2},{2,3},{3,4},{4,5},{5,6},{6,7},{8,9},{9,10},{10,11},{11... | collective-permute-start | bytes 196616 | tf_op jit(solution)/shard_map/ppermute | solution.py:386
  7.4 0.0 copy-start.1
  7.4 2.3 %shard_map.65 = (f32[128,1024]{1,0:T(8,128)S(1)}, bf16[128,128]{1,0:T(8,128)(2,1)S(1)}, bf16[9,128,1024]{2,1,0:T(8,128)(2,1)S(1)}) custom-call(bf16[128,1024]{1,0:T(8,128)(2,1)S(1)} %get-tuple-element.20.coarse, f32[5,128]{1,0:T(8,128)S(1)} %get-tuple-element.21.weights, s32[8,8]{1,0:T(8,128)} %pattern.3, bf16[8,8,128,128]{3,2,1,0:T(8,128)(2,1)} %conv.3), custom_call_target="tpu_custom_call" | custom-call | flops 16777216 | bytes 1048576 | tf_op jit(solution)/shard_map/pallas_call | solution.py:333
  9.7 0.0 collective-permute-done.high
  9.7 1.6 %collective-permute-done.1.low = bf16[32,1024]{1,0:T(8,128)(2,1)S(1)} collective-permute-done((bf16[32,1024]{1,0:T(8,128)(2,1)S(1)}, bf16[32,1024]{1,0:T(8,128)(2,1)S(1)}, u32[]{:S(2)}, u32[]{:S(2)}) %collective-permute-start.1) | collective-permute-done | bytes 65568 | tf_op jit(solution)/shard_map/ppermute | solution.py:386
  11.3 0.9 %shard_map.66 = (bf16[128,1024]{1,0:T(8,128)(2,1)S(1)}, bf16[4,128,128]{2,1,0:T(8,128)(2,1)S(1)}, bf16[4,128,128]{2,1,0:T(8,128)(2,1)S(1)}) custom-call(f32[128,1024]{1,0:T(8,128)S(1)} %get-tuple-element.22.partial, bf16[128,128]{1,0:T(8,128)(2,1)S(1)} %get-tuple-element.23.halo_matrix, bf16[32,1024]{1,0:T(8,128)(2,1)S(1)} %collective-permute-done.high, ...), custom_call_target="tpu_custom_call" | custom-call | flops 16777216 | bytes 1048576 | tf_op jit(solution)/shard_map/pallas_call | solution.py:333
  12.2 13.1 %collective-permute-start.2 = (bf16[4,128,128]{2,1,0:T(8,128)(2,1)S(1)}, bf16[4,128,128]{2,1,0:T(8,128)(2,1)S(1)}, u32[]{:S(2)}, u32[]{:S(2)}) collective-permute-start(bf16[4,128,128]{2,1,0:T(8,128)(2,1)S(1)} %get-tuple-element.29.second), channel_id=1, source_target_pairs={{0,496},{8,504},{16,32},{24,40},{32,16},{40,24},{48,64},{56,72},{6... | collective-permute-start | bytes 393224 | tf_op jit(solution)/shard_map/ppermute | solution.py:368
  25.4 1.9 %collective-permute-start.3 = (bf16[4,128,128]{2,1,0:T(8,128)(2,1)S(1)}, bf16[4,128,128]{2,1,0:T(8,128)(2,1)S(1)}, u32[]{:S(2)}, u32[]{:S(2)}) collective-permute-start(bf16[4,128,128]{2,1,0:T(8,128)(2,1)S(1)} %get-tuple-element.30.first), channel_id=1, source_target_pairs={{0,16},{8,24},{16,0},{24,8},{32,48},{40,56},{48,32},{56,40},{64,80... | collective-permute-start | bytes 393224 | tf_op jit(solution)/shard_map/ppermute | solution.py:368
  27.3 0.0 copy-done.1
  27.3 0.1 copy.9.send
  27.4 3.0 %shard_map.67 = (f32[8,128,128]{2,1,0:T(8,128)S(1)}, bf16[9,128,1024]{2,1,0:T(8,128)(2,1)S(1)}) custom-call(bf16[128,1024]{1,0:T(8,128)(2,1)S(1)} %get-tuple-element.27.smooth, s32[8,8]{1,0:T(8,128)} %pattern.3, bf16[8,8,128,128]{3,2,1,0:T(8,128)(2,1)} %conv.3), custom_call_target="tpu_custom_call" | custom-call | flops 16777216 | bytes 1048576 | tf_op jit(solution)/shard_map/pallas_call | solution.py:333
  30.4 0.0 collective-permute-done.2.from_second
  30.4 1.8 %collective-permute-done.3.from_first = bf16[4,128,128]{2,1,0:T(8,128)(2,1)S(1)} collective-permute-done((bf16[4,128,128]{2,1,0:T(8,128)(2,1)S(1)}, bf16[4,128,128]{2,1,0:T(8,128)(2,1)S(1)}, u32[]{:S(2)}, u32[]{:S(2)}) %collective-permute-start.3) | collective-permute-done | bytes 131104 | tf_op jit(solution)/shard_map/ppermute | solution.py:368
  32.2 0.7 %shard_map.69.payload = bf16[9,128,128]{2,1,0:T(8,128)(2,1)S(1)} custom-call(s32[1,4,2]{2,1,0:T(4,128)S(1)} %copy.9.send, f32[8,128,128]{2,1,0:T(8,128)S(1)} %get-tuple-element.28.own, bf16[4,128,128]{2,1,0:T(8,128)(2,1)S(1)} %get-tuple-element.29.second, bf16[4,128,128]{2,1,0:T(8,128)(2,1)S(1)} %get-tuple-element.30.first, ...), custom_call_target="tpu_custom_call" | custom-call | flops 16777216 | bytes 1048576 | tf_op jit(solution)/shard_map/pallas_call | solution.py:333
  32.9 1.9 %collective-permute-start.4 = (bf16[9,128,128]{2,1,0:T(8,128)(2,1)S(1)}, bf16[9,128,128]{2,1,0:T(8,128)(2,1)S(1)}, u32[]{:S(2)}, u32[]{:S(2)}) collective-permute-start(bf16[9,128,128]{2,1,0:T(8,128)(2,1)S(1)} %shard_map.69.payload), channel_id=1, source_target_pairs={{0,8},{8,0},{16,24},{24,16},{32,40},{40,32},{48,56},{56,48},{64,72... | collective-permute-start | bytes 884744 | tf_op jit(solution)/shard_map/ppermute | solution.py:424
  34.9 0.6 %shard_map.68.partial = f32[8,128,128]{2,1,0:T(8,128)S(1)} custom-call(s32[1,4,2]{2,1,0:T(4,128)S(1)} %copy.9.send, f32[8,128,128]{2,1,0:T(8,128)S(1)} %get-tuple-element.28.own, bf16[4,128,128]{2,1,0:T(8,128)(2,1)S(1)} %collective-permute-done.2.from_second, bf16[4,128,128]{2,1,0:T(8,128)(2,1)S(1)} %collective-permute-done.3.from_first), custom_call_target="tpu_custom_call" | custom-call | flops 16777216 | bytes 1048576 | tf_op jit(solution)/shard_map/pallas_call | solution.py:333
  35.5 0.0 copy-start
  35.5 0.9 %collective-permute-done.4.arrived = bf16[9,128,128]{2,1,0:T(8,128)(2,1)S(1)} collective-permute-done((bf16[9,128,128]{2,1,0:T(8,128)(2,1)S(1)}, bf16[9,128,128]{2,1,0:T(8,128)(2,1)S(1)}, u32[]{:S(2)}, u32[]{:S(2)}) %collective-permute-start.4) | collective-permute-done | bytes 294944 | tf_op jit(solution)/shard_map/ppermute | solution.py:424
  36.4 0.7 %shard_map.70 = (bf16[8,128,128]{2,1,0:T(8,128)(2,1)S(1)}, bf16[4,128,128]{2,1,0:T(8,128)(2,1)S(1)}, bf16[4,128,128]{2,1,0:T(8,128)(2,1)S(1)}) custom-call(s32[1,4,2]{2,1,0:T(4,128)S(1)} %copy.9.send, f32[8,128,128]{2,1,0:T(8,128)S(1)} %shard_map.68.partial, bf16[9,128,128]{2,1,0:T(8,128)(2,1)S(1)} %shard_map.69.payload, ...), custom_call_target="tpu_custom_call" | custom-call | flops 16777216 | bytes 1048576 | tf_op jit(solution)/shard_map/pallas_call | solution.py:333
  37.1 3.3 %collective-permute-start.5 = (bf16[4,128,128]{2,1,0:T(8,128)(2,1)S(1)}, bf16[4,128,128]{2,1,0:T(8,128)(2,1)S(1)}, u32[]{:S(2)}, u32[]{:S(2)}) collective-permute-start(bf16[4,128,128]{2,1,0:T(8,128)(2,1)S(1)} %get-tuple-element.33.second), channel_id=1, source_target_pairs={{0,496},{8,504},{16,32},{24,40},{32,16},{40,24},{48,64},{56,72},{6... | collective-permute-start | bytes 393224 | tf_op jit(solution)/shard_map/ppermute | solution.py:368
  40.4 1.9 %collective-permute-start.6 = (bf16[4,128,128]{2,1,0:T(8,128)(2,1)S(1)}, bf16[4,128,128]{2,1,0:T(8,128)(2,1)S(1)}, u32[]{:S(2)}, u32[]{:S(2)}) collective-permute-start(bf16[4,128,128]{2,1,0:T(8,128)(2,1)S(1)} %get-tuple-element.34.first), channel_id=1, source_target_pairs={{0,16},{8,24},{16,0},{24,8},{32,48},{40,56},{48,32},{56,40},{64,80... | collective-permute-start | bytes 393224 | tf_op jit(solution)/shard_map/ppermute | solution.py:368
  42.3 0.5 shard_map.71.partial
  42.8 5.0 %collective-permute-done.5.from_second = bf16[4,128,128]{2,1,0:T(8,128)(2,1)S(1)} collective-permute-done((bf16[4,128,128]{2,1,0:T(8,128)(2,1)S(1)}, bf16[4,128,128]{2,1,0:T(8,128)(2,1)S(1)}, u32[]{:S(2)}, u32[]{:S(2)}) %collective-permute-start.5) | collective-permute-done | bytes 131104 | tf_op jit(solution)/shard_map/ppermute | solution.py:368
  47.8 0.0 collective-permute-done.6.from_first
  47.8 0.0 copy-done
  47.8 1.7 %shard_map.72 = f32[8,16,2048]{2,1,0:T(8,128)} custom-call(f32[128,1024]{1,0:T(8,128)S(1)} %shard_map.71.partial, bf16[4,128,128]{2,1,0:T(8,128)(2,1)S(1)} %get-tuple-element.33.second, bf16[4,128,128]{2,1,0:T(8,128)(2,1)S(1)} %get-tuple-element.34.first, bf16[4,128,128]{2,1,0:T(8,128)(2,1)S(1)} %collective-permute-done.5.from_second, ...), custom_call_target="tpu_custom_call" | custom-call | flops 16777216 | bytes 1048576 | tf_op jit(solution)/shard_map/pallas_call | solution.py:333
Async XLA Ops:
  1.5 8.1 %collective-permute-start = (bf16[32,1024]{1,0:T(8,128)(2,1)S(1)}, bf16[32,1024]{1,0:T(8,128)(2,1)S(1)}, u32[]{:S(2)}, u32[]{:S(2)}) collective-permute-start(bf16[32,1024]{1,0:T(8,128)(2,1)S(1)} %get-tuple-element.24), channel_id=1, source_target_pairs={{1,0},{2,1},{3,2},{4,3},{5,4},{6,5},{7,6},{9,8},{10,9},{11,10},{12... | collective-permute-start | bytes 196616 | tf_op jit(solution)/shard_map/ppermute | solution.py:387
  3.9 7.4 %collective-permute-start.1 = (bf16[32,1024]{1,0:T(8,128)(2,1)S(1)}, bf16[32,1024]{1,0:T(8,128)(2,1)S(1)}, u32[]{:S(2)}, u32[]{:S(2)}) collective-permute-start(bf16[32,1024]{1,0:T(8,128)(2,1)S(1)} %get-tuple-element.25), channel_id=1, source_target_pairs={{0,1},{1,2},{2,3},{3,4},{4,5},{5,6},{6,7},{8,9},{9,10},{10,11},{11... | collective-permute-start | bytes 196616 | tf_op jit(solution)/shard_map/ppermute | solution.py:386
  7.4 19.9 %copy-start.1 = (s32[1,4,2]{1,2,0:T(2,128)S(1)}, s32[1,4,2]{1,2,0:T(2,128)}, u32[]{:S(2)}) copy-start(s32[1,4,2]{1,2,0:T(2,128)} %param.10) | copy-start | bytes 100
  12.2 18.2 %collective-permute-start.2 = (bf16[4,128,128]{2,1,0:T(8,128)(2,1)S(1)}, bf16[4,128,128]{2,1,0:T(8,128)(2,1)S(1)}, u32[]{:S(2)}, u32[]{:S(2)}) collective-permute-start(bf16[4,128,128]{2,1,0:T(8,128)(2,1)S(1)} %get-tuple-element.29.second), channel_id=1, source_target_pairs={{0,496},{8,504},{16,32},{24,40},{32,16},{40,24},{48,64},{56,72},{6... | collective-permute-start | bytes 393224 | tf_op jit(solution)/shard_map/ppermute | solution.py:368
  25.4 6.9 %collective-permute-start.3 = (bf16[4,128,128]{2,1,0:T(8,128)(2,1)S(1)}, bf16[4,128,128]{2,1,0:T(8,128)(2,1)S(1)}, u32[]{:S(2)}, u32[]{:S(2)}) collective-permute-start(bf16[4,128,128]{2,1,0:T(8,128)(2,1)S(1)} %get-tuple-element.30.first), channel_id=1, source_target_pairs={{0,16},{8,24},{16,0},{24,8},{32,48},{40,56},{48,32},{56,40},{64,80... | collective-permute-start | bytes 393224 | tf_op jit(solution)/shard_map/ppermute | solution.py:368
  32.9 3.5 %collective-permute-start.4 = (bf16[9,128,128]{2,1,0:T(8,128)(2,1)S(1)}, bf16[9,128,128]{2,1,0:T(8,128)(2,1)S(1)}, u32[]{:S(2)}, u32[]{:S(2)}) collective-permute-start(bf16[9,128,128]{2,1,0:T(8,128)(2,1)S(1)} %shard_map.69.payload), channel_id=1, source_target_pairs={{0,8},{8,0},{16,24},{24,16},{32,40},{40,32},{48,56},{56,48},{64,72... | collective-permute-start | bytes 884744 | tf_op jit(solution)/shard_map/ppermute | solution.py:424
  35.5 12.3 %copy-start = (bf16[8,128,256]{2,1,0:T(8,128)(2,1)S(1)}, bf16[8,128,256]{2,1,0:T(8,128)(2,1)}, u32[]{:S(2)}) copy-start(bf16[8,128,256]{2,1,0:T(8,128)(2,1)} %interp.3) | copy-start | bytes 1572868
  37.1 10.8 %collective-permute-start.5 = (bf16[4,128,128]{2,1,0:T(8,128)(2,1)S(1)}, bf16[4,128,128]{2,1,0:T(8,128)(2,1)S(1)}, u32[]{:S(2)}, u32[]{:S(2)}) collective-permute-start(bf16[4,128,128]{2,1,0:T(8,128)(2,1)S(1)} %get-tuple-element.33.second), channel_id=1, source_target_pairs={{0,496},{8,504},{16,32},{24,40},{32,16},{40,24},{48,64},{56,72},{6... | collective-permute-start | bytes 393224 | tf_op jit(solution)/shard_map/ppermute | solution.py:368
  40.4 7.4 %collective-permute-start.6 = (bf16[4,128,128]{2,1,0:T(8,128)(2,1)S(1)}, bf16[4,128,128]{2,1,0:T(8,128)(2,1)S(1)}, u32[]{:S(2)}, u32[]{:S(2)}) collective-permute-start(bf16[4,128,128]{2,1,0:T(8,128)(2,1)S(1)} %get-tuple-element.34.first), channel_id=1, source_target_pairs={{0,16},{8,24},{16,0},{24,8},{32,48},{40,56},{48,32},{56,40},{64,80... | collective-permute-start | bytes 393224 | tf_op jit(solution)/shard_map/ppermute | solution.py:368

commit v9 on v8

--- a/solution.py
+++ b/solution.py
@@ -79,10 +79,10 @@
 
 
 def fetch_weights(pattern, conv, table, conv_copy, sems):
-    fetches = (
-        pltpu.make_async_copy(pattern, table, sems.at[0]),
-        pltpu.make_async_copy(conv, conv_copy, sems.at[1]),
-    )
+    fetches = [pltpu.make_async_copy(pattern, table, sems.at[0])] + [
+        pltpu.make_async_copy(conv.at[t], conv_copy.at[t], sems.at[1 + t])
+        for t in range(conv.shape[0])
+    ]
     for fetch in fetches:
         fetch.start()
     return fetches
@@ -91,9 +91,9 @@
 def lay_blocks(fetches, table, conv_copy, blocks, first_entry):
     tiles, count, tile_len, _ = conv_copy.shape
     spare = blocks.shape[0] - 1
-    for fetch in fetches:
-        fetch.wait()
+    fetches[0].wait()
     for t in range(tiles):
+        fetches[1 + t].wait()
         for k in range(count):
             entry = table[t, k] - first_entry
 
@@ -388,7 +388,7 @@
     weight_scratch = [
         pltpu.VMEM(conv_weight.shape, BF16),
         pltpu.SMEM(tile_pattern.shape, jnp.int32),
-        pltpu.SemaphoreType.DMA((2,)),
+        pltpu.SemaphoreType.DMA((1 + tiles,)),
     ]
     partial, halo_matrix, received_blocks = call(
         functools.partial(vertical_kernel, level_len, halo),

time: 49.8 us -> 49.8 us (level)
  Pallas kernels: 11.9 us -> 11 us
  waiting for transfers between devices: 9.27 us -> 10.1 us
    pallas_call x9, Pallas kernels: 11.9 us -> 11 us  [call(): pl.pallas_call(kernel, out_shape=outs, in_specs=specs, out_specs=jax.tree...]
    ppermute x4, waiting for transfers between devices: 6.8 us -> 7.34 us  [swap(): return lax.ppermute(block, 'patch', partner)]
  transfers between devices with their start and end apart: 7 -> 7, of which waited for: 4 -> 4; matrix products, arithmetic and copies ran while one was open for 0% -> 0% of each run, Pallas kernels for 13% -> 11%
where the time goes in v9:
time: 49.8 us; the launch traced here: 49.5 us
  starting transfers between devices  28.1 us (56%)
  Pallas kernels  11 us (22%)
  waiting for transfers between devices  10.1 us (20%)
    ppermute x4, starting transfers between devices, swap(): return lax.ppermute(block, 'patch', partner)  20.3 us
    pallas_call x9, Pallas kernels, call(): pl.pallas_call(kernel, out_shape=outs, in_specs=specs, out_specs=jax.tree...  11 us
    ppermute x4, waiting for transfers between devices, swap(): return lax.ppermute(block, 'patch', partner)  7.34 us
    ppermute x1, starting transfers between devices, shards(): low = lax.ppermute(top, 'lev', [(i, i + 1) for i in range(levs - 1)])  3.48 us
    ppermute x1, starting transfers between devices, shards(): high = lax.ppermute(bottom, 'lev', [(i + 1, i) for i in range(levs - 1)])  2.36 us
    ppermute x1, starting transfers between devices, shards(): lax.ppermute(payload, 'patch', [(i, i ^ 1) for i in range(patches)])  1.92 us
    ppermute x1, waiting for transfers between devices, shards(): low = lax.ppermute(top, 'lev', [(i, i + 1) for i in range(levs - 1)])  1.92 us
  transfers between devices with their start and end apart: 7, of which 4 were waited for; matrix products, arithmetic and copies ran while one was open for 0% of the time, Pallas kernels for 11%

profile of v9, /device:TPU:32, one launch (start us, length us, event | category | flops | bytes accessed | tf_op | source)
XLA Modules:
  0.0 49.5 jit_solution(16157610170799566279)
XLA Ops:
  0.0 1.5 %shard_map.64 = (bf16[128,1024]{1,0:T(8,128)(2,1)S(1)}, bf16[32,1024]{1,0:T(8,128)(2,1)S(1)}, bf16[32,1024]{1,0:T(8,128)(2,1)S(1)}, f32[5,128]{1,0:T(8,128)S(1)}) custom-call(bf16[8,16,2048]{2,1,0:T(8,128)(2,1)} %fields.1, bf16[8,128,256]{2,1,0:T(8,128)(2,1)} %interp.3, f32[5,128]{1,0:T(8,128)} %bitcast.1), custom_call_target="tpu_custom_call" | custom-call | flops 16777216 | bytes 1048576 | tf_op jit(solution)/shard_map/pallas_call | solution.py:333
  1.5 2.4 %collective-permute-start = (bf16[32,1024]{1,0:T(8,128)(2,1)S(1)}, bf16[32,1024]{1,0:T(8,128)(2,1)S(1)}, u32[]{:S(2)}, u32[]{:S(2)}) collective-permute-start(bf16[32,1024]{1,0:T(8,128)(2,1)S(1)} %get-tuple-element.24), channel_id=1, source_target_pairs={{1,0},{2,1},{3,2},{4,3},{5,4},{6,5},{7,6},{9,8},{10,9},{11,10},{12... | collective-permute-start | bytes 196616 | tf_op jit(solution)/shard_map/ppermute | solution.py:387
  3.9 3.5 %collective-permute-start.1 = (bf16[32,1024]{1,0:T(8,128)(2,1)S(1)}, bf16[32,1024]{1,0:T(8,128)(2,1)S(1)}, u32[]{:S(2)}, u32[]{:S(2)}) collective-permute-start(bf16[32,1024]{1,0:T(8,128)(2,1)S(1)} %get-tuple-element.25), channel_id=1, source_target_pairs={{0,1},{1,2},{2,3},{3,4},{4,5},{5,6},{6,7},{8,9},{9,10},{10,11},{11... | collective-permute-start | bytes 196616 | tf_op jit(solution)/shard_map/ppermute | solution.py:386
  7.4 0.0 copy-start.1
  7.4 1.9 %shard_map.65 = (f32[128,1024]{1,0:T(8,128)S(1)}, bf16[128,128]{1,0:T(8,128)(2,1)S(1)}, bf16[9,128,1024]{2,1,0:T(8,128)(2,1)S(1)}) custom-call(bf16[128,1024]{1,0:T(8,128)(2,1)S(1)} %get-tuple-element.20.coarse, f32[5,128]{1,0:T(8,128)S(1)} %get-tuple-element.21.weights, s32[8,8]{1,0:T(8,128)} %pattern.3, bf16[8,8,128,128]{3,2,1,0:T(8,128)(2,1)} %conv.3), custom_call_target="tpu_custom_call" | custom-call | flops 16777216 | bytes 1048576 | tf_op jit(solution)/shard_map/pallas_call | solution.py:333
  9.4 0.0 collective-permute-done.high
  9.4 1.9 %collective-permute-done.1.low = bf16[32,1024]{1,0:T(8,128)(2,1)S(1)} collective-permute-done((bf16[32,1024]{1,0:T(8,128)(2,1)S(1)}, bf16[32,1024]{1,0:T(8,128)(2,1)S(1)}, u32[]{:S(2)}, u32[]{:S(2)}) %collective-permute-start.1) | collective-permute-done | bytes 65568 | tf_op jit(solution)/shard_map/ppermute | solution.py:386
  11.3 0.9 %shard_map.66 = (bf16[128,1024]{1,0:T(8,128)(2,1)S(1)}, bf16[4,128,128]{2,1,0:T(8,128)(2,1)S(1)}, bf16[4,128,128]{2,1,0:T(8,128)(2,1)S(1)}) custom-call(f32[128,1024]{1,0:T(8,128)S(1)} %get-tuple-element.22.partial, bf16[128,128]{1,0:T(8,128)(2,1)S(1)} %get-tuple-element.23.halo_matrix, bf16[32,1024]{1,0:T(8,128)(2,1)S(1)} %collective-permute-done.high, ...), custom_call_target="tpu_custom_call" | custom-call | flops 16777216 | bytes 1048576 | tf_op jit(solution)/shard_map/pallas_call | solution.py:333
  12.2 13.1 %collective-permute-start.2 = (bf16[4,128,128]{2,1,0:T(8,128)(2,1)S(1)}, bf16[4,128,128]{2,1,0:T(8,128)(2,1)S(1)}, u32[]{:S(2)}, u32[]{:S(2)}) collective-permute-start(bf16[4,128,128]{2,1,0:T(8,128)(2,1)S(1)} %get-tuple-element.29.second), channel_id=1, source_target_pairs={{0,496},{8,504},{16,32},{24,40},{32,16},{40,24},{48,64},{56,72},{6... | collective-permute-start | bytes 393224 | tf_op jit(solution)/shard_map/ppermute | solution.py:368
  25.4 1.9 %collective-permute-start.3 = (bf16[4,128,128]{2,1,0:T(8,128)(2,1)S(1)}, bf16[4,128,128]{2,1,0:T(8,128)(2,1)S(1)}, u32[]{:S(2)}, u32[]{:S(2)}) collective-permute-start(bf16[4,128,128]{2,1,0:T(8,128)(2,1)S(1)} %get-tuple-element.30.first), channel_id=1, source_target_pairs={{0,16},{8,24},{16,0},{24,8},{32,48},{40,56},{48,32},{56,40},{64,80... | collective-permute-start | bytes 393224 | tf_op jit(solution)/shard_map/ppermute | solution.py:368
  27.3 0.0 copy-done.1
  27.3 0.1 copy.9.send
  27.4 2.5 %shard_map.67 = (f32[8,128,128]{2,1,0:T(8,128)S(1)}, bf16[9,128,1024]{2,1,0:T(8,128)(2,1)S(1)}) custom-call(bf16[128,1024]{1,0:T(8,128)(2,1)S(1)} %get-tuple-element.27.smooth, s32[8,8]{1,0:T(8,128)} %pattern.3, bf16[8,8,128,128]{3,2,1,0:T(8,128)(2,1)} %conv.3), custom_call_target="tpu_custom_call" | custom-call | flops 16777216 | bytes 1048576 | tf_op jit(solution)/shard_map/pallas_call | solution.py:333
  29.9 0.0 collective-permute-done.2.from_second
  29.9 2.3 %collective-permute-done.3.from_first = bf16[4,128,128]{2,1,0:T(8,128)(2,1)S(1)} collective-permute-done((bf16[4,128,128]{2,1,0:T(8,128)(2,1)S(1)}, bf16[4,128,128]{2,1,0:T(8,128)(2,1)S(1)}, u32[]{:S(2)}, u32[]{:S(2)}) %collective-permute-start.3) | collective-permute-done | bytes 131104 | tf_op jit(solution)/shard_map/ppermute | solution.py:368
  32.2 0.7 %shard_map.69.payload = bf16[9,128,128]{2,1,0:T(8,128)(2,1)S(1)} custom-call(s32[1,4,2]{2,1,0:T(4,128)S(1)} %copy.9.send, f32[8,128,128]{2,1,0:T(8,128)S(1)} %get-tuple-element.28.own, bf16[4,128,128]{2,1,0:T(8,128)(2,1)S(1)} %get-tuple-element.29.second, bf16[4,128,128]{2,1,0:T(8,128)(2,1)S(1)} %get-tuple-element.30.first, ...), custom_call_target="tpu_custom_call" | custom-call | flops 16777216 | bytes 1048576 | tf_op jit(solution)/shard_map/pallas_call | solution.py:333
  32.9 1.9 %collective-permute-start.4 = (bf16[9,128,128]{2,1,0:T(8,128)(2,1)S(1)}, bf16[9,128,128]{2,1,0:T(8,128)(2,1)S(1)}, u32[]{:S(2)}, u32[]{:S(2)}) collective-permute-start(bf16[9,128,128]{2,1,0:T(8,128)(2,1)S(1)} %shard_map.69.payload), channel_id=1, source_target_pairs={{0,8},{8,0},{16,24},{24,16},{32,40},{40,32},{48,56},{56,48},{64,72... | collective-permute-start | bytes 884744 | tf_op jit(solution)/shard_map/ppermute | solution.py:424
  34.9 0.6 %shard_map.68.partial = f32[8,128,128]{2,1,0:T(8,128)S(1)} custom-call(s32[1,4,2]{2,1,0:T(4,128)S(1)} %copy.9.send, f32[8,128,128]{2,1,0:T(8,128)S(1)} %get-tuple-element.28.own, bf16[4,128,128]{2,1,0:T(8,128)(2,1)S(1)} %collective-permute-done.2.from_second, bf16[4,128,128]{2,1,0:T(8,128)(2,1)S(1)} %collective-permute-done.3.from_first), custom_call_target="tpu_custom_call" | custom-call | flops 16777216 | bytes 1048576 | tf_op jit(solution)/shard_map/pallas_call | solution.py:333
  35.5 0.0 copy-start
  35.5 0.9 %collective-permute-done.4.arrived = bf16[9,128,128]{2,1,0:T(8,128)(2,1)S(1)} collective-permute-done((bf16[9,128,128]{2,1,0:T(8,128)(2,1)S(1)}, bf16[9,128,128]{2,1,0:T(8,128)(2,1)S(1)}, u32[]{:S(2)}, u32[]{:S(2)}) %collective-permute-start.4) | collective-permute-done | bytes 294944 | tf_op jit(solution)/shard_map/ppermute | solution.py:424
  36.4 0.7 %shard_map.70 = (bf16[8,128,128]{2,1,0:T(8,128)(2,1)S(1)}, bf16[4,128,128]{2,1,0:T(8,128)(2,1)S(1)}, bf16[4,128,128]{2,1,0:T(8,128)(2,1)S(1)}) custom-call(s32[1,4,2]{2,1,0:T(4,128)S(1)} %copy.9.send, f32[8,128,128]{2,1,0:T(8,128)S(1)} %shard_map.68.partial, bf16[9,128,128]{2,1,0:T(8,128)(2,1)S(1)} %shard_map.69.payload, ...), custom_call_target="tpu_custom_call" | custom-call | flops 16777216 | bytes 1048576 | tf_op jit(solution)/shard_map/pallas_call | solution.py:333
  37.1 3.3 %collective-permute-start.5 = (bf16[4,128,128]{2,1,0:T(8,128)(2,1)S(1)}, bf16[4,128,128]{2,1,0:T(8,128)(2,1)S(1)}, u32[]{:S(2)}, u32[]{:S(2)}) collective-permute-start(bf16[4,128,128]{2,1,0:T(8,128)(2,1)S(1)} %get-tuple-element.33.second), channel_id=1, source_target_pairs={{0,496},{8,504},{16,32},{24,40},{32,16},{40,24},{48,64},{56,72},{6... | collective-permute-start | bytes 393224 | tf_op jit(solution)/shard_map/ppermute | solution.py:368
  40.4 1.9 %collective-permute-start.6 = (bf16[4,128,128]{2,1,0:T(8,128)(2,1)S(1)}, bf16[4,128,128]{2,1,0:T(8,128)(2,1)S(1)}, u32[]{:S(2)}, u32[]{:S(2)}) collective-permute-start(bf16[4,128,128]{2,1,0:T(8,128)(2,1)S(1)} %get-tuple-element.34.first), channel_id=1, source_target_pairs={{0,16},{8,24},{16,0},{24,8},{32,48},{40,56},{48,32},{56,40},{64,80... | collective-permute-start | bytes 393224 | tf_op jit(solution)/shard_map/ppermute | solution.py:368
  42.3 0.5 shard_map.71.partial
  42.8 5.0 %collective-permute-done.5.from_second = bf16[4,128,128]{2,1,0:T(8,128)(2,1)S(1)} collective-permute-done((bf16[4,128,128]{2,1,0:T(8,128)(2,1)S(1)}, bf16[4,128,128]{2,1,0:T(8,128)(2,1)S(1)}, u32[]{:S(2)}, u32[]{:S(2)}) %collective-permute-start.5) | collective-permute-done | bytes 131104 | tf_op jit(solution)/shard_map/ppermute | solution.py:368
  47.8 0.0 collective-permute-done.6.from_first
  47.8 0.0 copy-done
  47.8 1.7 %shard_map.72 = f32[8,16,2048]{2,1,0:T(8,128)} custom-call(f32[128,1024]{1,0:T(8,128)S(1)} %shard_map.71.partial, bf16[4,128,128]{2,1,0:T(8,128)(2,1)S(1)} %get-tuple-element.33.second, bf16[4,128,128]{2,1,0:T(8,128)(2,1)S(1)} %get-tuple-element.34.first, bf16[4,128,128]{2,1,0:T(8,128)(2,1)S(1)} %collective-permute-done.5.from_second, ...), custom_call_target="tpu_custom_call" | custom-call | flops 16777216 | bytes 1048576 | tf_op jit(solution)/shard_map/pallas_call | solution.py:333
Async XLA Ops:
  1.5 7.8 %collective-permute-start = (bf16[32,1024]{1,0:T(8,128)(2,1)S(1)}, bf16[32,1024]{1,0:T(8,128)(2,1)S(1)}, u32[]{:S(2)}, u32[]{:S(2)}) collective-permute-start(bf16[32,1024]{1,0:T(8,128)(2,1)S(1)} %get-tuple-element.24), channel_id=1, source_target_pairs={{1,0},{2,1},{3,2},{4,3},{5,4},{6,5},{7,6},{9,8},{10,9},{11,10},{12... | collective-permute-start | bytes 196616 | tf_op jit(solution)/shard_map/ppermute | solution.py:387
  3.9 7.4 %collective-permute-start.1 = (bf16[32,1024]{1,0:T(8,128)(2,1)S(1)}, bf16[32,1024]{1,0:T(8,128)(2,1)S(1)}, u32[]{:S(2)}, u32[]{:S(2)}) collective-permute-start(bf16[32,1024]{1,0:T(8,128)(2,1)S(1)} %get-tuple-element.25), channel_id=1, source_target_pairs={{0,1},{1,2},{2,3},{3,4},{4,5},{5,6},{6,7},{8,9},{9,10},{10,11},{11... | collective-permute-start | bytes 196616 | tf_op jit(solution)/shard_map/ppermute | solution.py:386
  7.4 19.9 %copy-start.1 = (s32[1,4,2]{1,2,0:T(2,128)S(1)}, s32[1,4,2]{1,2,0:T(2,128)}, u32[]{:S(2)}) copy-start(s32[1,4,2]{1,2,0:T(2,128)} %param.10) | copy-start | bytes 100
  12.2 17.7 %collective-permute-start.2 = (bf16[4,128,128]{2,1,0:T(8,128)(2,1)S(1)}, bf16[4,128,128]{2,1,0:T(8,128)(2,1)S(1)}, u32[]{:S(2)}, u32[]{:S(2)}) collective-permute-start(bf16[4,128,128]{2,1,0:T(8,128)(2,1)S(1)} %get-tuple-element.29.second), channel_id=1, source_target_pairs={{0,496},{8,504},{16,32},{24,40},{32,16},{40,24},{48,64},{56,72},{6... | collective-permute-start | bytes 393224 | tf_op jit(solution)/shard_map/ppermute | solution.py:368
  25.4 6.9 %collective-permute-start.3 = (bf16[4,128,128]{2,1,0:T(8,128)(2,1)S(1)}, bf16[4,128,128]{2,1,0:T(8,128)(2,1)S(1)}, u32[]{:S(2)}, u32[]{:S(2)}) collective-permute-start(bf16[4,128,128]{2,1,0:T(8,128)(2,1)S(1)} %get-tuple-element.30.first), channel_id=1, source_target_pairs={{0,16},{8,24},{16,0},{24,8},{32,48},{40,56},{48,32},{56,40},{64,80... | collective-permute-start | bytes 393224 | tf_op jit(solution)/shard_map/ppermute | solution.py:368
  32.9 3.5 %collective-permute-start.4 = (bf16[9,128,128]{2,1,0:T(8,128)(2,1)S(1)}, bf16[9,128,128]{2,1,0:T(8,128)(2,1)S(1)}, u32[]{:S(2)}, u32[]{:S(2)}) collective-permute-start(bf16[9,128,128]{2,1,0:T(8,128)(2,1)S(1)} %shard_map.69.payload), channel_id=1, source_target_pairs={{0,8},{8,0},{16,24},{24,16},{32,40},{40,32},{48,56},{56,48},{64,72... | collective-permute-start | bytes 884744 | tf_op jit(solution)/shard_map/ppermute | solution.py:424
  35.5 12.3 %copy-start = (bf16[8,128,256]{2,1,0:T(8,128)(2,1)S(1)}, bf16[8,128,256]{2,1,0:T(8,128)(2,1)}, u32[]{:S(2)}) copy-start(bf16[8,128,256]{2,1,0:T(8,128)(2,1)} %interp.3) | copy-start | bytes 1572868
  37.1 10.8 %collective-permute-start.5 = (bf16[4,128,128]{2,1,0:T(8,128)(2,1)S(1)}, bf16[4,128,128]{2,1,0:T(8,128)(2,1)S(1)}, u32[]{:S(2)}, u32[]{:S(2)}) collective-permute-start(bf16[4,128,128]{2,1,0:T(8,128)(2,1)S(1)} %get-tuple-element.33.second), channel_id=1, source_target_pairs={{0,496},{8,504},{16,32},{24,40},{32,16},{40,24},{48,64},{56,72},{6... | collective-permute-start | bytes 393224 | tf_op jit(solution)/shard_map/ppermute | solution.py:368
  40.4 7.4 %collective-permute-start.6 = (bf16[4,128,128]{2,1,0:T(8,128)(2,1)S(1)}, bf16[4,128,128]{2,1,0:T(8,128)(2,1)S(1)}, u32[]{:S(2)}, u32[]{:S(2)}) collective-permute-start(bf16[4,128,128]{2,1,0:T(8,128)(2,1)S(1)} %get-tuple-element.34.first), channel_id=1, source_target_pairs={{0,16},{8,24},{16,0},{24,8},{32,48},{40,56},{48,32},{56,40},{64,80... | collective-permute-start | bytes 393224 | tf_op jit(solution)/shard_map/ppermute | solution.py:368
